TPU v7x, 512 devices: a whole 4x8x8 slice. The times are simulated.
512 devices in a mesh: gx: 64 (over y, z), gy: 8 (over x, core).
Axes of the slice: x: 4, y: 8, z: 8, core: 2. Of those that a mesh axis runs over, the one named last changes fastest.
Arguments:
- features: float32 [32, 64, 256, 128], P(None, 'gx', 'gy'), may hold values from -6 to 6
- conv_weight: float32 [3, 3, 3, 32, 32], replicated, may hold values from -0.21875 to 0.21875
- conv_bias: float32 [32], replicated, may hold values from -3 to 3
- spectral_weight: float32 [4096, 2048], P(('gx', 'gy')), may hold values from -12 to 12
Outputs:
- layer_out: float32 [32, 64, 256, 128], P(None, 'gx', 'gy')
All inputs are finite; a program needn't handle non-finite values.
Results may differ from a plain program's by a relative error of at most 0.000062.
Values sent between devices are 32-bit elements; how exact they have to be, the bound alone decides.
No kernel may reach another device: no remote copies, remote signals or barrier semaphores. Data moves between devices by JAX's collectives and lax.ppermute only.
A program may use at most 64 MiB of HBM per device.

v0:
```python
import math

import jax
import jax.numpy as jnp
import numpy as np
from jax import lax
from jax.experimental import pallas as pl
from jax.experimental.pallas import tpu as pltpu
from jax.sharding import PartitionSpec as P

KX = 16
KY = 16
KZ = 16
GROUP = 8
LANES = 128

f32 = jnp.float32
bf16 = jnp.bfloat16
highest = lax.Precision.HIGHEST


def halves_of(value):
    high = value.astype(bf16)
    return high, (value - high.astype(f32)).astype(bf16)


def fixed_halves(table):
    table = np.asarray(table, np.float32)
    high = table.astype(bf16)
    return jnp.asarray(high), jnp.asarray((table - high.astype(np.float32)).astype(bf16))


def product(left, right, dims):
    return lax.dot_general(left, right, (dims, ((), ())), preferred_element_type=f32)


def product_of_halves(left, right, dims):
    return (
        product(left[0], right[0], dims)
        + product(left[0], right[1], dims)
        + product(left[1], right[0], dims)
    )


def signed_modes(number):
    series = np.arange(number)
    return np.where(series < number // 2, series, series - number)


def forward_tables(rows_y, length_y, depth):
    angle = 2.0 * np.pi / length_y * np.outer(signed_modes(KY), np.arange(rows_y))
    same = np.eye(GROUP)
    wide = np.einsum("rby,ij->rbijy", np.stack([np.cos(angle), -np.sin(angle)]), same)
    wide = wide.reshape(2 * KY * GROUP, GROUP * rows_y)
    angle = 2.0 * np.pi / depth * np.outer(np.arange(KZ), np.arange(depth))
    deep_cos = np.cos(angle)
    deep_sin = np.sin(angle)
    deep = np.concatenate(
        [
            np.concatenate([deep_cos, deep_sin], axis=1),
            np.concatenate([-deep_sin, deep_cos], axis=1),
        ],
        axis=0,
    )
    return wide, deep


def inverse_tables(rows_y, length_y, depth, norm_factor):
    angle = 2.0 * np.pi / length_y * np.outer(np.arange(rows_y), signed_modes(KY))
    same = np.eye(GROUP)
    wide = np.einsum("ryb,ij->iyrbj", np.stack([np.cos(angle), -np.sin(angle)]), same)
    wide = wide.reshape(GROUP * rows_y, 2 * KY * GROUP)
    angle = 2.0 * np.pi / depth * np.outer(np.arange(KZ), np.arange(depth))
    factor = norm_factor * np.where(np.arange(KZ) == 0, 1.0, 2.0)[:, None]
    deep_cos = factor * np.cos(angle)
    deep_sin = factor * np.sin(angle)
    deep = np.concatenate(
        [
            np.concatenate([deep_cos, deep_sin], axis=1),
            np.concatenate([-deep_sin, deep_cos], axis=1),
        ],
        axis=0,
    )
    return wide, deep


def forward_kernel(
    cells_ref, wide_high, wide_low, deep_high, deep_low, out_ref, middle_ref, pair_ref
):
    channels = middle_ref.shape[0] // KY
    block = wide_high.shape[1]
    groups = channels // GROUP
    wide = (wide_high[...], wide_low[...])
    for first in range(0, groups, 2):
        cells = jnp.concatenate(
            [
                cells_ref[first * block : (first + 1) * block, :],
                cells_ref[(first + 1) * block : (first + 2) * block, :],
            ],
            axis=1,
        )
        summed = product_of_halves(wide, halves_of(cells), ((1,), (0,)))
        for part in range(2):
            for mode in range(KY):
                row = (part * KY + mode) * GROUP
                for side in range(2):
                    place = mode * channels + (first + side) * GROUP
                    middle_ref[place : place + GROUP, part * LANES : (part + 1) * LANES] = (
                        summed[row : row + GROUP, side * LANES : (side + 1) * LANES]
                    )
    modes = product_of_halves(
        (deep_high[...], deep_low[...]), halves_of(middle_ref[...]), ((1,), (1,))
    )
    pair_ref[...] = jnp.zeros_like(pair_ref)
    for mode in range(KY):
        first = mode * channels
        for part in range(2):
            pair_ref[mode * KZ : (mode + 1) * KZ, part * channels : (part + 1) * channels] = (
                modes[part * KZ : (part + 1) * KZ, first : first + channels]
            )
    pairs = pair_ref[...]
    out_ref[pl.ds(0, KY * KZ, stride=2), :] = pairs
    out_ref[pl.ds(1, KY * KZ, stride=2), :] = pairs


def middle_kernel(rows_ref, basis_ref, weight_ref, out_ref, *, channels, norm_factor):
    basis = basis_ref[...]
    share = basis.shape[0] // 2
    sums = norm_factor * jnp.dot(
        basis, rows_ref[...], precision=highest, preferred_element_type=f32
    )
    hat_real = sums[:share, :channels] + sums[share:, channels : 2 * channels]
    hat_imag = sums[:share, channels : 2 * channels] - sums[share:, :channels]
    size = channels * channels
    lane = lax.broadcasted_iota(jnp.int32, (channels, size), 1)
    row = lax.broadcasted_iota(jnp.int32, (channels, size), 0)
    spread = jnp.where(lane // channels == row, 1.0, 0.0).astype(f32)
    hat = jnp.dot(
        jnp.concatenate([hat_real, hat_imag], axis=0),
        spread,
        precision=highest,
        preferred_element_type=f32,
    )
    real = hat[:share]
    imag = hat[share:]
    weight_real = weight_ref[:, :size]
    weight_imag = weight_ref[:, size:]
    terms = jnp.concatenate(
        [real * weight_real - imag * weight_imag, real * weight_imag + imag * weight_real], axis=0
    )
    mixed = terms[:, :LANES]
    for start in range(LANES, size, LANES):
        mixed = mixed + terms[:, start : start + LANES]
    step = LANES // 2
    while step >= channels:
        mixed = mixed + pltpu.roll(mixed, step, axis=1)
        step = step // 2
    lane = lax.broadcasted_iota(jnp.int32, (share, LANES), 1)
    mixed_real = mixed[:share]
    mixed_imag = mixed[share:]
    stacked = jnp.concatenate(
        [
            jnp.where(lane < channels, mixed_real, mixed_imag),
            jnp.where(lane < channels, -mixed_imag, mixed_real),
        ],
        axis=0,
    )
    out_ref[...] = lax.dot_general(
        basis, stacked, (((0,), (0,)), ((), ())), precision=highest, preferred_element_type=f32
    )


def edges_kernel(left_ref, cells_ref, right_ref, tails_ref, heads_ref, *, rows_y, channels):
    planes = (left_ref, cells_ref, right_ref)
    for plane in range(3):
        rows = pl.ds(plane * channels, channels)
        heads_ref[rows, :] = planes[plane][pl.ds(0, channels, stride=rows_y), :]
        tails_ref[rows, :] = planes[plane][pl.ds(rows_y - 1, channels, stride=rows_y), :]


def doubled_taps(taps):
    high, low = halves_of(taps)
    return jnp.concatenate([high, high, low], axis=1)


def doubled_cells(cells):
    high, low = halves_of(cells)
    return jnp.concatenate([high, low, high], axis=0)


def shifted_sum(parts, depth):
    lane = lax.broadcasted_iota(jnp.int32, parts[1].shape, 1)
    below = jnp.where(lane == 0, 0.0, pltpu.roll(parts[0], 1, axis=1))
    above = jnp.where(lane == depth - 1, 0.0, pltpu.roll(parts[2], depth - 1, axis=1))
    return parts[1] + below + above


def conv_kernel(
    left_ref, cells_ref, right_ref, taps_ref, bias_ref, out_ref, taps_scratch, sums_scratch,
    *, rows_y, channels, depth
):
    planes = (left_ref, cells_ref, right_ref)
    width = 3 * channels
    taps_scratch[...] = doubled_taps(taps_ref[...])
    sums_scratch[0, :width, :] = jnp.zeros((width, depth), f32)
    sums_scratch[rows_y + 1, 2 * width :, :] = jnp.zeros((width, depth), f32)

    def row_cells(row):
        return jnp.concatenate(
            [plane[pl.ds(row, channels, stride=rows_y), :] for plane in planes], axis=0
        )

    def multiply(step, _):
        cells = jnp.concatenate([row_cells(2 * step), row_cells(2 * step + 1)], axis=1)
        sums = product(taps_scratch[...], doubled_cells(cells), ((1,), (0,)))
        sums_scratch[2 * step + 1] = sums[:, :depth]
        sums_scratch[2 * step + 2] = sums[:, depth:]
        return 0

    lax.fori_loop(0, rows_y // 2, multiply, 0)
    bias = bias_ref[...]

    def collect(row, _):
        parts = []
        for shift in range(3):
            first = shift * channels
            parts.append(
                sums_scratch[row, first : first + channels, :]
                + sums_scratch[row + 1, width + first : width + first + channels, :]
                + sums_scratch[row + 2, 2 * width + first : 2 * width + first + channels, :]
            )
        out_ref[pl.ds(row, channels, stride=rows_y), :] = shifted_sum(parts, depth) + bias
        return 0

    lax.fori_loop(0, rows_y, collect, 0)


def inverse_kernel(
    rows_ref, wide_high, wide_low, deep_high, deep_low, conv_ref, before_ref, after_ref, taps_ref,
    out_ref, modes_ref, middle_ref, conv_scratch, *, rows_y
):
    pairs = rows_ref[pl.ds(0, KY * KZ, stride=2), :] + rows_ref[pl.ds(1, KY * KZ, stride=2), :]
    channels = modes_ref.shape[1] // KY
    groups = channels // GROUP
    depth = conv_ref.shape[1]
    width = 3 * channels
    conv_scratch[...] = conv_ref[...]
    taps = jnp.concatenate([taps_ref[:width, :], taps_ref[2 * width :, :]], axis=0)
    cells = jnp.concatenate([before_ref[...], after_ref[...]], axis=1)
    sums = product(doubled_taps(taps), doubled_cells(cells), ((1,), (0,)))
    for row, values in ((0, sums[:width, :depth]), (rows_y - 1, sums[width:, depth:])):
        place = pl.ds(row, channels, stride=rows_y)
        parts = [values[r * channels : (r + 1) * channels] for r in range(3)]
        conv_scratch[place, :] = conv_scratch[place, :] + shifted_sum(parts, depth)
    for mode in range(KY):
        for part in range(2):
            modes_ref[part * KZ : (part + 1) * KZ, mode * channels : (mode + 1) * channels] = pairs[
                mode * KZ : (mode + 1) * KZ, part * channels : (part + 1) * channels
            ]
    deep = product_of_halves(
        halves_of(modes_ref[...]), (deep_high[...], deep_low[...]), ((0,), (0,))
    )
    for group in range(groups):
        for part in range(2):
            for mode in range(KY):
                row = (part * KY + mode) * GROUP
                place = mode * channels + group * GROUP
                middle_ref[row : row + GROUP, group * LANES : (group + 1) * LANES] = deep[
                    place : place + GROUP, part * LANES : (part + 1) * LANES
                ]
    wide = (wide_high[...], wide_low[...])
    block = wide_high.shape[0]
    for first in range(0, groups, 2):
        summed = product_of_halves(
            wide,
            halves_of(middle_ref[:, first * LANES : (first + 2) * LANES]),
            ((1,), (0,)),
        )
        for side in range(2):
            start = (first + side) * block
            value = (
                summed[:, side * LANES : (side + 1) * LANES] + conv_scratch[start : start + block, :]
            )
            out_ref[start : start + block, :] = (
                0.5 * value * (1.0 + lax.erf(value * math.sqrt(0.5)))
            )


def local(features, conv_weight, conv_bias, spectral_weight):
    channels, rows_x, rows_y, depth = features.shape
    count_x = lax.axis_size("gx")
    count_y = lax.axis_size("gy")
    length_x = rows_x * count_x
    length_y = rows_y * count_y
    norm_factor = 1.0 / math.sqrt(length_x * length_y * depth)
    pairs = KY * KZ
    owners = ("gx", "gy")
    devices = count_x * count_y
    halves = devices // pairs
    share = KX // halves
    params = pltpu.CompilerParams(vmem_limit_bytes=48 * 1024 * 1024)
    cells = features.reshape(channels * rows_y, depth)

    left = lax.ppermute(features, "gx", [(i, i + 1) for i in range(count_x - 1)])
    right = lax.ppermute(features, "gx", [(i + 1, i) for i in range(count_x - 1)])
    left = left.reshape(cells.shape)
    right = right.reshape(cells.shape)
    edge = jax.ShapeDtypeStruct((3 * channels, depth), f32)
    tails, heads = pl.pallas_call(
        lambda *refs: edges_kernel(*refs, rows_y=rows_y, channels=channels),
        out_shape=(edge, edge),
        compiler_params=params,
        name="edges",
    )(left, cells, right)
    before = lax.ppermute(tails, "gy", [(i, i + 1) for i in range(count_y - 1)])
    after = lax.ppermute(heads, "gy", [(i + 1, i) for i in range(count_y - 1)])

    wide, deep = forward_tables(rows_y, length_y, depth)
    outgoing = pl.pallas_call(
        forward_kernel,
        out_shape=jax.ShapeDtypeStruct((devices, LANES), f32),
        scratch_shapes=[
            pltpu.VMEM((KY * channels, 2 * depth), f32),
            pltpu.VMEM((pairs, LANES), f32),
        ],
        compiler_params=params,
        name="forward",
    )(cells, *fixed_halves(wide), *fixed_halves(deep))
    arrived = lax.all_to_all(outgoing, owners, 0, 0, tiled=True)

    device = lax.axis_index("gx") * count_y + lax.axis_index("gy")
    long_modes = device % halves * share + jnp.arange(share, dtype=jnp.int32)
    long_modes = jnp.where(long_modes < KX // 2, long_modes, length_x - KX + long_modes)
    wide_mode = device // halves // KZ
    wide_mode = jnp.where(wide_mode < KY // 2, wide_mode, length_y - KY + wide_mode)
    places = jnp.arange(devices, dtype=jnp.int32)
    steps = length_y // length_x * (long_modes[:, None] * (places // count_y)[None, :])
    steps = (steps + wide_mode * rows_y * (places % count_y)[None, :]) % length_y
    angle = 2.0 * math.pi / length_y * steps.astype(f32)
    basis = jnp.concatenate([jnp.cos(angle), jnp.sin(angle)], axis=0)
    returning = pl.pallas_call(
        lambda *refs: middle_kernel(*refs, channels=channels, norm_factor=norm_factor),
        out_shape=jax.ShapeDtypeStruct((devices, LANES), f32),
        compiler_params=params,
        name="middle",
    )(arrived, basis, spectral_weight)
    whole = lax.all_to_all(returning, owners, 0, 0, tiled=True)

    taps = jnp.transpose(conv_weight, (1, 2, 4, 0, 3)).reshape(9 * channels, 3 * channels)
    local_term = pl.pallas_call(
        lambda *refs: conv_kernel(*refs, rows_y=rows_y, channels=channels, depth=depth),
        out_shape=jax.ShapeDtypeStruct((channels * rows_y, depth), f32),
        scratch_shapes=[
            pltpu.VMEM((9 * channels, 9 * channels), bf16),
            pltpu.VMEM((rows_y + 2, 9 * channels, depth), f32),
        ],
        compiler_params=params,
        name="conv",
    )(left, cells, right, taps, jnp.broadcast_to(conv_bias[:, None], (channels, depth)))

    wide, deep = inverse_tables(rows_y, length_y, depth, norm_factor)
    layer_out = pl.pallas_call(
        lambda *refs: inverse_kernel(*refs, rows_y=rows_y),
        out_shape=jax.ShapeDtypeStruct((channels * rows_y, depth), f32),
        scratch_shapes=[
            pltpu.VMEM((2 * KZ, KY * channels), f32),
            pltpu.VMEM((2 * KY * GROUP, channels // GROUP * LANES), f32),
            pltpu.VMEM((channels * rows_y, depth), f32),
        ],
        compiler_params=params,
        name="inverse",
    )(whole, *fixed_halves(wide), *fixed_halves(deep), local_term, before, after, taps)
    return layer_out.reshape(features.shape)


def solution(mesh):
    return jax.shard_map(
        local,
        mesh=mesh,
        in_specs=(P(None, "gx", "gy", None), P(), P(), P(("gx", "gy"), None)),
        out_specs=P(None, "gx", "gy", None),
        check_vma=False,
    )
```

profile of v0, /device:TPU:1, one launch (start us, length us, event | category | flops | bytes accessed | tf_op | source)
XLA Modules:
  0.0 80.4 jit_solution(16405483196656625668)
XLA Ops:
  0.0 5.0 %collective-permute-start = (f32[32,1,32,128]{3,2,1,0:T(8,128)}, f32[32,1,32,128]{3,2,1,0:T(8,128)S(1)}, u32[]{:S(2)}, u32[]{:S(2)}) collective-permute-start(f32[32,1,32,128]{3,2,1,0:T(8,128)} %param.12), channel_id=1, source_target_pairs={{0,8},{8,16},{16,24},{24,32},{32,40},{40,48},{48,56},{56,64},{64,7... | collective-permute-start | bytes 1572872 | tf_op jit(solution)/shard_map/ppermute | solution.py:304
  5.0 1.3 %collective-permute-start.1 = (f32[32,1,32,128]{3,2,1,0:T(8,128)}, f32[32,1,32,128]{3,2,1,0:T(8,128)S(1)}, u32[]{:S(2)}, u32[]{:S(2)}) collective-permute-start(f32[32,1,32,128]{3,2,1,0:T(8,128)} %param.12), channel_id=1, source_target_pairs={{8,0},{16,8},{24,16},{32,24},{40,32},{48,40},{56,48},{64,56},{72,6... | collective-permute-start | bytes 1572872 | tf_op jit(solution)/shard_map/ppermute | solution.py:305
  6.3 0.0 copy-start
  6.3 1.0 %copy-done = f32[32,1,32,128]{3,2,1,0:T(8,128)S(1)} copy-done((f32[32,1,32,128]{3,2,1,0:T(8,128)S(1)}, f32[32,1,32,128]{3,2,1,0:T(8,128)}, u32[]{:S(2)}) %copy-start) | copy-done | bytes 524312
  7.4 0.9 %copy-done.4 = bf16[256,256]{1,0:T(8,128)(2,1)S(1)} copy-done((bf16[256,256]{1,0:T(8,128)(2,1)S(1)}, bf16[256,256]{1,0:T(8,128)(2,1)}, u32[]{:S(2)}) %copy-start.4) | copy-done | bytes 131096
  8.3 0.9 %copy-done.5 = bf16[256,256]{1,0:T(8,128)(2,1)S(1)} copy-done((bf16[256,256]{1,0:T(8,128)(2,1)S(1)}, bf16[256,256]{1,0:T(8,128)(2,1)}, u32[]{:S(2)}) %copy-start.5) | copy-done | bytes 131096
  9.2 1.5 %forward.1 = f32[512,128]{1,0:T(8,128)} custom-call(f32[1024,128]{1,0:T(8,128)S(1)} %bitcast.15, bf16[256,256]{1,0:T(8,128)(2,1)S(1)} %copy-done.4, bf16[256,256]{1,0:T(8,128)(2,1)S(1)} %copy-done.5, bf16[32,256]{1,0:T(8,128)(2,1)S(1)} %copy-done.9, bf16[32,256]{1,0:T(8,128)(2,1)S(1)} %copy-done.10), custom_call_target="tpu_custom_call" | custom-call | tf_op jit(solution)/shard_map/forward/pallas_call | solution.py:319
  10.7 23.1 %all-to-all-start = ((f32[512,1,128]{2,1,0:T(1,128)}), f32[512,1,128]{2,1,0:T(1,128)S(1)}, u32[]{:S(2)}, u32[]{:S(2)}) async-start(f32[512,1,128]{2,1,0:T(1,128)} %bitcast.2), calls=%async_computation | async-start | bytes 524288 | tf_op jit(solution)/shard_map/all_to_all | solution.py:329
  33.8 0.0 copy-start.6
  33.8 0.2 fusion.4
  34.0 17.1 %all-to-all-done = f32[512,1,128]{2,1,0:T(1,128)S(1)} async-done(((f32[512,1,128]{2,1,0:T(1,128)}), f32[512,1,128]{2,1,0:T(1,128)S(1)}, u32[]{:S(2)}, u32[]{:S(2)}) %all-to-all-start) | async-done | bytes 262176 | tf_op jit(solution)/shard_map/all_to_all | solution.py:329
  51.1 1.8 %middle.1 = f32[512,128]{1,0:T(8,128)} custom-call(f32[512,128]{1,0:T(8,128)S(1)} %bitcast.23, f32[16,512]{1,0:T(8,128)S(1)} %pad_maximum_fusion.refs_1_, f32[8,2048]{1,0:T(8,128)S(1)} %copy-done.6), custom_call_target="tpu_custom_call" | custom-call | tf_op jit(solution)/shard_map/middle/pallas_call | solution.py:341
  52.9 8.3 %all-to-all-start.1 = ((f32[512,1,128]{2,1,0:T(1,128)}), f32[512,1,128]{2,1,0:T(1,128)S(1)}, u32[]{:S(2)}, u32[]{:S(2)}) async-start(f32[512,1,128]{2,1,0:T(1,128)} %bitcast.5), calls=%async_computation.1 | async-start | bytes 524288 | tf_op jit(solution)/shard_map/all_to_all | solution.py:347
  61.3 0.0 copy-start.11
  61.3 0.1 edges.1
  61.4 3.3 %collective-permute-start.2 = (f32[96,128]{1,0:T(8,128)S(1)}, f32[96,128]{1,0:T(8,128)S(1)}, u32[]{:S(2)}, u32[]{:S(2)}) collective-permute-start(f32[96,128]{1,0:T(8,128)S(1)} %get-tuple-element.7), channel_id=1, source_target_pairs={{0,1},{1,2},{2,3},{3,4},{4,5},{5,6},{6,7},{8,9},{9,10},{10,11},{11... | collective-permute-start | bytes 147464 | tf_op jit(solution)/shard_map/ppermute | solution.py:315
  64.7 4.1 %collective-permute-start.3 = (f32[96,128]{1,0:T(8,128)S(1)}, f32[96,128]{1,0:T(8,128)S(1)}, u32[]{:S(2)}, u32[]{:S(2)}) collective-permute-start(f32[96,128]{1,0:T(8,128)S(1)} %get-tuple-element.8), channel_id=1, source_target_pairs={{1,0},{2,1},{3,2},{4,3},{5,4},{6,5},{7,6},{9,8},{10,9},{11,10},{12... | collective-permute-start | bytes 147464 | tf_op jit(solution)/shard_map/ppermute | solution.py:316
  68.8 0.3 copy.19
  69.1 0.2 reshape.54.refs_3_.refs_8_
  69.3 0.4 copy-done.12
  69.7 0.1 broadcast_in_dim.2.refs_4_
  69.8 7.5 %conv.1.refs_5_ = f32[1024,128]{1,0:T(8,128)S(1)} custom-call(f32[1024,128]{1,0:T(8,128)S(1)} %bitcast.19, f32[1024,128]{1,0:T(8,128)S(1)} %bitcast.17, f32[1024,128]{1,0:T(8,128)S(1)} %bitcast.21, f32[288,96]{1,0:T(8,128)S(1)} %reshape.54.refs_3_.refs_8_, f32[32,128]{1,0:T(8,128)S(1)} %broadcast_in_dim.2.refs_4_), custom_call_target="tpu_custom_call" | custom-call | tf_op jit(solution)/shard_map/conv/pallas_call | solution.py:350
  77.4 1.0 %all-to-all-done.1 = f32[512,1,128]{2,1,0:T(1,128)S(1)} async-done(((f32[512,1,128]{2,1,0:T(1,128)}), f32[512,1,128]{2,1,0:T(1,128)S(1)}, u32[]{:S(2)}, u32[]{:S(2)}) %all-to-all-start.1) | async-done | bytes 262176 | tf_op jit(solution)/shard_map/all_to_all | solution.py:347
  78.4 2.0 %inverse.1 = f32[1024,128]{1,0:T(8,128)} custom-call(f32[512,128]{1,0:T(8,128)S(1)} %bitcast.22, bf16[256,256]{1,0:T(8,128)(2,1)S(1)} %copy-done.2, bf16[256,256]{1,0:T(8,128)(2,1)S(1)} %copy-done.3, bf16[32,256]{1,0:T(8,128)(2,1)S(1)} %copy-done.7, bf16[32,256]{1,0:T(8,128)(2,1)S(1)} %copy-done.8, f32[1024,128]{1,0:T(8,128)S(1)} %conv.1.refs_5_, ...), custom_call_target="tpu_custom_call" | custom-call | tf_op jit(solution)/shard_map/inverse/pallas_call | solution.py:362
  (26 shorter events, 0.1 us)
Async XLA Ops:
  0.0 6.3 %copy-start.9 = (bf16[32,256]{1,0:T(8,128)(2,1)S(1)}, bf16[32,256]{1,0:T(8,128)(2,1)}, u32[]{:S(2)}) copy-start(bf16[32,256]{1,0:T(8,128)(2,1)} %constant.114.clone.deep_high) | copy-start | bytes 49156
  0.0 6.3 %copy-start.10 = (bf16[32,256]{1,0:T(8,128)(2,1)S(1)}, bf16[32,256]{1,0:T(8,128)(2,1)}, u32[]{:S(2)}) copy-start(bf16[32,256]{1,0:T(8,128)(2,1)} %constant.115.clone.deep_low) | copy-start | bytes 49156
  0.0 61.2 %collective-permute-start = (f32[32,1,32,128]{3,2,1,0:T(8,128)}, f32[32,1,32,128]{3,2,1,0:T(8,128)S(1)}, u32[]{:S(2)}, u32[]{:S(2)}) collective-permute-start(f32[32,1,32,128]{3,2,1,0:T(8,128)} %param.12), channel_id=1, source_target_pairs={{0,8},{8,16},{16,24},{24,32},{32,40},{40,48},{48,56},{56,64},{64,7... | collective-permute-start | bytes 1572872 | tf_op jit(solution)/shard_map/ppermute | solution.py:304
  5.0 56.3 %collective-permute-start.1 = (f32[32,1,32,128]{3,2,1,0:T(8,128)}, f32[32,1,32,128]{3,2,1,0:T(8,128)S(1)}, u32[]{:S(2)}, u32[]{:S(2)}) collective-permute-start(f32[32,1,32,128]{3,2,1,0:T(8,128)} %param.12), channel_id=1, source_target_pairs={{8,0},{16,8},{24,16},{32,24},{40,32},{48,40},{56,48},{64,56},{72,6... | collective-permute-start | bytes 1572872 | tf_op jit(solution)/shard_map/ppermute | solution.py:305
  6.3 1.0 %copy-start = (f32[32,1,32,128]{3,2,1,0:T(8,128)S(1)}, f32[32,1,32,128]{3,2,1,0:T(8,128)}, u32[]{:S(2)}) copy-start(f32[32,1,32,128]{3,2,1,0:T(8,128)} %param.12) | copy-start | bytes 1572868
  7.4 0.9 %copy-start.4 = (bf16[256,256]{1,0:T(8,128)(2,1)S(1)}, bf16[256,256]{1,0:T(8,128)(2,1)}, u32[]{:S(2)}) copy-start(bf16[256,256]{1,0:T(8,128)(2,1)} %constant.112.clone.wide_high) | copy-start | bytes 393220
  8.3 0.9 %copy-start.5 = (bf16[256,256]{1,0:T(8,128)(2,1)S(1)}, bf16[256,256]{1,0:T(8,128)(2,1)}, u32[]{:S(2)}) copy-start(bf16[256,256]{1,0:T(8,128)(2,1)} %constant.113.clone.wide_low) | copy-start | bytes 393220
  10.7 40.4 %all-to-all-start = ((f32[512,1,128]{2,1,0:T(1,128)}), f32[512,1,128]{2,1,0:T(1,128)S(1)}, u32[]{:S(2)}, u32[]{:S(2)}) async-start(f32[512,1,128]{2,1,0:T(1,128)} %bitcast.2), calls=%async_computation | async-start | bytes 524288 | tf_op jit(solution)/shard_map/all_to_all | solution.py:329
  33.8 17.3 %copy-start.6 = (f32[8,2048]{1,0:T(8,128)S(1)}, f32[8,2048]{1,0:T(8,128)}, u32[]{:S(2)}) copy-start(f32[8,2048]{1,0:T(8,128)} %refs_2_.2) | copy-start | bytes 196612
  51.1 10.2 %copy-start.1 = (f32[32,1,32,128]{3,2,1,0:T(8,128)S(1)}, f32[32,1,32,128]{3,2,1,0:T(8,128)}, u32[]{:S(2)}) copy-start(f32[32,1,32,128]{3,2,1,0:T(8,128)} %param.12) | copy-start | bytes 1572868
  52.9 25.5 %all-to-all-start.1 = ((f32[512,1,128]{2,1,0:T(1,128)}), f32[512,1,128]{2,1,0:T(1,128)S(1)}, u32[]{:S(2)}, u32[]{:S(2)}) async-start(f32[512,1,128]{2,1,0:T(1,128)} %bitcast.5), calls=%async_computation.1 | async-start | bytes 524288 | tf_op jit(solution)/shard_map/all_to_all | solution.py:347
  61.3 7.5 %copy-start.11 = (f32[3,3,3,32,32]{4,3,2,1,0:T(8,128)S(1)}, f32[3,3,3,32,32]{4,3,2,1,0:T(8,128)}, u32[]{:S(2)}) copy-start(f32[3,3,3,32,32]{4,3,2,1,0:T(8,128)} %param.13) | copy-start | bytes 331780
  61.4 16.0 %collective-permute-start.2 = (f32[96,128]{1,0:T(8,128)S(1)}, f32[96,128]{1,0:T(8,128)S(1)}, u32[]{:S(2)}, u32[]{:S(2)}) collective-permute-start(f32[96,128]{1,0:T(8,128)S(1)} %get-tuple-element.7), channel_id=1, source_target_pairs={{0,1},{1,2},{2,3},{3,4},{4,5},{5,6},{6,7},{8,9},{9,10},{10,11},{11... | collective-permute-start | bytes 147464 | tf_op jit(solution)/shard_map/ppermute | solution.py:315
  64.7 12.7 %collective-permute-start.3 = (f32[96,128]{1,0:T(8,128)S(1)}, f32[96,128]{1,0:T(8,128)S(1)}, u32[]{:S(2)}, u32[]{:S(2)}) collective-permute-start(f32[96,128]{1,0:T(8,128)S(1)} %get-tuple-element.8), channel_id=1, source_target_pairs={{1,0},{2,1},{3,2},{4,3},{5,4},{6,5},{7,6},{9,8},{10,9},{11,10},{12... | collective-permute-start | bytes 147464 | tf_op jit(solution)/shard_map/ppermute | solution.py:316
  69.1 0.7 copy-start.12
  69.8 8.6 %copy-start.2 = (bf16[256,256]{1,0:T(8,128)(2,1)S(1)}, bf16[256,256]{1,0:T(8,128)(2,1)}, u32[]{:S(2)}) copy-start(bf16[256,256]{1,0:T(8,128)(2,1)} %constant.116.clone.refs_1_) | copy-start | bytes 393220
  69.8 8.6 %copy-start.3 = (bf16[256,256]{1,0:T(8,128)(2,1)S(1)}, bf16[256,256]{1,0:T(8,128)(2,1)}, u32[]{:S(2)}) copy-start(bf16[256,256]{1,0:T(8,128)(2,1)} %constant.117.clone.refs_2_) | copy-start | bytes 393220
  69.8 8.6 %copy-start.7 = (bf16[32,256]{1,0:T(8,128)(2,1)S(1)}, bf16[32,256]{1,0:T(8,128)(2,1)}, u32[]{:S(2)}) copy-start(bf16[32,256]{1,0:T(8,128)(2,1)} %constant.118.clone.refs_3_) | copy-start | bytes 49156
  69.8 8.6 %copy-start.8 = (bf16[32,256]{1,0:T(8,128)(2,1)S(1)}, bf16[32,256]{1,0:T(8,128)(2,1)}, u32[]{:S(2)}) copy-start(bf16[32,256]{1,0:T(8,128)(2,1)} %constant.119.clone.refs_4_) | copy-start | bytes 49156
where the time goes:
time: 80.8 us; the launch traced here: 80.4 us
  starting transfers between devices  45.1 us (56%)
  waiting for transfers between devices  18.1 us (22%)
  Pallas kernels  12.9 us (16%)
  local copies, waits for them, and re-layouts  3.86 us (5%)
    all_to_all x1, starting transfers between devices, local(): arrived = lax.all_to_all(outgoing, owners, 0, 0, tiled=True)  23.1 us
    all_to_all x1, waiting for transfers between devices, local(): arrived = lax.all_to_all(outgoing, owners, 0, 0, tiled=True)  17.1 us
    all_to_all x1, starting transfers between devices, local(): whole = lax.all_to_all(returning, owners, 0, 0, tiled=True)  8.35 us
    pallas_call x1, Pallas kernels, local(): pl.pallas_call(lambda *refs: conv_kernel(*refs, rows_y=rows_y, channels=c...  7.54 us
    ppermute x1, starting transfers between devices, local(): lax.ppermute(features, 'gx', [(i, i + 1) for i in range(count_x - 1)])  4.98 us
    ppermute x1, starting transfers between devices, local(): after = lax.ppermute(heads, 'gy', [(i + 1, i) for i in range(count_y - 1)])  4.09 us
    ppermute x1, starting transfers between devices, local(): before = lax.ppermute(tails, 'gy', [(i, i + 1) for i in range(count_y - 1)])  3.34 us
    unnamed x26, local copies, waits for them, and re-layouts  3.29 us
  transfers between devices with their start and end apart: 6, of which 2 were waited for; matrix products, arithmetic and copies ran while one was open for 1% of the time, Pallas kernels for 14%

commit v1 on v0

--- a/solution.py
+++ b/solution.py
@@ -47,12 +47,17 @@
     return np.where(series < number // 2, series, series - number)
 
 
+def deep_angles(depth):
+    order = np.concatenate([np.arange(0, KZ, 2), np.arange(1, KZ, 2)])
+    return order, 2.0 * np.pi / depth * np.outer(order, np.arange(depth))
+
+
 def forward_tables(rows_y, length_y, depth):
     angle = 2.0 * np.pi / length_y * np.outer(signed_modes(KY), np.arange(rows_y))
     same = np.eye(GROUP)
     wide = np.einsum("rby,ij->rbijy", np.stack([np.cos(angle), -np.sin(angle)]), same)
     wide = wide.reshape(2 * KY * GROUP, GROUP * rows_y)
-    angle = 2.0 * np.pi / depth * np.outer(np.arange(KZ), np.arange(depth))
+    _, angle = deep_angles(depth)
     deep_cos = np.cos(angle)
     deep_sin = np.sin(angle)
     deep = np.concatenate(
@@ -70,8 +75,8 @@
     same = np.eye(GROUP)
     wide = np.einsum("ryb,ij->iyrbj", np.stack([np.cos(angle), -np.sin(angle)]), same)
     wide = wide.reshape(GROUP * rows_y, 2 * KY * GROUP)
-    angle = 2.0 * np.pi / depth * np.outer(np.arange(KZ), np.arange(depth))
-    factor = norm_factor * np.where(np.arange(KZ) == 0, 1.0, 2.0)[:, None]
+    order, angle = deep_angles(depth)
+    factor = norm_factor * np.where(order == 0, 1.0, 2.0)[:, None]
     deep_cos = factor * np.cos(angle)
     deep_sin = factor * np.sin(angle)
     deep = np.concatenate(
@@ -85,13 +90,31 @@
 
 
 def forward_kernel(
-    cells_ref, wide_high, wide_low, deep_high, deep_low, out_ref, middle_ref, pair_ref
+    cells_hbm, wide_high_hbm, wide_low_hbm, deep_high_hbm, deep_low_hbm, out_ref,
+    cells_ref, wide_high, wide_low, deep_high, deep_low, middle_ref, sems
 ):
+    half = cells_ref.shape[0] // 2
+    chunks = [pl.ds(0, half), pl.ds(half, half)]
+    moves = [
+        (wide_high_hbm, wide_high),
+        (wide_low_hbm, wide_low),
+        (cells_hbm.at[chunks[0]], cells_ref.at[chunks[0]]),
+        (cells_hbm.at[chunks[1]], cells_ref.at[chunks[1]]),
+        (deep_high_hbm, deep_high),
+        (deep_low_hbm, deep_low),
+    ]
+    copies = [pltpu.make_async_copy(*pair, sems.at[i]) for i, pair in enumerate(moves)]
+    for copy in copies:
+        copy.start()
+    for copy in copies[:3]:
+        copy.wait()
     channels = middle_ref.shape[0] // KY
     block = wide_high.shape[1]
     groups = channels // GROUP
     wide = (wide_high[...], wide_low[...])
     for first in range(0, groups, 2):
+        if first == groups // 2:
+            copies[3].wait()
         cells = jnp.concatenate(
             [
                 cells_ref[first * block : (first + 1) * block, :],
@@ -108,29 +131,71 @@
                     middle_ref[place : place + GROUP, part * LANES : (part + 1) * LANES] = (
                         summed[row : row + GROUP, side * LANES : (side + 1) * LANES]
                     )
+    copies[4].wait()
+    copies[5].wait()
     modes = product_of_halves(
         (deep_high[...], deep_low[...]), halves_of(middle_ref[...]), ((1,), (1,))
     )
-    pair_ref[...] = jnp.zeros_like(pair_ref)
     for mode in range(KY):
-        first = mode * channels
         for part in range(2):
-            pair_ref[mode * KZ : (mode + 1) * KZ, part * channels : (part + 1) * channels] = (
-                modes[part * KZ : (part + 1) * KZ, first : first + channels]
-            )
-    pairs = pair_ref[...]
-    out_ref[pl.ds(0, KY * KZ, stride=2), :] = pairs
-    out_ref[pl.ds(1, KY * KZ, stride=2), :] = pairs
-
-
-def middle_kernel(rows_ref, basis_ref, weight_ref, out_ref, *, channels, norm_factor):
-    basis = basis_ref[...]
-    share = basis.shape[0] // 2
-    sums = norm_factor * jnp.dot(
-        basis, rows_ref[...], precision=highest, preferred_element_type=f32
-    )
-    hat_real = sums[:share, :channels] + sums[share:, channels : 2 * channels]
-    hat_imag = sums[:share, channels : 2 * channels] - sums[share:, :channels]
+            for odd in range(2):
+                lane = odd * 2 * channels + part * channels
+                row = (part * 2 + odd) * (KZ // 2)
+                out_ref[mode * KZ // 2 : (mode + 1) * KZ // 2, lane : lane + channels] = modes[
+                    row : row + KZ // 2, mode * channels : (mode + 1) * channels
+                ]
+
+
+def crossed(value, channels, sign):
+    lane = lax.broadcasted_iota(jnp.int32, value.shape, 1)
+    width = value.shape[1]
+    return jnp.where(
+        lane % (2 * channels) < channels,
+        sign * pltpu.roll(value, width - channels, axis=1),
+        -sign * pltpu.roll(value, channels, axis=1),
+    )
+
+
+def gather_kernel(rows_ref, basis_ref, out_ref, *, channels, share):
+    length = basis_ref.shape[1]
+    cells = jnp.concatenate(
+        [rows_ref[pl.ds(0, length, stride=2), :], rows_ref[pl.ds(1, length, stride=2), :]], axis=1
+    )
+    sums = jnp.dot(basis_ref[...], cells, precision=highest, preferred_element_type=f32)
+    for tile in range(2):
+        lanes = slice(tile * LANES, (tile + 1) * LANES)
+        modes = sums[:KX, lanes] + crossed(sums[KX:, lanes], channels, 1.0)
+        start = 2 * tile * KX
+        out_ref[start : start + KX, :] = modes
+        out_ref[start + KX : start + 2 * KX, :] = pltpu.roll(modes, LANES // 2, axis=1)
+
+
+def spread_kernel(rows_ref, basis_ref, out_ref, *, channels):
+    length = basis_ref.shape[1]
+    for tile in range(2):
+        start = 2 * tile * KX
+        even = rows_ref[start : start + KX, :]
+        odd = pltpu.roll(rows_ref[start + KX : start + 2 * KX, :], LANES // 2, axis=1)
+        lane = lax.broadcasted_iota(jnp.int32, even.shape, 1)
+        modes = jnp.where(lane < LANES // 2, even, odd)
+        both = jnp.concatenate([modes, crossed(modes, channels, -1.0)], axis=0)
+        out_ref[pl.ds(tile, length, stride=2), :] = lax.dot_general(
+            basis_ref[...],
+            both,
+            (((0,), (0,)), ((), ())),
+            precision=highest,
+            preferred_element_type=f32,
+        )
+
+
+def middle_kernel(rows_ref, weight_ref, out_ref, *, channels, norm_factor):
+    share = weight_ref.shape[0]
+    sums = rows_ref[:share, :]
+    for start in range(share, rows_ref.shape[0], share):
+        sums = sums + rows_ref[start : start + share, :]
+    sums = norm_factor * sums
+    hat_real = sums[:, :channels]
+    hat_imag = sums[:, channels : 2 * channels]
     size = channels * channels
     lane = lax.broadcasted_iota(jnp.int32, (channels, size), 1)
     row = lax.broadcasted_iota(jnp.int32, (channels, size), 0)
@@ -158,16 +223,9 @@
     lane = lax.broadcasted_iota(jnp.int32, (share, LANES), 1)
     mixed_real = mixed[:share]
     mixed_imag = mixed[share:]
-    stacked = jnp.concatenate(
-        [
-            jnp.where(lane < channels, mixed_real, mixed_imag),
-            jnp.where(lane < channels, -mixed_imag, mixed_real),
-        ],
-        axis=0,
-    )
-    out_ref[...] = lax.dot_general(
-        basis, stacked, (((0,), (0,)), ((), ())), precision=highest, preferred_element_type=f32
-    )
+    mixed = jnp.where(lane < channels, mixed_real, mixed_imag)
+    for start in range(0, out_ref.shape[0], share):
+        out_ref[start : start + share, :] = mixed
 
 
 def edges_kernel(left_ref, cells_ref, right_ref, tails_ref, heads_ref, *, rows_y, channels):
@@ -195,32 +253,23 @@
     return parts[1] + below + above
 
 
-def conv_kernel(
-    left_ref, cells_ref, right_ref, taps_ref, bias_ref, out_ref, taps_scratch, sums_scratch,
-    *, rows_y, channels, depth
-):
-    planes = (left_ref, cells_ref, right_ref)
+def conv_kernel(*refs, planes, rows_y, channels, depth):
+    plane_refs = refs[: len(planes)]
+    taps_ref, base_ref, out_ref, sums_scratch = refs[len(planes) :]
     width = 3 * channels
-    taps_scratch[...] = doubled_taps(taps_ref[...])
+    taps = jnp.concatenate(
+        [taps_ref[:, plane * channels : (plane + 1) * channels] for plane in planes], axis=1
+    )
+    taps = doubled_taps(taps)
     sums_scratch[0, :width, :] = jnp.zeros((width, depth), f32)
     sums_scratch[rows_y + 1, 2 * width :, :] = jnp.zeros((width, depth), f32)
 
     def row_cells(row):
         return jnp.concatenate(
-            [plane[pl.ds(row, channels, stride=rows_y), :] for plane in planes], axis=0
+            [plane[pl.ds(row, channels, stride=rows_y), :] for plane in plane_refs], axis=0
         )
 
-    def multiply(step, _):
-        cells = jnp.concatenate([row_cells(2 * step), row_cells(2 * step + 1)], axis=1)
-        sums = product(taps_scratch[...], doubled_cells(cells), ((1,), (0,)))
-        sums_scratch[2 * step + 1] = sums[:, :depth]
-        sums_scratch[2 * step + 2] = sums[:, depth:]
-        return 0
-
-    lax.fori_loop(0, rows_y // 2, multiply, 0)
-    bias = bias_ref[...]
-
-    def collect(row, _):
+    def collect(row):
         parts = []
         for shift in range(3):
             first = shift * channels
@@ -229,17 +278,26 @@
                 + sums_scratch[row + 1, width + first : width + first + channels, :]
                 + sums_scratch[row + 2, 2 * width + first : 2 * width + first + channels, :]
             )
-        out_ref[pl.ds(row, channels, stride=rows_y), :] = shifted_sum(parts, depth) + bias
-        return 0
-
-    lax.fori_loop(0, rows_y, collect, 0)
+        place = pl.ds(row, channels, stride=rows_y)
+        base = base_ref[place, :] if base_ref.shape == out_ref.shape else base_ref[...]
+        out_ref[place, :] = shifted_sum(parts, depth) + base
+
+    for step in range(rows_y // 2):
+        cells = jnp.concatenate([row_cells(2 * step), row_cells(2 * step + 1)], axis=1)
+        sums = product(taps, doubled_cells(cells), ((1,), (0,)))
+        sums_scratch[2 * step + 1] = sums[:, :depth]
+        sums_scratch[2 * step + 2] = sums[:, depth:]
+        if step:
+            collect(2 * step - 2)
+            collect(2 * step - 1)
+    collect(rows_y - 2)
+    collect(rows_y - 1)
 
 
 def inverse_kernel(
     rows_ref, wide_high, wide_low, deep_high, deep_low, conv_ref, before_ref, after_ref, taps_ref,
     out_ref, modes_ref, middle_ref, conv_scratch, *, rows_y
 ):
-    pairs = rows_ref[pl.ds(0, KY * KZ, stride=2), :] + rows_ref[pl.ds(1, KY * KZ, stride=2), :]
     channels = modes_ref.shape[1] // KY
     groups = channels // GROUP
     depth = conv_ref.shape[1]
@@ -254,9 +312,12 @@
         conv_scratch[place, :] = conv_scratch[place, :] + shifted_sum(parts, depth)
     for mode in range(KY):
         for part in range(2):
-            modes_ref[part * KZ : (part + 1) * KZ, mode * channels : (mode + 1) * channels] = pairs[
-                mode * KZ : (mode + 1) * KZ, part * channels : (part + 1) * channels
-            ]
+            for odd in range(2):
+                lane = odd * 2 * channels + part * channels
+                row = (part * 2 + odd) * (KZ // 2)
+                modes_ref[row : row + KZ // 2, mode * channels : (mode + 1) * channels] = rows_ref[
+                    mode * KZ // 2 : (mode + 1) * KZ // 2, lane : lane + channels
+                ]
     deep = product_of_halves(
         halves_of(modes_ref[...]), (deep_high[...], deep_low[...]), ((0,), (0,))
     )
@@ -294,12 +355,42 @@
     length_y = rows_y * count_y
     norm_factor = 1.0 / math.sqrt(length_x * length_y * depth)
     pairs = KY * KZ
-    owners = ("gx", "gy")
     devices = count_x * count_y
     halves = devices // pairs
     share = KX // halves
     params = pltpu.CompilerParams(vmem_limit_bytes=48 * 1024 * 1024)
     cells = features.reshape(channels * rows_y, depth)
+
+    wide, deep = forward_tables(rows_y, length_y, depth)
+    outgoing = pl.pallas_call(
+        forward_kernel,
+        out_shape=jax.ShapeDtypeStruct((pairs // 2, LANES), f32),
+        in_specs=[pl.BlockSpec(memory_space=pltpu.HBM)] * 5,
+        scratch_shapes=[
+            pltpu.VMEM(cells.shape, f32),
+            pltpu.VMEM(wide.shape, bf16),
+            pltpu.VMEM(wide.shape, bf16),
+            pltpu.VMEM(deep.shape, bf16),
+            pltpu.VMEM(deep.shape, bf16),
+            pltpu.VMEM((KY * channels, 2 * depth), f32),
+            pltpu.SemaphoreType.DMA((6,)),
+        ],
+        compiler_params=params,
+        name="forward",
+    )(cells, *fixed_halves(wide), *fixed_halves(deep))
+    taps = jnp.transpose(conv_weight, (1, 2, 4, 0, 3)).reshape(9 * channels, 3 * channels)
+    bias = jnp.broadcast_to(conv_bias[:, None], (channels, depth))
+
+    def conv(name, planes, *operands):
+        return pl.pallas_call(
+            lambda *refs: conv_kernel(
+                *refs, planes=planes, rows_y=rows_y, channels=channels, depth=depth
+            ),
+            out_shape=jax.ShapeDtypeStruct(cells.shape, f32),
+            scratch_shapes=[pltpu.VMEM((rows_y + 2, 9 * channels, depth), f32)],
+            compiler_params=params,
+            name=name,
+        )(*operands)
 
     left = lax.ppermute(features, "gx", [(i, i + 1) for i in range(count_x - 1)])
     right = lax.ppermute(features, "gx", [(i + 1, i) for i in range(count_x - 1)])
@@ -314,49 +405,42 @@
     )(left, cells, right)
     before = lax.ppermute(tails, "gy", [(i, i + 1) for i in range(count_y - 1)])
     after = lax.ppermute(heads, "gy", [(i + 1, i) for i in range(count_y - 1)])
-
-    wide, deep = forward_tables(rows_y, length_y, depth)
-    outgoing = pl.pallas_call(
-        forward_kernel,
-        out_shape=jax.ShapeDtypeStruct((devices, LANES), f32),
-        scratch_shapes=[
-            pltpu.VMEM((KY * channels, 2 * depth), f32),
-            pltpu.VMEM((pairs, LANES), f32),
-        ],
-        compiler_params=params,
-        name="forward",
-    )(cells, *fixed_halves(wide), *fixed_halves(deep))
-    arrived = lax.all_to_all(outgoing, owners, 0, 0, tiled=True)
-
-    device = lax.axis_index("gx") * count_y + lax.axis_index("gy")
-    long_modes = device % halves * share + jnp.arange(share, dtype=jnp.int32)
+    local_term = conv("conv", (0, 1, 2), left, cells, right, taps, bias)
+
+    long_modes = jnp.arange(KX, dtype=jnp.int32)
     long_modes = jnp.where(long_modes < KX // 2, long_modes, length_x - KX + long_modes)
-    wide_mode = device // halves // KZ
+    wide_mode = lax.axis_index("gx") * pairs // count_x // KZ
     wide_mode = jnp.where(wide_mode < KY // 2, wide_mode, length_y - KY + wide_mode)
-    places = jnp.arange(devices, dtype=jnp.int32)
-    steps = length_y // length_x * (long_modes[:, None] * (places // count_y)[None, :])
-    steps = (steps + wide_mode * rows_y * (places % count_y)[None, :]) % length_y
+    places = jnp.arange(length_x, dtype=jnp.int32)
+    steps = length_y // length_x * (long_modes[:, None] * places[None, :])
+    steps = (steps + wide_mode * rows_y * lax.axis_index("gy")) % length_y
     angle = 2.0 * math.pi / length_y * steps.astype(f32)
     basis = jnp.concatenate([jnp.cos(angle), jnp.sin(angle)], axis=0)
-    returning = pl.pallas_call(
+
+    def small(kernel, name, rows, *operands):
+        return pl.pallas_call(
+            kernel,
+            out_shape=jax.ShapeDtypeStruct((rows, LANES), f32),
+            compiler_params=params,
+            name=name,
+        )(*operands)
+
+    arrived = lax.all_to_all(outgoing, "gx", 0, 0, tiled=True)
+    partial_modes = small(
+        lambda *refs: gather_kernel(*refs, channels=channels, share=share),
+        "gather", count_y * share, arrived, basis,
+    )
+    owned = lax.all_to_all(partial_modes, "gy", 0, 0, tiled=True)
+    mixed = small(
         lambda *refs: middle_kernel(*refs, channels=channels, norm_factor=norm_factor),
-        out_shape=jax.ShapeDtypeStruct((devices, LANES), f32),
-        compiler_params=params,
-        name="middle",
-    )(arrived, basis, spectral_weight)
-    whole = lax.all_to_all(returning, owners, 0, 0, tiled=True)
-
-    taps = jnp.transpose(conv_weight, (1, 2, 4, 0, 3)).reshape(9 * channels, 3 * channels)
-    local_term = pl.pallas_call(
-        lambda *refs: conv_kernel(*refs, rows_y=rows_y, channels=channels, depth=depth),
-        out_shape=jax.ShapeDtypeStruct((channels * rows_y, depth), f32),
-        scratch_shapes=[
-            pltpu.VMEM((9 * channels, 9 * channels), bf16),
-            pltpu.VMEM((rows_y + 2, 9 * channels, depth), f32),
-        ],
-        compiler_params=params,
-        name="conv",
-    )(left, cells, right, taps, jnp.broadcast_to(conv_bias[:, None], (channels, depth)))
+        "middle", count_y * share, owned, spectral_weight,
+    )
+    shared = lax.all_to_all(mixed, "gy", 0, 0, tiled=True)
+    returning = small(
+        lambda *refs: spread_kernel(*refs, channels=channels),
+        "spread", pairs // 2, shared, basis,
+    )
+    whole = lax.all_to_all(returning, "gx", 0, 0, tiled=True)
 
     wide, deep = inverse_tables(rows_y, length_y, depth, norm_factor)
     layer_out = pl.pallas_call(

time: 80.8 us -> 80.5 us (level)
  blocking collectives: 0 us -> 19.3 us
  starting transfers between devices: 45.1 us -> 34.3 us
  Pallas kernels: 12.9 us -> 8.33 us
  waiting for transfers between devices: 18.1 us -> 13.8 us
    all_to_all x0 -> x2, blocking collectives: none -> 19.3 us  [the longest x1 11.5 us: local(): owned = lax.all_to_all(partial_modes, 'gy', 0, 0, tiled=True)]
    all_to_all x2, starting transfers between devices: 31.4 us -> 22.5 us  [the longest x1 17.9 us: local(): arrived = lax.all_to_all(outgoing, 'gx', 0, 0, tiled=True)]
    pallas_call x3 -> x5, Pallas kernels: 10.8 us -> 6.25 us  [the longest x1 2.32 us: conv(): pl.pallas_call(lambda *refs: conv_kernel(*refs, planes=planes, rows_y=row...]
    all_to_all x2, waiting for transfers between devices: 18.1 us -> 13.8 us  [the longest x1 10.9 us: local(): arrived = lax.all_to_all(outgoing, 'gx', 0, 0, tiled=True)]
    ppermute x1, starting transfers between devices: 4.09 us -> 1.92 us  [local(): after = lax.ppermute(heads, 'gy', [(i + 1, i) for i in range(count_y - 1)])]
  transfers between devices with their start and end apart: 6 -> 6, of which waited for: 2 -> 2; matrix products, arithmetic and copies ran while one was open for 1% -> 1% of each run, Pallas kernels for 14% -> 8%
where the time goes in v1:
time: 80.5 us; the launch traced here: 80 us
  starting transfers between devices  34.3 us (43%)
  blocking collectives  19.3 us (24%)
  waiting for transfers between devices  13.8 us (17%)
  Pallas kernels  8.33 us (10%)
  local copies, waits for them, and re-layouts  3.85 us (5%)
    all_to_all x1, starting transfers between devices, local(): arrived = lax.all_to_all(outgoing, 'gx', 0, 0, tiled=True)  17.9 us
    all_to_all x1, blocking collectives, local(): owned = lax.all_to_all(partial_modes, 'gy', 0, 0, tiled=True)  11.5 us
    all_to_all x1, waiting for transfers between devices, local(): arrived = lax.all_to_all(outgoing, 'gx', 0, 0, tiled=True)  10.9 us
    all_to_all x1, blocking collectives, local(): shared = lax.all_to_all(mixed, 'gy', 0, 0, tiled=True)  7.82 us
    ppermute x1, starting transfers between devices, local(): lax.ppermute(features, 'gx', [(i, i + 1) for i in range(count_x - 1)])  5.49 us
    all_to_all x1, starting transfers between devices, local(): whole = lax.all_to_all(returning, 'gx', 0, 0, tiled=True)  4.62 us
    unnamed x26, local copies, waits for them, and re-layouts  3.29 us
    ppermute x1, starting transfers between devices, local(): before = lax.ppermute(tails, 'gy', [(i, i + 1) for i in range(count_y - 1)])  2.95 us
  transfers between devices with their start and end apart: 6, of which 2 were waited for; matrix products, arithmetic and copies ran while one was open for 1% of the time, Pallas kernels for 8%

profile of v1, /device:TPU:1, one launch (start us, length us, event | category | flops | bytes accessed | tf_op | source)
XLA Modules:
  0.0 80.0 jit_solution(10155138867614838276)
XLA Ops:
  0.0 1.4 %collective-permute-start.1 = (f32[32,1,32,128]{3,2,1,0:T(8,128)}, f32[32,1,32,128]{3,2,1,0:T(8,128)S(1)}, u32[]{:S(2)}, u32[]{:S(2)}) collective-permute-start(f32[32,1,32,128]{3,2,1,0:T(8,128)} %param.12), channel_id=1, source_target_pairs={{8,0},{16,8},{24,16},{32,24},{40,32},{48,40},{56,48},{64,56},{72,6... | collective-permute-start | bytes 1572872 | tf_op jit(solution)/shard_map/ppermute | solution.py:396
  1.4 5.5 %collective-permute-start = (f32[32,1,32,128]{3,2,1,0:T(8,128)}, f32[32,1,32,128]{3,2,1,0:T(8,128)S(1)}, u32[]{:S(2)}, u32[]{:S(2)}) collective-permute-start(f32[32,1,32,128]{3,2,1,0:T(8,128)} %param.12), channel_id=1, source_target_pairs={{0,8},{8,16},{16,24},{24,32},{32,40},{40,48},{48,56},{56,64},{64,7... | collective-permute-start | bytes 1572872 | tf_op jit(solution)/shard_map/ppermute | solution.py:395
  7.0 1.0 %copy-done = f32[32,1,32,128]{3,2,1,0:T(8,128)S(1)} copy-done((f32[32,1,32,128]{3,2,1,0:T(8,128)S(1)}, f32[32,1,32,128]{3,2,1,0:T(8,128)}, u32[]{:S(2)}) %copy-start) | copy-done | bytes 524312
  8.0 0.9 %copy-done.4 = bf16[256,256]{1,0:T(8,128)(2,1)S(1)} copy-done((bf16[256,256]{1,0:T(8,128)(2,1)S(1)}, bf16[256,256]{1,0:T(8,128)(2,1)}, u32[]{:S(2)}) %copy-start.4) | copy-done | bytes 131096
  8.9 0.9 %copy-done.5 = bf16[256,256]{1,0:T(8,128)(2,1)S(1)} copy-done((bf16[256,256]{1,0:T(8,128)(2,1)S(1)}, bf16[256,256]{1,0:T(8,128)(2,1)}, u32[]{:S(2)}) %copy-start.5) | copy-done | bytes 131096
  9.8 2.2 %forward.1 = f32[128,128]{1,0:T(8,128)} custom-call(f32[1024,128]{1,0:T(8,128)S(1)} %bitcast.15, bf16[256,256]{1,0:T(8,128)(2,1)S(1)} %copy-done.4, bf16[256,256]{1,0:T(8,128)(2,1)S(1)} %copy-done.5, bf16[32,256]{1,0:T(8,128)(2,1)S(1)} %copy-done.9, bf16[32,256]{1,0:T(8,128)(2,1)S(1)} %copy-done.10), custom_call_target="tpu_custom_call" | custom-call | tf_op jit(solution)/shard_map/forward/pallas_call | solution.py:365
  12.1 17.9 %all-to-all-start = ((f32[64,2,128]{2,1,0:T(2,128)}), f32[64,2,128]{2,1,0:T(2,128)S(1)}, u32[]{:S(2)}, u32[]{:S(2)}) async-start(f32[64,2,128]{2,1,0:T(2,128)} %bitcast.1), calls=%async_computation | async-start | bytes 131072 | tf_op jit(solution)/shard_map/all_to_all | solution.py:428
  30.0 0.1 fusion.4
  30.2 10.9 %all-to-all-done = f32[64,2,128]{2,1,0:T(2,128)S(1)} async-done(((f32[64,2,128]{2,1,0:T(2,128)}), f32[64,2,128]{2,1,0:T(2,128)S(1)}, u32[]{:S(2)}, u32[]{:S(2)}) %all-to-all-start) | async-done | bytes 65568 | tf_op jit(solution)/shard_map/all_to_all | solution.py:428
  41.1 0.3 gather.1
  41.4 11.5 %all_to_all.44 = f32[8,8,128]{2,1,0:T(8,128)S(1)} all-to-all(f32[8,8,128]{2,1,0:T(8,128)S(1)} %bitcast.25), channel_id=1, replica_groups=mesh['gx'=64,'gy'=8] {'gy'}, dimensions={0} | all-to-all | bytes 65536 | tf_op jit(solution)/shard_map/all_to_all | solution.py:433
  52.9 0.4 middle.1
  53.3 7.8 %all_to_all.45 = f32[8,8,128]{2,1,0:T(8,128)S(1)} all-to-all(f32[8,8,128]{2,1,0:T(8,128)S(1)} %bitcast.27), channel_id=1, replica_groups=mesh['gx'=64,'gy'=8] {'gy'}, dimensions={0} | all-to-all | bytes 65536 | tf_op jit(solution)/shard_map/all_to_all | solution.py:438
  61.1 1.0 %spread.1 = f32[128,128]{1,0:T(8,128)} custom-call(f32[64,128]{1,0:T(8,128)S(1)} %bitcast.24, f32[32,64]{1,0:T(8,128)S(1)} %pad_maximum_fusion.refs_1_), custom_call_target="tpu_custom_call" | custom-call | tf_op jit(solution)/shard_map/spread/pallas_call | solution.py:421
  62.1 4.6 %all-to-all-start.3 = ((f32[64,2,128]{2,1,0:T(2,128)}), f32[64,2,128]{2,1,0:T(2,128)S(1)}, u32[]{:S(2)}, u32[]{:S(2)}) async-start(f32[64,2,128]{2,1,0:T(2,128)} %bitcast.7), calls=%async_computation.3 | async-start | bytes 131072 | tf_op jit(solution)/shard_map/all_to_all | solution.py:443
  66.8 2.9 %collective-permute-start.2 = (f32[96,128]{1,0:T(8,128)S(1)}, f32[96,128]{1,0:T(8,128)S(1)}, u32[]{:S(2)}, u32[]{:S(2)}) collective-permute-start(f32[96,128]{1,0:T(8,128)S(1)} %get-tuple-element.7), channel_id=1, source_target_pairs={{0,1},{1,2},{2,3},{3,4},{4,5},{5,6},{6,7},{8,9},{9,10},{10,11},{11... | collective-permute-start | bytes 147464 | tf_op jit(solution)/shard_map/ppermute | solution.py:406
  69.8 1.9 %collective-permute-start.3 = (f32[96,128]{1,0:T(8,128)S(1)}, f32[96,128]{1,0:T(8,128)S(1)}, u32[]{:S(2)}, u32[]{:S(2)}) collective-permute-start(f32[96,128]{1,0:T(8,128)S(1)} %get-tuple-element.8), channel_id=1, source_target_pairs={{1,0},{2,1},{3,2},{4,3},{5,4},{6,5},{7,6},{9,8},{10,9},{11,10},{12... | collective-permute-start | bytes 147464 | tf_op jit(solution)/shard_map/ppermute | solution.py:407
  71.7 0.3 copy.15
  72.0 0.2 reshape.35.refs_3_.refs_8_
  72.3 0.4 copy-done.12
  72.7 0.1 broadcast_in_dim.2.refs_4_
  72.7 2.3 %conv.1.refs_5_ = f32[1024,128]{1,0:T(8,128)S(1)} custom-call(f32[1024,128]{1,0:T(8,128)S(1)} %bitcast.21, f32[1024,128]{1,0:T(8,128)S(1)} %bitcast.17, f32[1024,128]{1,0:T(8,128)S(1)} %bitcast.19, f32[288,96]{1,0:T(8,128)S(1)} %reshape.35.refs_3_.refs_8_, f32[32,128]{1,0:T(8,128)S(1)} %broadcast_in_dim.2.refs_4_), custom_call_target="tpu_custom_call" | custom-call | tf_op jit(solution)/shard_map/conv/pallas_call | solution.py:385
  75.1 2.8 %all-to-all-done.3 = f32[64,2,128]{2,1,0:T(2,128)S(1)} async-done(((f32[64,2,128]{2,1,0:T(2,128)}), f32[64,2,128]{2,1,0:T(2,128)S(1)}, u32[]{:S(2)}, u32[]{:S(2)}) %all-to-all-start.3) | async-done | bytes 65568 | tf_op jit(solution)/shard_map/all_to_all | solution.py:443
  77.9 2.0 %inverse.1 = f32[1024,128]{1,0:T(8,128)} custom-call(f32[128,128]{1,0:T(8,128)S(1)} %bitcast.22, bf16[256,256]{1,0:T(8,128)(2,1)S(1)} %copy-done.2, bf16[256,256]{1,0:T(8,128)(2,1)S(1)} %copy-done.3, bf16[32,256]{1,0:T(8,128)(2,1)S(1)} %copy-done.7, bf16[32,256]{1,0:T(8,128)(2,1)S(1)} %copy-done.8, f32[1024,128]{1,0:T(8,128)S(1)} %conv.1.refs_5_, ...), custom_call_target="tpu_custom_call" | custom-call | tf_op jit(solution)/shard_map/inverse/pallas_call | solution.py:446
  (29 shorter events, 0.1 us)
Async XLA Ops:
  0.0 6.9 %copy-start.9 = (bf16[32,256]{1,0:T(8,128)(2,1)S(1)}, bf16[32,256]{1,0:T(8,128)(2,1)}, u32[]{:S(2)}) copy-start(bf16[32,256]{1,0:T(8,128)(2,1)} %constant.80.clone.deep_high_hbm) | copy-start | bytes 49156
  0.0 6.9 %copy-start.10 = (bf16[32,256]{1,0:T(8,128)(2,1)S(1)}, bf16[32,256]{1,0:T(8,128)(2,1)}, u32[]{:S(2)}) copy-start(bf16[32,256]{1,0:T(8,128)(2,1)} %constant.81.clone.deep_low_hbm) | copy-start | bytes 49156
  0.0 66.7 %collective-permute-start.1 = (f32[32,1,32,128]{3,2,1,0:T(8,128)}, f32[32,1,32,128]{3,2,1,0:T(8,128)S(1)}, u32[]{:S(2)}, u32[]{:S(2)}) collective-permute-start(f32[32,1,32,128]{3,2,1,0:T(8,128)} %param.12), channel_id=1, source_target_pairs={{8,0},{16,8},{24,16},{32,24},{40,32},{48,40},{56,48},{64,56},{72,6... | collective-permute-start | bytes 1572872 | tf_op jit(solution)/shard_map/ppermute | solution.py:396
  1.4 65.3 %collective-permute-start = (f32[32,1,32,128]{3,2,1,0:T(8,128)}, f32[32,1,32,128]{3,2,1,0:T(8,128)S(1)}, u32[]{:S(2)}, u32[]{:S(2)}) collective-permute-start(f32[32,1,32,128]{3,2,1,0:T(8,128)} %param.12), channel_id=1, source_target_pairs={{0,8},{8,16},{16,24},{24,32},{32,40},{40,48},{48,56},{56,64},{64,7... | collective-permute-start | bytes 1572872 | tf_op jit(solution)/shard_map/ppermute | solution.py:395
  6.9 1.0 %copy-start = (f32[32,1,32,128]{3,2,1,0:T(8,128)S(1)}, f32[32,1,32,128]{3,2,1,0:T(8,128)}, u32[]{:S(2)}) copy-start(f32[32,1,32,128]{3,2,1,0:T(8,128)} %param.12) | copy-start | bytes 1572868
  8.0 0.9 %copy-start.4 = (bf16[256,256]{1,0:T(8,128)(2,1)S(1)}, bf16[256,256]{1,0:T(8,128)(2,1)}, u32[]{:S(2)}) copy-start(bf16[256,256]{1,0:T(8,128)(2,1)} %constant.78.clone.wide_high_hbm) | copy-start | bytes 393220
  8.9 0.9 %copy-start.5 = (bf16[256,256]{1,0:T(8,128)(2,1)S(1)}, bf16[256,256]{1,0:T(8,128)(2,1)}, u32[]{:S(2)}) copy-start(bf16[256,256]{1,0:T(8,128)(2,1)} %constant.79.clone.wide_low_hbm) | copy-start | bytes 393220
  9.8 43.1 %copy-start.6 = (f32[8,2048]{1,0:T(8,128)S(1)}, f32[8,2048]{1,0:T(8,128)}, u32[]{:S(2)}) copy-start(f32[8,2048]{1,0:T(8,128)} %refs_1_.2) | copy-start | bytes 196612
  12.1 54.7 %copy-start.1 = (f32[32,1,32,128]{3,2,1,0:T(8,128)S(1)}, f32[32,1,32,128]{3,2,1,0:T(8,128)}, u32[]{:S(2)}) copy-start(f32[32,1,32,128]{3,2,1,0:T(8,128)} %param.12) | copy-start | bytes 1572868
  12.1 29.0 %all-to-all-start = ((f32[64,2,128]{2,1,0:T(2,128)}), f32[64,2,128]{2,1,0:T(2,128)S(1)}, u32[]{:S(2)}, u32[]{:S(2)}) async-start(f32[64,2,128]{2,1,0:T(2,128)} %bitcast.1), calls=%async_computation | async-start | bytes 131072 | tf_op jit(solution)/shard_map/all_to_all | solution.py:428
  62.1 15.8 %all-to-all-start.3 = ((f32[64,2,128]{2,1,0:T(2,128)}), f32[64,2,128]{2,1,0:T(2,128)S(1)}, u32[]{:S(2)}, u32[]{:S(2)}) async-start(f32[64,2,128]{2,1,0:T(2,128)} %bitcast.7), calls=%async_computation.3 | async-start | bytes 131072 | tf_op jit(solution)/shard_map/all_to_all | solution.py:443
  66.8 5.0 %copy-start.11 = (f32[3,3,3,32,32]{4,3,2,1,0:T(8,128)S(1)}, f32[3,3,3,32,32]{4,3,2,1,0:T(8,128)}, u32[]{:S(2)}) copy-start(f32[3,3,3,32,32]{4,3,2,1,0:T(8,128)} %param.13) | copy-start | bytes 331780
  66.8 11.1 %collective-permute-start.2 = (f32[96,128]{1,0:T(8,128)S(1)}, f32[96,128]{1,0:T(8,128)S(1)}, u32[]{:S(2)}, u32[]{:S(2)}) collective-permute-start(f32[96,128]{1,0:T(8,128)S(1)} %get-tuple-element.7), channel_id=1, source_target_pairs={{0,1},{1,2},{2,3},{3,4},{4,5},{5,6},{6,7},{8,9},{9,10},{10,11},{11... | collective-permute-start | bytes 147464 | tf_op jit(solution)/shard_map/ppermute | solution.py:406
  69.8 8.1 %collective-permute-start.3 = (f32[96,128]{1,0:T(8,128)S(1)}, f32[96,128]{1,0:T(8,128)S(1)}, u32[]{:S(2)}, u32[]{:S(2)}) collective-permute-start(f32[96,128]{1,0:T(8,128)S(1)} %get-tuple-element.8), channel_id=1, source_target_pairs={{1,0},{2,1},{3,2},{4,3},{5,4},{6,5},{7,6},{9,8},{10,9},{11,10},{12... | collective-permute-start | bytes 147464 | tf_op jit(solution)/shard_map/ppermute | solution.py:407
  72.0 0.7 copy-start.12
  72.7 5.2 %copy-start.2 = (bf16[256,256]{1,0:T(8,128)(2,1)S(1)}, bf16[256,256]{1,0:T(8,128)(2,1)}, u32[]{:S(2)}) copy-start(bf16[256,256]{1,0:T(8,128)(2,1)} %constant.82.clone.refs_1_) | copy-start | bytes 393220
  72.7 5.2 %copy-start.3 = (bf16[256,256]{1,0:T(8,128)(2,1)S(1)}, bf16[256,256]{1,0:T(8,128)(2,1)}, u32[]{:S(2)}) copy-start(bf16[256,256]{1,0:T(8,128)(2,1)} %constant.83.clone.refs_2_) | copy-start | bytes 393220
  72.7 5.2 %copy-start.7 = (bf16[32,256]{1,0:T(8,128)(2,1)S(1)}, bf16[32,256]{1,0:T(8,128)(2,1)}, u32[]{:S(2)}) copy-start(bf16[32,256]{1,0:T(8,128)(2,1)} %constant.84.clone.refs_3_) | copy-start | bytes 49156
  72.7 5.2 %copy-start.8 = (bf16[32,256]{1,0:T(8,128)(2,1)S(1)}, bf16[32,256]{1,0:T(8,128)(2,1)}, u32[]{:S(2)}) copy-start(bf16[32,256]{1,0:T(8,128)(2,1)} %constant.85.clone.refs_4_) | copy-start | bytes 49156

commit v2 on v1

--- a/solution.py
+++ b/solution.py
@@ -377,7 +377,10 @@
         ],
         compiler_params=params,
         name="forward",
-    )(cells, *fixed_halves(wide), *fixed_halves(deep))
+    )(*[
+        pltpu.with_memory_space_constraint(value, pltpu.HBM)
+        for value in (cells, *fixed_halves(wide), *fixed_halves(deep))
+    ])
     taps = jnp.transpose(conv_weight, (1, 2, 4, 0, 3)).reshape(9 * channels, 3 * channels)
     bias = jnp.broadcast_to(conv_bias[:, None], (channels, depth))
 
@@ -392,8 +395,28 @@
             name=name,
         )(*operands)
 
-    left = lax.ppermute(features, "gx", [(i, i + 1) for i in range(count_x - 1)])
-    right = lax.ppermute(features, "gx", [(i + 1, i) for i in range(count_x - 1)])
+    long_modes = jnp.arange(KX, dtype=jnp.int32)
+    long_modes = jnp.where(long_modes < KX // 2, long_modes, length_x - KX + long_modes)
+    wide_mode = lax.axis_index("gx") * pairs // count_x // KZ
+    wide_mode = jnp.where(wide_mode < KY // 2, wide_mode, length_y - KY + wide_mode)
+    places = jnp.arange(length_x, dtype=jnp.int32)
+    steps = length_y // length_x * (long_modes[:, None] * places[None, :])
+    steps = (steps + wide_mode * rows_y * lax.axis_index("gy")) % length_y
+    angle = 2.0 * math.pi / length_y * steps.astype(f32)
+    basis = jnp.concatenate([jnp.cos(angle), jnp.sin(angle)], axis=0)
+
+    def small(kernel, name, rows, *operands):
+        return pl.pallas_call(
+            kernel,
+            out_shape=jax.ShapeDtypeStruct((rows, LANES), f32),
+            compiler_params=params,
+            name=name,
+        )(*operands)
+
+    arrived = lax.all_to_all(outgoing, "gx", 0, 0, tiled=True)
+    later, arrived = lax.optimization_barrier((features, arrived))
+    left = lax.ppermute(later, "gx", [(i, i + 1) for i in range(count_x - 1)])
+    right = lax.ppermute(later, "gx", [(i + 1, i) for i in range(count_x - 1)])
     left = left.reshape(cells.shape)
     right = right.reshape(cells.shape)
     edge = jax.ShapeDtypeStruct((3 * channels, depth), f32)
@@ -407,25 +430,6 @@
     after = lax.ppermute(heads, "gy", [(i + 1, i) for i in range(count_y - 1)])
     local_term = conv("conv", (0, 1, 2), left, cells, right, taps, bias)
 
-    long_modes = jnp.arange(KX, dtype=jnp.int32)
-    long_modes = jnp.where(long_modes < KX // 2, long_modes, length_x - KX + long_modes)
-    wide_mode = lax.axis_index("gx") * pairs // count_x // KZ
-    wide_mode = jnp.where(wide_mode < KY // 2, wide_mode, length_y - KY + wide_mode)
-    places = jnp.arange(length_x, dtype=jnp.int32)
-    steps = length_y // length_x * (long_modes[:, None] * places[None, :])
-    steps = (steps + wide_mode * rows_y * lax.axis_index("gy")) % length_y
-    angle = 2.0 * math.pi / length_y * steps.astype(f32)
-    basis = jnp.concatenate([jnp.cos(angle), jnp.sin(angle)], axis=0)
-
-    def small(kernel, name, rows, *operands):
-        return pl.pallas_call(
-            kernel,
-            out_shape=jax.ShapeDtypeStruct((rows, LANES), f32),
-            compiler_params=params,
-            name=name,
-        )(*operands)
-
-    arrived = lax.all_to_all(outgoing, "gx", 0, 0, tiled=True)
     partial_modes = small(
         lambda *refs: gather_kernel(*refs, channels=channels, share=share),
         "gather", count_y * share, arrived, basis,

time: 80.5 us -> 76.6 us (0.952)
  blocking collectives: 19.3 us -> 47.3 us
  starting transfers between devices: 34.3 us -> 16.5 us
  waiting for transfers between devices: 13.8 us -> 2.54 us
  local copies, waits for them, and re-layouts: 3.85 us -> 1 us
    all_to_all x0 -> x1, blocking collectives: none -> 28.1 us  [local(): arrived = lax.all_to_all(outgoing, 'gx', 0, 0, tiled=True)]
    all_to_all x1 -> x0, starting transfers between devices: 17.9 us -> none  [local(): arrived = lax.all_to_all(outgoing, 'gx', 0, 0, tiled=True)]
    all_to_all x1 -> x0, waiting for transfers between devices: 10.9 us -> none  [local(): arrived = lax.all_to_all(outgoing, 'gx', 0, 0, tiled=True)]
    unnamed x26 -> x16, local copies, waits for them, and re-layouts: 3.29 us -> 0.44 us
    ppermute x2, starting transfers between devices: 6.9 us -> 5.3 us  [the longest x1 4.02 us: local(): left = lax.ppermute(later, 'gx', [(i, i + 1) for i in range(count_x - 1)])]
    all_to_all x1, starting transfers between devices: 4.62 us -> 6.04 us  [local(): whole = lax.all_to_all(returning, 'gx', 0, 0, tiled=True)]
  transfers between devices with their start and end apart: 6 -> 5, of which waited for: 2 -> 1; matrix products, arithmetic and copies ran while one was open for 1% -> 1% of each run, Pallas kernels for 8% -> 5%
where the time goes in v2:
time: 76.6 us; the launch traced here: 76.2 us
  blocking collectives  47.3 us (62%)
  starting transfers between devices  16.5 us (22%)
  Pallas kernels  8.43 us (11%)
  waiting for transfers between devices  2.54 us (3%)
  local copies, waits for them, and re-layouts  1 us (1%)
    all_to_all x1, blocking collectives, local(): arrived = lax.all_to_all(outgoing, 'gx', 0, 0, tiled=True)  28.1 us
    all_to_all x1, blocking collectives, local(): owned = lax.all_to_all(partial_modes, 'gy', 0, 0, tiled=True)  11.5 us
    all_to_all x1, blocking collectives, local(): shared = lax.all_to_all(mixed, 'gy', 0, 0, tiled=True)  7.82 us
    all_to_all x1, starting transfers between devices, local(): whole = lax.all_to_all(returning, 'gx', 0, 0, tiled=True)  6.04 us
    ppermute x1, starting transfers between devices, local(): left = lax.ppermute(later, 'gx', [(i, i + 1) for i in range(count_x - 1)])  4.02 us
    ppermute x1, starting transfers between devices, local(): before = lax.ppermute(tails, 'gy', [(i, i + 1) for i in range(count_y - 1)])  3.23 us
    all_to_all x1, waiting for transfers between devices, local(): whole = lax.all_to_all(returning, 'gx', 0, 0, tiled=True)  2.53 us
    pallas_call x1, Pallas kernels, local(): pl.pallas_call(forward_kernel, out_shape=jax.ShapeDtypeStruct((pairs // 2...  2.35 us
  transfers between devices with their start and end apart: 5, of which 1 were waited for; matrix products, arithmetic and copies ran while one was open for 1% of the time, Pallas kernels for 5%

profile of v2, /device:TPU:1, one launch (start us, length us, event | category | flops | bytes accessed | tf_op | source)
XLA Modules:
  0.0 76.2 jit_solution(437636033399315074)
XLA Ops:
  0.0 2.4 %forward.1 = f32[128,128]{1,0:T(8,128)S(1)} custom-call(f32[1024,128]{1,0:T(8,128)} %bitcast.15, bf16[256,256]{1,0:T(8,128)(2,1)} %constant.78.clone.wide_high_hbm, bf16[256,256]{1,0:T(8,128)(2,1)} %constant.79.clone.wide_low_hbm, bf16[32,256]{1,0:T(8,128)(2,1)} %constant.80.clone.deep_high_hbm, bf16[32,256]{1,0:T(8,128)(2,1)} %constant.81.clone.deep_low_hbm), custom_call_target="tpu_custom_call" | custom-call | tf_op jit(solution)/shard_map/forward/pallas_call | solution.py:365
  2.4 28.1 %all_to_all.45 = f32[64,2,128]{2,1,0:T(2,128)S(1)} all-to-all(f32[64,2,128]{2,1,0:T(2,128)S(1)} %bitcast.23), channel_id=1, replica_groups=mesh['gx'=64,'gy'=8] {'gx'}, dimensions={0} | all-to-all | bytes 131072 | tf_op jit(solution)/shard_map/all_to_all | solution.py:416
  30.4 1.3 %collective-permute-start.1 = (f32[32,1,32,128]{3,2,1,0:T(8,128)S(1)}, f32[32,1,32,128]{3,2,1,0:T(8,128)S(1)}, u32[]{:S(2)}, u32[]{:S(2)}) collective-permute-start(f32[32,1,32,128]{3,2,1,0:T(8,128)S(1)} %copy-done), channel_id=1, source_target_pairs={{8,0},{16,8},{24,16},{32,24},{40,32},{48,40},{56,48},{64,56},{72,6... | collective-permute-start | bytes 1572872 | tf_op jit(solution)/shard_map/ppermute | solution.py:419
  31.7 4.0 %collective-permute-start = (f32[32,1,32,128]{3,2,1,0:T(8,128)S(1)}, f32[32,1,32,128]{3,2,1,0:T(8,128)S(1)}, u32[]{:S(2)}, u32[]{:S(2)}) collective-permute-start(f32[32,1,32,128]{3,2,1,0:T(8,128)S(1)} %copy-done), channel_id=1, source_target_pairs={{0,8},{8,16},{16,24},{24,32},{32,40},{40,48},{48,56},{56,64},{64,7... | collective-permute-start | bytes 1572872 | tf_op jit(solution)/shard_map/ppermute | solution.py:418
  35.8 0.1 fusion.4
  35.9 0.0 copy-start.3
  35.9 0.3 gather.1
  36.2 11.5 %all_to_all.46 = f32[8,8,128]{2,1,0:T(8,128)S(1)} all-to-all(f32[8,8,128]{2,1,0:T(8,128)S(1)} %bitcast.26), channel_id=1, replica_groups=mesh['gx'=64,'gy'=8] {'gy'}, dimensions={0} | all-to-all | bytes 65536 | tf_op jit(solution)/shard_map/all_to_all | solution.py:437
  47.7 0.4 middle.1
  48.1 7.8 %all_to_all.47 = f32[8,8,128]{2,1,0:T(8,128)S(1)} all-to-all(f32[8,8,128]{2,1,0:T(8,128)S(1)} %bitcast.28), channel_id=1, replica_groups=mesh['gx'=64,'gy'=8] {'gy'}, dimensions={0} | all-to-all | bytes 65536 | tf_op jit(solution)/shard_map/all_to_all | solution.py:442
  55.9 1.0 %spread.1 = f32[128,128]{1,0:T(8,128)} custom-call(f32[64,128]{1,0:T(8,128)S(1)} %bitcast.25, f32[32,64]{1,0:T(8,128)S(1)} %pad_maximum_fusion.refs_1_), custom_call_target="tpu_custom_call" | custom-call | tf_op jit(solution)/shard_map/spread/pallas_call | solution.py:409
  56.9 6.0 %all-to-all-start.3 = ((f32[64,2,128]{2,1,0:T(2,128)}), f32[64,2,128]{2,1,0:T(2,128)S(1)}, u32[]{:S(2)}, u32[]{:S(2)}) async-start(f32[64,2,128]{2,1,0:T(2,128)} %bitcast.7), calls=%async_computation.3 | async-start | bytes 131072 | tf_op jit(solution)/shard_map/all_to_all | solution.py:447
  63.0 0.0 copy-start.6
  63.0 0.1 edges.1
  63.1 3.2 %collective-permute-start.2 = (f32[96,128]{1,0:T(8,128)S(1)}, f32[96,128]{1,0:T(8,128)S(1)}, u32[]{:S(2)}, u32[]{:S(2)}) collective-permute-start(f32[96,128]{1,0:T(8,128)S(1)} %get-tuple-element.11), channel_id=1, source_target_pairs={{0,1},{1,2},{2,3},{3,4},{4,5},{5,6},{6,7},{8,9},{9,10},{10,11},{11... | collective-permute-start | bytes 147464 | tf_op jit(solution)/shard_map/ppermute | solution.py:429
  66.3 1.9 %collective-permute-start.3 = (f32[96,128]{1,0:T(8,128)S(1)}, f32[96,128]{1,0:T(8,128)S(1)}, u32[]{:S(2)}, u32[]{:S(2)}) collective-permute-start(f32[96,128]{1,0:T(8,128)S(1)} %get-tuple-element.12), channel_id=1, source_target_pairs={{1,0},{2,1},{3,2},{4,3},{5,4},{6,5},{7,6},{9,8},{10,9},{11,10},{12... | collective-permute-start | bytes 147464 | tf_op jit(solution)/shard_map/ppermute | solution.py:430
  68.2 0.3 copy.15
  68.5 0.0 copy-start.7
  68.5 0.2 reshape.35.refs_3_.refs_8_
  68.8 0.4 copy-done.7
  69.2 0.1 broadcast_in_dim.2.refs_4_
  69.2 2.3 %conv.1.refs_5_ = f32[1024,128]{1,0:T(8,128)S(1)} custom-call(f32[1024,128]{1,0:T(8,128)S(1)} %bitcast.21, f32[1024,128]{1,0:T(8,128)S(1)} %bitcast.17, f32[1024,128]{1,0:T(8,128)S(1)} %bitcast.19, f32[288,96]{1,0:T(8,128)S(1)} %reshape.35.refs_3_.refs_8_, f32[32,128]{1,0:T(8,128)S(1)} %broadcast_in_dim.2.refs_4_), custom_call_target="tpu_custom_call" | custom-call | tf_op jit(solution)/shard_map/conv/pallas_call | solution.py:388
  71.6 2.5 %all-to-all-done.3 = f32[64,2,128]{2,1,0:T(2,128)S(1)} async-done(((f32[64,2,128]{2,1,0:T(2,128)}), f32[64,2,128]{2,1,0:T(2,128)S(1)}, u32[]{:S(2)}, u32[]{:S(2)}) %all-to-all-start.3) | async-done | bytes 65568 | tf_op jit(solution)/shard_map/all_to_all | solution.py:447
  74.1 2.0 %inverse.1 = f32[1024,128]{1,0:T(8,128)} custom-call(f32[128,128]{1,0:T(8,128)S(1)} %bitcast.22, bf16[256,256]{1,0:T(8,128)(2,1)S(1)} %copy-done.1, bf16[256,256]{1,0:T(8,128)(2,1)S(1)} %copy-done.2, bf16[32,256]{1,0:T(8,128)(2,1)S(1)} %copy-done.4, bf16[32,256]{1,0:T(8,128)(2,1)S(1)} %copy-done.5, f32[1024,128]{1,0:T(8,128)S(1)} %conv.1.refs_5_, ...), custom_call_target="tpu_custom_call" | custom-call | tf_op jit(solution)/shard_map/inverse/pallas_call | solution.py:450
  (18 shorter events, 0.0 us)
Async XLA Ops:
  0.0 30.4 %copy-start = (f32[32,1,32,128]{3,2,1,0:T(8,128)S(1)}, f32[32,1,32,128]{3,2,1,0:T(8,128)}, u32[]{:S(2)}) copy-start(f32[32,1,32,128]{3,2,1,0:T(8,128)} %param.12) | copy-start | bytes 1572868
  30.4 32.6 %collective-permute-start.1 = (f32[32,1,32,128]{3,2,1,0:T(8,128)S(1)}, f32[32,1,32,128]{3,2,1,0:T(8,128)S(1)}, u32[]{:S(2)}, u32[]{:S(2)}) collective-permute-start(f32[32,1,32,128]{3,2,1,0:T(8,128)S(1)} %copy-done), channel_id=1, source_target_pairs={{8,0},{16,8},{24,16},{32,24},{40,32},{48,40},{56,48},{64,56},{72,6... | collective-permute-start | bytes 1572872 | tf_op jit(solution)/shard_map/ppermute | solution.py:419
  31.7 31.3 %collective-permute-start = (f32[32,1,32,128]{3,2,1,0:T(8,128)S(1)}, f32[32,1,32,128]{3,2,1,0:T(8,128)S(1)}, u32[]{:S(2)}, u32[]{:S(2)}) collective-permute-start(f32[32,1,32,128]{3,2,1,0:T(8,128)S(1)} %copy-done), channel_id=1, source_target_pairs={{0,8},{8,16},{16,24},{24,32},{32,40},{40,48},{48,56},{56,64},{64,7... | collective-permute-start | bytes 1572872 | tf_op jit(solution)/shard_map/ppermute | solution.py:418
  35.9 11.8 %copy-start.3 = (f32[8,2048]{1,0:T(8,128)S(1)}, f32[8,2048]{1,0:T(8,128)}, u32[]{:S(2)}) copy-start(f32[8,2048]{1,0:T(8,128)} %refs_1_.2) | copy-start | bytes 196612
  56.9 17.2 %all-to-all-start.3 = ((f32[64,2,128]{2,1,0:T(2,128)}), f32[64,2,128]{2,1,0:T(2,128)S(1)}, u32[]{:S(2)}, u32[]{:S(2)}) async-start(f32[64,2,128]{2,1,0:T(2,128)} %bitcast.7), calls=%async_computation.3 | async-start | bytes 131072 | tf_op jit(solution)/shard_map/all_to_all | solution.py:447
  63.0 5.2 %copy-start.6 = (f32[3,3,3,32,32]{4,3,2,1,0:T(8,128)S(1)}, f32[3,3,3,32,32]{4,3,2,1,0:T(8,128)}, u32[]{:S(2)}) copy-start(f32[3,3,3,32,32]{4,3,2,1,0:T(8,128)} %param.13) | copy-start | bytes 331780
  63.1 11.0 %collective-permute-start.2 = (f32[96,128]{1,0:T(8,128)S(1)}, f32[96,128]{1,0:T(8,128)S(1)}, u32[]{:S(2)}, u32[]{:S(2)}) collective-permute-start(f32[96,128]{1,0:T(8,128)S(1)} %get-tuple-element.11), channel_id=1, source_target_pairs={{0,1},{1,2},{2,3},{3,4},{4,5},{5,6},{6,7},{8,9},{9,10},{10,11},{11... | collective-permute-start | bytes 147464 | tf_op jit(solution)/shard_map/ppermute | solution.py:429
  66.3 7.8 %collective-permute-start.3 = (f32[96,128]{1,0:T(8,128)S(1)}, f32[96,128]{1,0:T(8,128)S(1)}, u32[]{:S(2)}, u32[]{:S(2)}) collective-permute-start(f32[96,128]{1,0:T(8,128)S(1)} %get-tuple-element.12), channel_id=1, source_target_pairs={{1,0},{2,1},{3,2},{4,3},{5,4},{6,5},{7,6},{9,8},{10,9},{11,10},{12... | collective-permute-start | bytes 147464 | tf_op jit(solution)/shard_map/ppermute | solution.py:430
  68.5 0.7 copy-start.7
  69.2 4.9 %copy-start.1 = (bf16[256,256]{1,0:T(8,128)(2,1)S(1)}, bf16[256,256]{1,0:T(8,128)(2,1)}, u32[]{:S(2)}) copy-start(bf16[256,256]{1,0:T(8,128)(2,1)} %constant.82.clone.refs_1_) | copy-start | bytes 393220
  69.2 4.9 %copy-start.2 = (bf16[256,256]{1,0:T(8,128)(2,1)S(1)}, bf16[256,256]{1,0:T(8,128)(2,1)}, u32[]{:S(2)}) copy-start(bf16[256,256]{1,0:T(8,128)(2,1)} %constant.83.clone.refs_2_) | copy-start | bytes 393220
  69.2 4.9 %copy-start.4 = (bf16[32,256]{1,0:T(8,128)(2,1)S(1)}, bf16[32,256]{1,0:T(8,128)(2,1)}, u32[]{:S(2)}) copy-start(bf16[32,256]{1,0:T(8,128)(2,1)} %constant.84.clone.refs_3_) | copy-start | bytes 49156
  69.2 4.9 %copy-start.5 = (bf16[32,256]{1,0:T(8,128)(2,1)S(1)}, bf16[32,256]{1,0:T(8,128)(2,1)}, u32[]{:S(2)}) copy-start(bf16[32,256]{1,0:T(8,128)(2,1)} %constant.85.clone.refs_4_) | copy-start | bytes 49156

commit v3 on v2

--- a/solution.py
+++ b/solution.py
@@ -12,6 +12,7 @@
 KY = 16
 KZ = 16
 GROUP = 8
+CLASSES = 4
 LANES = 128
 
 f32 = jnp.float32
@@ -47,8 +48,8 @@
     return np.where(series < number // 2, series, series - number)
 
 
-def deep_angles(depth):
-    order = np.concatenate([np.arange(0, KZ, 2), np.arange(1, KZ, 2)])
+def deep_angles(depth, step):
+    order = np.concatenate([np.arange(start, KZ, step) for start in range(step)])
     return order, 2.0 * np.pi / depth * np.outer(order, np.arange(depth))
 
 
@@ -57,7 +58,7 @@
     same = np.eye(GROUP)
     wide = np.einsum("rby,ij->rbijy", np.stack([np.cos(angle), -np.sin(angle)]), same)
     wide = wide.reshape(2 * KY * GROUP, GROUP * rows_y)
-    _, angle = deep_angles(depth)
+    _, angle = deep_angles(depth, CLASSES)
     deep_cos = np.cos(angle)
     deep_sin = np.sin(angle)
     deep = np.concatenate(
@@ -75,7 +76,7 @@
     same = np.eye(GROUP)
     wide = np.einsum("ryb,ij->iyrbj", np.stack([np.cos(angle), -np.sin(angle)]), same)
     wide = wide.reshape(GROUP * rows_y, 2 * KY * GROUP)
-    order, angle = deep_angles(depth)
+    order, angle = deep_angles(depth, 2)
     factor = norm_factor * np.where(order == 0, 1.0, 2.0)[:, None]
     deep_cos = factor * np.cos(angle)
     deep_sin = factor * np.sin(angle)
@@ -89,9 +90,28 @@
     return wide, deep
 
 
+def long_tables(length_x, count_y, share):
+    modes = signed_modes(KX)
+    angle = 2.0 * np.pi / length_x * np.outer(modes, np.arange(length_x))
+    halves = [
+        np.concatenate([np.cos(angle[i : i + share]), np.sin(angle[i : i + share])])
+        for i in range(0, KX, share)
+    ]
+    turned = [angle + 2.0 * np.pi / count_y * turn for turn in range(count_y)]
+    whole = [np.concatenate([np.cos(each), np.sin(each)]) for each in turned]
+    return jnp.asarray(np.concatenate(halves), f32), jnp.asarray(np.concatenate(whole), f32)
+
+
+def turn_tables(count_y, rows):
+    wide = 2 * (np.arange(rows) // (KZ // CLASSES))[:, None] + np.arange(LANES) // (LANES // 2)
+    angle = 2.0 * np.pi / count_y * (np.arange(count_y)[:, None, None] * wide % count_y)
+    angle = angle.reshape(count_y * rows, LANES)
+    return jnp.asarray(np.cos(angle), f32), jnp.asarray(np.sin(angle), f32)
+
+
 def forward_kernel(
     cells_hbm, wide_high_hbm, wide_low_hbm, deep_high_hbm, deep_low_hbm, out_ref,
-    cells_ref, wide_high, wide_low, deep_high, deep_low, middle_ref, sems
+    cells_ref, wide_high, wide_low, deep_high, deep_low, middle_ref, pair_ref, sems
 ):
     half = cells_ref.shape[0] // 2
     chunks = [pl.ds(0, half), pl.ds(half, half)]
@@ -136,14 +156,22 @@
     modes = product_of_halves(
         (deep_high[...], deep_low[...]), halves_of(middle_ref[...]), ((1,), (1,))
     )
+    size = KZ // CLASSES
+    rows = KY // 2 * size
     for mode in range(KY):
         for part in range(2):
-            for odd in range(2):
-                lane = odd * 2 * channels + part * channels
-                row = (part * 2 + odd) * (KZ // 2)
-                out_ref[mode * KZ // 2 : (mode + 1) * KZ // 2, lane : lane + channels] = modes[
-                    row : row + KZ // 2, mode * channels : (mode + 1) * channels
+            for kind in range(CLASSES):
+                lane = mode % 2 * 2 * channels + part * channels
+                row = kind * rows + mode // 2 * size
+                source = part * KZ + kind * size
+                pair_ref[row : row + size, lane : lane + channels] = modes[
+                    source : source + size, mode * channels : (mode + 1) * channels
                 ]
+    copies_of = out_ref.shape[0] // (CLASSES * rows)
+    for kind in range(CLASSES):
+        for each in range(copies_of):
+            start = (kind * copies_of + each) * rows
+            out_ref[start : start + rows, :] = pair_ref[kind * rows : (kind + 1) * rows, :]
 
 
 def crossed(value, channels, sign):
@@ -156,22 +184,27 @@
     )
 
 
-def gather_kernel(rows_ref, basis_ref, out_ref, *, channels, share):
-    length = basis_ref.shape[1]
-    cells = jnp.concatenate(
-        [rows_ref[pl.ds(0, length, stride=2), :], rows_ref[pl.ds(1, length, stride=2), :]], axis=1
-    )
-    sums = jnp.dot(basis_ref[...], cells, precision=highest, preferred_element_type=f32)
-    for tile in range(2):
-        lanes = slice(tile * LANES, (tile + 1) * LANES)
-        modes = sums[:KX, lanes] + crossed(sums[KX:, lanes], channels, 1.0)
-        start = 2 * tile * KX
-        out_ref[start : start + KX, :] = modes
-        out_ref[start + KX : start + 2 * KX, :] = pltpu.roll(modes, LANES // 2, axis=1)
-
-
-def spread_kernel(rows_ref, basis_ref, out_ref, *, channels):
-    length = basis_ref.shape[1]
+def fold_kernel(rows_ref, cos_ref, sin_ref, out_ref, *, channels):
+    rows = out_ref.shape[0] // 2
+    total = jnp.zeros((rows, LANES), f32)
+    for start in range(0, rows_ref.shape[0], rows):
+        place = slice(start, start + rows)
+        value = rows_ref[place, :]
+        total = total + value * cos_ref[place, :] + crossed(value, channels, 1.0) * sin_ref[place, :]
+    other = pltpu.roll(total, LANES // 2, axis=1)
+    size = KZ // CLASSES
+    for tile in range(rows // size):
+        start = tile * size
+        out_ref[2 * start : 2 * start + size, :] = total[start : start + size, :]
+        out_ref[2 * start + size : 2 * start + 2 * size, :] = other[start : start + size, :]
+
+
+def spread_kernel(rows_ref, table_ref, out_ref, *, channels, rows_x):
+    length = table_ref.shape[1]
+    turns = table_ref.shape[0] // (2 * KX)
+    wide_mode = lax.axis_index("gx") // rows_x
+    turn = lax.rem(wide_mode * lax.axis_index("gy"), turns)
+    basis = table_ref[pl.ds(pl.multiple_of(turn * 2 * KX, 2 * KX), 2 * KX), :]
     for tile in range(2):
         start = 2 * tile * KX
         even = rows_ref[start : start + KX, :]
@@ -180,7 +213,7 @@
         modes = jnp.where(lane < LANES // 2, even, odd)
         both = jnp.concatenate([modes, crossed(modes, channels, -1.0)], axis=0)
         out_ref[pl.ds(tile, length, stride=2), :] = lax.dot_general(
-            basis_ref[...],
+            basis,
             both,
             (((0,), (0,)), ((), ())),
             precision=highest,
@@ -188,12 +221,12 @@
         )
 
 
-def middle_kernel(rows_ref, weight_ref, out_ref, *, channels, norm_factor):
+def middle_kernel(rows_ref, table_ref, weight_ref, out_ref, *, channels, norm_factor):
     share = weight_ref.shape[0]
-    sums = rows_ref[:share, :]
-    for start in range(share, rows_ref.shape[0], share):
-        sums = sums + rows_ref[start : start + share, :]
-    sums = norm_factor * sums
+    half = lax.rem(lax.axis_index("gy"), KX // share)
+    basis = table_ref[pl.ds(pl.multiple_of(half * 2 * share, 2 * share), 2 * share), :]
+    sums = jnp.dot(basis, rows_ref[...], precision=highest, preferred_element_type=f32)
+    sums = norm_factor * (sums[:share] + crossed(sums[share:], channels, 1.0))
     hat_real = sums[:, :channels]
     hat_imag = sums[:, channels : 2 * channels]
     size = channels * channels
@@ -364,7 +397,7 @@
     wide, deep = forward_tables(rows_y, length_y, depth)
     outgoing = pl.pallas_call(
         forward_kernel,
-        out_shape=jax.ShapeDtypeStruct((pairs // 2, LANES), f32),
+        out_shape=jax.ShapeDtypeStruct((pairs // 2 // CLASSES * count_y, LANES), f32),
         in_specs=[pl.BlockSpec(memory_space=pltpu.HBM)] * 5,
         scratch_shapes=[
             pltpu.VMEM(cells.shape, f32),
@@ -373,6 +406,7 @@
             pltpu.VMEM(deep.shape, bf16),
             pltpu.VMEM(deep.shape, bf16),
             pltpu.VMEM((KY * channels, 2 * depth), f32),
+            pltpu.VMEM((pairs // 2, LANES), f32),
             pltpu.SemaphoreType.DMA((6,)),
         ],
         compiler_params=params,
@@ -395,16 +429,6 @@
             name=name,
         )(*operands)
 
-    long_modes = jnp.arange(KX, dtype=jnp.int32)
-    long_modes = jnp.where(long_modes < KX // 2, long_modes, length_x - KX + long_modes)
-    wide_mode = lax.axis_index("gx") * pairs // count_x // KZ
-    wide_mode = jnp.where(wide_mode < KY // 2, wide_mode, length_y - KY + wide_mode)
-    places = jnp.arange(length_x, dtype=jnp.int32)
-    steps = length_y // length_x * (long_modes[:, None] * places[None, :])
-    steps = (steps + wide_mode * rows_y * lax.axis_index("gy")) % length_y
-    angle = 2.0 * math.pi / length_y * steps.astype(f32)
-    basis = jnp.concatenate([jnp.cos(angle), jnp.sin(angle)], axis=0)
-
     def small(kernel, name, rows, *operands):
         return pl.pallas_call(
             kernel,
@@ -413,10 +437,8 @@
             name=name,
         )(*operands)
 
-    arrived = lax.all_to_all(outgoing, "gx", 0, 0, tiled=True)
-    later, arrived = lax.optimization_barrier((features, arrived))
-    left = lax.ppermute(later, "gx", [(i, i + 1) for i in range(count_x - 1)])
-    right = lax.ppermute(later, "gx", [(i + 1, i) for i in range(count_x - 1)])
+    left = lax.ppermute(features, "gx", [(i, i + 1) for i in range(count_x - 1)])
+    right = lax.ppermute(features, "gx", [(i + 1, i) for i in range(count_x - 1)])
     left = left.reshape(cells.shape)
     right = right.reshape(cells.shape)
     edge = jax.ShapeDtypeStruct((3 * channels, depth), f32)
@@ -430,19 +452,21 @@
     after = lax.ppermute(heads, "gy", [(i + 1, i) for i in range(count_y - 1)])
     local_term = conv("conv", (0, 1, 2), left, cells, right, taps, bias)
 
-    partial_modes = small(
-        lambda *refs: gather_kernel(*refs, channels=channels, share=share),
-        "gather", count_y * share, arrived, basis,
-    )
-    owned = lax.all_to_all(partial_modes, "gy", 0, 0, tiled=True)
+    half_table, whole_table = long_tables(length_x, count_y, share)
+    gathered = lax.all_to_all(outgoing, "gy", 0, 0, tiled=True)
+    folded = small(
+        lambda *refs: fold_kernel(*refs, channels=channels),
+        "fold", count_x, gathered, *turn_tables(count_y, count_x // 2),
+    )
+    arrived = lax.all_to_all(folded, "gx", 0, 0, tiled=True)
     mixed = small(
         lambda *refs: middle_kernel(*refs, channels=channels, norm_factor=norm_factor),
-        "middle", count_y * share, owned, spectral_weight,
+        "middle", count_y * share, arrived, half_table, spectral_weight,
     )
     shared = lax.all_to_all(mixed, "gy", 0, 0, tiled=True)
     returning = small(
-        lambda *refs: spread_kernel(*refs, channels=channels),
-        "spread", pairs // 2, shared, basis,
+        lambda *refs: spread_kernel(*refs, channels=channels, rows_x=count_x // KY),
+        "spread", pairs // 2, shared, whole_table,
     )
     whole = lax.all_to_all(returning, "gx", 0, 0, tiled=True)
 

time: 76.6 us -> 77 us (level)
  blocking collectives: 47.3 us -> 48.3 us
  starting transfers between devices: 16.5 us -> 15.6 us
    all_to_all x1, blocking collectives: 7.82 us -> 9.38 us  [local(): shared = lax.all_to_all(mixed, 'gy', 0, 0, tiled=True)]
    all_to_all x1, starting transfers between devices: 6.04 us -> 4.62 us  [local(): whole = lax.all_to_all(returning, 'gx', 0, 0, tiled=True)]
    ppermute x2, starting transfers between devices: 5.3 us -> 6.14 us  [the longest x1 4.85 us: local(): lax.ppermute(features, 'gx', [(i, i + 1) for i in range(count_x - 1)])]
  transfers between devices with their start and end apart: 5 -> 5, of which waited for: 1 -> 1; matrix products, arithmetic and copies ran while one was open for 1% -> 1% of each run, Pallas kernels for 5% -> 9%
where the time goes in v3:
time: 77 us; the launch traced here: 76.6 us
  blocking collectives  48.3 us (63%)
  starting transfers between devices  15.6 us (20%)
  Pallas kernels  8.61 us (11%)
  waiting for transfers between devices  2.85 us (4%)
  local copies, waits for them, and re-layouts  1.03 us (1%)
    all_to_all x1, blocking collectives, local(): arrived = lax.all_to_all(folded, 'gx', 0, 0, tiled=True)  27.8 us
    all_to_all x1, blocking collectives, local(): gathered = lax.all_to_all(outgoing, 'gy', 0, 0, tiled=True)  11.1 us
    all_to_all x1, blocking collectives, local(): shared = lax.all_to_all(mixed, 'gy', 0, 0, tiled=True)  9.38 us
    ppermute x1, starting transfers between devices, local(): lax.ppermute(features, 'gx', [(i, i + 1) for i in range(count_x - 1)])  4.85 us
    all_to_all x1, starting transfers between devices, local(): whole = lax.all_to_all(returning, 'gx', 0, 0, tiled=True)  4.62 us
    ppermute x1, starting transfers between devices, local(): before = lax.ppermute(tails, 'gy', [(i, i + 1) for i in range(count_y - 1)])  2.95 us
    all_to_all x1, waiting for transfers between devices, local(): whole = lax.all_to_all(returning, 'gx', 0, 0, tiled=True)  2.84 us
    pallas_call x1, Pallas kernels, local(): pl.pallas_call(forward_kernel, out_shape=jax.ShapeDtypeStruct((pairs // 2...  2.35 us
  transfers between devices with their start and end apart: 5, of which 1 were waited for; matrix products, arithmetic and copies ran while one was open for 1% of the time, Pallas kernels for 9%

profile of v3, /device:TPU:1, one launch (start us, length us, event | category | flops | bytes accessed | tf_op | source)
XLA Modules:
  0.0 76.6 jit_solution(6420758833855479283)
XLA Ops:
  0.0 4.8 %collective-permute-start = (f32[32,1,32,128]{3,2,1,0:T(8,128)}, f32[32,1,32,128]{3,2,1,0:T(8,128)S(1)}, u32[]{:S(2)}, u32[]{:S(2)}) collective-permute-start(f32[32,1,32,128]{3,2,1,0:T(8,128)} %param.16), channel_id=1, source_target_pairs={{0,8},{8,16},{16,24},{24,32},{32,40},{40,48},{48,56},{56,64},{64,7... | collective-permute-start | bytes 1572872 | tf_op jit(solution)/shard_map/ppermute | solution.py:440
  4.9 1.3 %collective-permute-start.1 = (f32[32,1,32,128]{3,2,1,0:T(8,128)}, f32[32,1,32,128]{3,2,1,0:T(8,128)S(1)}, u32[]{:S(2)}, u32[]{:S(2)}) collective-permute-start(f32[32,1,32,128]{3,2,1,0:T(8,128)} %param.16), channel_id=1, source_target_pairs={{8,0},{16,8},{24,16},{32,24},{40,32},{48,40},{56,48},{64,56},{72,6... | collective-permute-start | bytes 1572872 | tf_op jit(solution)/shard_map/ppermute | solution.py:441
  6.2 2.4 %forward.1 = f32[256,128]{1,0:T(8,128)S(1)} custom-call(f32[1024,128]{1,0:T(8,128)} %bitcast.17, bf16[256,256]{1,0:T(8,128)(2,1)} %constant.24.clone.wide_high_hbm, bf16[256,256]{1,0:T(8,128)(2,1)} %constant.25.clone.wide_low_hbm, bf16[32,256]{1,0:T(8,128)(2,1)} %constant.26.clone.deep_high_hbm, bf16[32,256]{1,0:T(8,128)(2,1)} %constant.27.clone.deep_low_hbm), custom_call_target="tpu_custom_call" | custom-call | tf_op jit(solution)/shard_map/forward/pallas_call | solution.py:398
  8.5 0.0 copy-start.4
  8.5 0.0 copy-start.5
  8.6 0.0 copy-start.9
  8.6 11.1 %all_to_all.44 = f32[8,32,128]{2,1,0:T(8,128)S(1)} all-to-all(f32[8,32,128]{2,1,0:T(8,128)S(1)} %bitcast.25), channel_id=1, replica_groups=mesh['gx'=64,'gy'=8] {'gy'}, dimensions={0} | all-to-all | bytes 262144 | tf_op jit(solution)/shard_map/all_to_all | solution.py:456
  19.7 0.2 fold.1
  19.9 27.8 %all_to_all.45 = f32[64,1,128]{2,1,0:T(1,128)S(1)} all-to-all(f32[64,1,128]{2,1,0:T(1,128)S(1)} %bitcast.30), channel_id=1, replica_groups=mesh['gx'=64,'gy'=8] {'gx'}, dimensions={0} | all-to-all | bytes 65536 | tf_op jit(solution)/shard_map/all_to_all | solution.py:461
  47.7 0.7 middle.1
  48.4 9.4 %all_to_all.46 = f32[8,8,128]{2,1,0:T(8,128)S(1)} all-to-all(f32[8,8,128]{2,1,0:T(8,128)S(1)} %bitcast.29), channel_id=1, replica_groups=mesh['gx'=64,'gy'=8] {'gy'}, dimensions={0} | all-to-all | bytes 65536 | tf_op jit(solution)/shard_map/all_to_all | solution.py:466
  57.8 1.0 %spread.1 = f32[128,128]{1,0:T(8,128)} custom-call(f32[64,128]{1,0:T(8,128)S(1)} %bitcast.27, f32[256,64]{1,0:T(8,128)S(1)} %copy-done.3), custom_call_target="tpu_custom_call" | custom-call | tf_op jit(solution)/shard_map/spread/pallas_call | solution.py:433
  58.8 4.6 %all-to-all-start.3 = ((f32[64,2,128]{2,1,0:T(2,128)}), f32[64,2,128]{2,1,0:T(2,128)S(1)}, u32[]{:S(2)}, u32[]{:S(2)}) async-start(f32[64,2,128]{2,1,0:T(2,128)} %bitcast.8), calls=%async_computation.3 | async-start | bytes 131072 | tf_op jit(solution)/shard_map/all_to_all | solution.py:471
  63.4 0.0 copy-start.10
  63.4 0.1 edges.1
  63.5 2.9 %collective-permute-start.2 = (f32[96,128]{1,0:T(8,128)S(1)}, f32[96,128]{1,0:T(8,128)S(1)}, u32[]{:S(2)}, u32[]{:S(2)}) collective-permute-start(f32[96,128]{1,0:T(8,128)S(1)} %get-tuple-element.7), channel_id=1, source_target_pairs={{0,1},{1,2},{2,3},{3,4},{4,5},{5,6},{6,7},{8,9},{9,10},{10,11},{11... | collective-permute-start | bytes 147464 | tf_op jit(solution)/shard_map/ppermute | solution.py:451
  66.5 1.9 %collective-permute-start.3 = (f32[96,128]{1,0:T(8,128)S(1)}, f32[96,128]{1,0:T(8,128)S(1)}, u32[]{:S(2)}, u32[]{:S(2)}) collective-permute-start(f32[96,128]{1,0:T(8,128)S(1)} %get-tuple-element.8), channel_id=1, source_target_pairs={{1,0},{2,1},{3,2},{4,3},{5,4},{6,5},{7,6},{9,8},{10,9},{11,10},{12... | collective-permute-start | bytes 147464 | tf_op jit(solution)/shard_map/ppermute | solution.py:452
  68.4 0.3 copy.22
  68.7 0.2 reshape.27.refs_3_.refs_8_
  68.9 0.4 copy-done.11
  69.3 0.1 broadcast_in_dim.2.refs_4_
  69.4 2.3 %conv.1.refs_5_ = f32[1024,128]{1,0:T(8,128)S(1)} custom-call(f32[1024,128]{1,0:T(8,128)S(1)} %bitcast.21, f32[1024,128]{1,0:T(8,128)S(1)} %bitcast.19, f32[1024,128]{1,0:T(8,128)S(1)} %bitcast.23, f32[288,96]{1,0:T(8,128)S(1)} %reshape.27.refs_3_.refs_8_, f32[32,128]{1,0:T(8,128)S(1)} %broadcast_in_dim.2.refs_4_), custom_call_target="tpu_custom_call" | custom-call | tf_op jit(solution)/shard_map/conv/pallas_call | solution.py:422
  71.7 2.8 %all-to-all-done.3 = f32[64,2,128]{2,1,0:T(2,128)S(1)} async-done(((f32[64,2,128]{2,1,0:T(2,128)}), f32[64,2,128]{2,1,0:T(2,128)S(1)}, u32[]{:S(2)}, u32[]{:S(2)}) %all-to-all-start.3) | async-done | bytes 65568 | tf_op jit(solution)/shard_map/all_to_all | solution.py:471
  74.6 2.0 %inverse.1 = f32[1024,128]{1,0:T(8,128)} custom-call(f32[128,128]{1,0:T(8,128)S(1)} %bitcast.26, bf16[256,256]{1,0:T(8,128)(2,1)S(1)} %copy-done.1, bf16[256,256]{1,0:T(8,128)(2,1)S(1)} %copy-done.2, bf16[32,256]{1,0:T(8,128)(2,1)S(1)} %copy-done.7, bf16[32,256]{1,0:T(8,128)(2,1)S(1)} %copy-done.8, f32[1024,128]{1,0:T(8,128)S(1)} %conv.1.refs_5_, ...), custom_call_target="tpu_custom_call" | custom-call | tf_op jit(solution)/shard_map/inverse/pallas_call | solution.py:474
  (23 shorter events, 0.0 us)
Async XLA Ops:
  0.0 63.4 %collective-permute-start = (f32[32,1,32,128]{3,2,1,0:T(8,128)}, f32[32,1,32,128]{3,2,1,0:T(8,128)S(1)}, u32[]{:S(2)}, u32[]{:S(2)}) collective-permute-start(f32[32,1,32,128]{3,2,1,0:T(8,128)} %param.16), channel_id=1, source_target_pairs={{0,8},{8,16},{16,24},{24,32},{32,40},{40,48},{48,56},{56,64},{64,7... | collective-permute-start | bytes 1572872 | tf_op jit(solution)/shard_map/ppermute | solution.py:440
  4.9 58.6 %collective-permute-start.1 = (f32[32,1,32,128]{3,2,1,0:T(8,128)}, f32[32,1,32,128]{3,2,1,0:T(8,128)S(1)}, u32[]{:S(2)}, u32[]{:S(2)}) collective-permute-start(f32[32,1,32,128]{3,2,1,0:T(8,128)} %param.16), channel_id=1, source_target_pairs={{8,0},{16,8},{24,16},{32,24},{40,32},{48,40},{56,48},{64,56},{72,6... | collective-permute-start | bytes 1572872 | tf_op jit(solution)/shard_map/ppermute | solution.py:441
  6.2 41.6 %copy-start.6 = (f32[8,2048]{1,0:T(8,128)S(1)}, f32[8,2048]{1,0:T(8,128)}, u32[]{:S(2)}) copy-start(f32[8,2048]{1,0:T(8,128)} %refs_2_.3) | copy-start | bytes 196612
  8.5 11.2 %copy-start.4 = (f32[256,128]{1,0:T(8,128)S(1)}, f32[256,128]{1,0:T(8,128)}, u32[]{:S(2)}) copy-start(f32[256,128]{1,0:T(8,128)} %constant.30.clone.refs_1_) | copy-start | bytes 393220
  8.5 11.2 %copy-start.5 = (f32[256,128]{1,0:T(8,128)S(1)}, f32[256,128]{1,0:T(8,128)}, u32[]{:S(2)}) copy-start(f32[256,128]{1,0:T(8,128)} %constant.31.clone.refs_2_) | copy-start | bytes 393220
  8.6 39.2 %copy-start.9 = (f32[32,64]{1,0:T(8,128)S(1)}, f32[32,64]{1,0:T(8,128)}, u32[]{:S(2)}) copy-start(f32[32,64]{1,0:T(8,128)} %constant.28.clone.refs_1_) | copy-start | bytes 24580
  19.7 43.7 %copy-start = (f32[32,1,32,128]{3,2,1,0:T(8,128)S(1)}, f32[32,1,32,128]{3,2,1,0:T(8,128)}, u32[]{:S(2)}) copy-start(f32[32,1,32,128]{3,2,1,0:T(8,128)} %param.16) | copy-start | bytes 1572868
  19.9 37.9 %copy-start.3 = (f32[256,64]{1,0:T(8,128)S(1)}, f32[256,64]{1,0:T(8,128)}, u32[]{:S(2)}) copy-start(f32[256,64]{1,0:T(8,128)} %constant.29.clone.refs_1_) | copy-start | bytes 196612
  58.8 15.8 %all-to-all-start.3 = ((f32[64,2,128]{2,1,0:T(2,128)}), f32[64,2,128]{2,1,0:T(2,128)S(1)}, u32[]{:S(2)}, u32[]{:S(2)}) async-start(f32[64,2,128]{2,1,0:T(2,128)} %bitcast.8), calls=%async_computation.3 | async-start | bytes 131072 | tf_op jit(solution)/shard_map/all_to_all | solution.py:471
  63.4 5.0 %copy-start.10 = (f32[3,3,3,32,32]{4,3,2,1,0:T(8,128)S(1)}, f32[3,3,3,32,32]{4,3,2,1,0:T(8,128)}, u32[]{:S(2)}) copy-start(f32[3,3,3,32,32]{4,3,2,1,0:T(8,128)} %param.17) | copy-start | bytes 331780
  63.5 11.1 %collective-permute-start.2 = (f32[96,128]{1,0:T(8,128)S(1)}, f32[96,128]{1,0:T(8,128)S(1)}, u32[]{:S(2)}, u32[]{:S(2)}) collective-permute-start(f32[96,128]{1,0:T(8,128)S(1)} %get-tuple-element.7), channel_id=1, source_target_pairs={{0,1},{1,2},{2,3},{3,4},{4,5},{5,6},{6,7},{8,9},{9,10},{10,11},{11... | collective-permute-start | bytes 147464 | tf_op jit(solution)/shard_map/ppermute | solution.py:451
  66.5 8.1 %collective-permute-start.3 = (f32[96,128]{1,0:T(8,128)S(1)}, f32[96,128]{1,0:T(8,128)S(1)}, u32[]{:S(2)}, u32[]{:S(2)}) collective-permute-start(f32[96,128]{1,0:T(8,128)S(1)} %get-tuple-element.8), channel_id=1, source_target_pairs={{1,0},{2,1},{3,2},{4,3},{5,4},{6,5},{7,6},{9,8},{10,9},{11,10},{12... | collective-permute-start | bytes 147464 | tf_op jit(solution)/shard_map/ppermute | solution.py:452
  68.7 0.7 copy-start.11
  69.4 5.2 %copy-start.1 = (bf16[256,256]{1,0:T(8,128)(2,1)S(1)}, bf16[256,256]{1,0:T(8,128)(2,1)}, u32[]{:S(2)}) copy-start(bf16[256,256]{1,0:T(8,128)(2,1)} %constant.32.clone.refs_1_) | copy-start | bytes 393220
  69.4 5.2 %copy-start.2 = (bf16[256,256]{1,0:T(8,128)(2,1)S(1)}, bf16[256,256]{1,0:T(8,128)(2,1)}, u32[]{:S(2)}) copy-start(bf16[256,256]{1,0:T(8,128)(2,1)} %constant.33.clone.refs_2_) | copy-start | bytes 393220
  69.4 5.2 %copy-start.7 = (bf16[32,256]{1,0:T(8,128)(2,1)S(1)}, bf16[32,256]{1,0:T(8,128)(2,1)}, u32[]{:S(2)}) copy-start(bf16[32,256]{1,0:T(8,128)(2,1)} %constant.34.clone.refs_3_) | copy-start | bytes 49156
  69.4 5.2 %copy-start.8 = (bf16[32,256]{1,0:T(8,128)(2,1)S(1)}, bf16[32,256]{1,0:T(8,128)(2,1)}, u32[]{:S(2)}) copy-start(bf16[32,256]{1,0:T(8,128)(2,1)} %constant.35.clone.refs_4_) | copy-start | bytes 49156

commit v4 on v3

--- a/solution.py
+++ b/solution.py
@@ -14,6 +14,8 @@
 GROUP = 8
 CLASSES = 4
 LANES = 128
+LONG = pl.CostEstimate(flops=10**10, transcendentals=0, bytes_accessed=1 << 20)
+COSTLY = dict.fromkeys(("middle",), LONG)
 
 f32 = jnp.float32
 bf16 = jnp.bfloat16
@@ -426,6 +428,7 @@
             out_shape=jax.ShapeDtypeStruct(cells.shape, f32),
             scratch_shapes=[pltpu.VMEM((rows_y + 2, 9 * channels, depth), f32)],
             compiler_params=params,
+            cost_estimate=COSTLY.get(name),
             name=name,
         )(*operands)
 
@@ -434,11 +437,23 @@
             kernel,
             out_shape=jax.ShapeDtypeStruct((rows, LANES), f32),
             compiler_params=params,
+            cost_estimate=COSTLY.get(name),
             name=name,
         )(*operands)
 
+    right = lax.ppermute(features, "gx", [(i + 1, i) for i in range(count_x - 1)])
     left = lax.ppermute(features, "gx", [(i, i + 1) for i in range(count_x - 1)])
-    right = lax.ppermute(features, "gx", [(i + 1, i) for i in range(count_x - 1)])
+    half_table, whole_table = long_tables(length_x, count_y, share)
+    gathered = lax.all_to_all(outgoing, "gy", 0, 0, tiled=True)
+    folded = small(
+        lambda *refs: fold_kernel(*refs, channels=channels),
+        "fold", count_x, gathered, *turn_tables(count_y, count_x // 2),
+    )
+    arrived = lax.all_to_all(folded, "gx", 0, 0, tiled=True)
+    mixed = small(
+        lambda *refs: middle_kernel(*refs, channels=channels, norm_factor=norm_factor),
+        "middle", count_y * share, arrived, half_table, spectral_weight,
+    )
     left = left.reshape(cells.shape)
     right = right.reshape(cells.shape)
     edge = jax.ShapeDtypeStruct((3 * channels, depth), f32)
@@ -452,17 +467,6 @@
     after = lax.ppermute(heads, "gy", [(i + 1, i) for i in range(count_y - 1)])
     local_term = conv("conv", (0, 1, 2), left, cells, right, taps, bias)
 
-    half_table, whole_table = long_tables(length_x, count_y, share)
-    gathered = lax.all_to_all(outgoing, "gy", 0, 0, tiled=True)
-    folded = small(
-        lambda *refs: fold_kernel(*refs, channels=channels),
-        "fold", count_x, gathered, *turn_tables(count_y, count_x // 2),
-    )
-    arrived = lax.all_to_all(folded, "gx", 0, 0, tiled=True)
-    mixed = small(
-        lambda *refs: middle_kernel(*refs, channels=channels, norm_factor=norm_factor),
-        "middle", count_y * share, arrived, half_table, spectral_weight,
-    )
     shared = lax.all_to_all(mixed, "gy", 0, 0, tiled=True)
     returning = small(
         lambda *refs: spread_kernel(*refs, channels=channels, rows_x=count_x // KY),

time: 77 us -> 73.7 us (0.957)
  blocking collectives: 48.3 us -> 24.1 us
  starting transfers between devices: 15.6 us -> 29.7 us
  waiting for transfers between devices: 2.85 us -> 9.05 us
    all_to_all x1 -> x0, blocking collectives: 27.8 us -> none  [local(): arrived = lax.all_to_all(folded, 'gx', 0, 0, tiled=True)]
    all_to_all x0 -> x1, starting transfers between devices: none -> 12.8 us  [local(): arrived = lax.all_to_all(folded, 'gx', 0, 0, tiled=True)]
    all_to_all x0 -> x1, waiting for transfers between devices: none -> 6.52 us  [local(): arrived = lax.all_to_all(folded, 'gx', 0, 0, tiled=True)]
    all_to_all x1, blocking collectives: 11.1 us -> 14.7 us  [local(): gathered = lax.all_to_all(outgoing, 'gy', 0, 0, tiled=True)]
    all_to_all x1, starting transfers between devices: 4.62 us -> 7.58 us  [local(): whole = lax.all_to_all(returning, 'gx', 0, 0, tiled=True)]
    ppermute x1, starting transfers between devices: 4.85 us -> 2.95 us  [local(): lax.ppermute(features, 'gx', [(i, i + 1) for i in range(count_x - 1)])]
  transfers between devices with their start and end apart: 5 -> 6, of which waited for: 1 -> 2; matrix products, arithmetic and copies ran while one was open for 1% -> 1% of each run, Pallas kernels for 9% -> 6%
where the time goes in v4:
time: 73.7 us; the launch traced here: 73.3 us
  starting transfers between devices  29.7 us (40%)
  blocking collectives  24.1 us (33%)
  Pallas kernels  9.24 us (13%)
  waiting for transfers between devices  9.05 us (12%)
  local copies, waits for them, and re-layouts  1.02 us (1%)
    all_to_all x1, blocking collectives, local(): gathered = lax.all_to_all(outgoing, 'gy', 0, 0, tiled=True)  14.7 us
    all_to_all x1, starting transfers between devices, local(): arrived = lax.all_to_all(folded, 'gx', 0, 0, tiled=True)  12.8 us
    all_to_all x1, blocking collectives, local(): shared = lax.all_to_all(mixed, 'gy', 0, 0, tiled=True)  9.41 us
    all_to_all x1, starting transfers between devices, local(): whole = lax.all_to_all(returning, 'gx', 0, 0, tiled=True)  7.58 us
    all_to_all x1, waiting for transfers between devices, local(): arrived = lax.all_to_all(folded, 'gx', 0, 0, tiled=True)  6.52 us
    ppermute x1, starting transfers between devices, local(): before = lax.ppermute(tails, 'gy', [(i, i + 1) for i in range(count_y - 1)])  3.23 us
    ppermute x1, starting transfers between devices, local(): lax.ppermute(features, 'gx', [(i, i + 1) for i in range(count_x - 1)])  2.95 us
    all_to_all x1, waiting for transfers between devices, local(): whole = lax.all_to_all(returning, 'gx', 0, 0, tiled=True)  2.52 us
  transfers between devices with their start and end apart: 6, of which 2 were waited for; matrix products, arithmetic and copies ran while one was open for 1% of the time, Pallas kernels for 6%

profile of v4, /device:TPU:1, one launch (start us, length us, event | category | flops | bytes accessed | tf_op | source)
XLA Modules:
  0.0 73.3 jit_solution(6229563005067223168)
XLA Ops:
  0.0 2.4 %forward.1 = f32[256,128]{1,0:T(8,128)S(1)} custom-call(f32[1024,128]{1,0:T(8,128)} %bitcast.17, bf16[256,256]{1,0:T(8,128)(2,1)} %constant.24.clone.wide_high_hbm, bf16[256,256]{1,0:T(8,128)(2,1)} %constant.25.clone.wide_low_hbm, bf16[32,256]{1,0:T(8,128)(2,1)} %constant.26.clone.deep_high_hbm, bf16[32,256]{1,0:T(8,128)(2,1)} %constant.27.clone.deep_low_hbm), custom_call_target="tpu_custom_call" | custom-call | tf_op jit(solution)/shard_map/forward/pallas_call | solution.py:400
  2.4 0.0 copy-start
  2.4 14.7 %all_to_all.44 = f32[8,32,128]{2,1,0:T(8,128)S(1)} all-to-all(f32[8,32,128]{2,1,0:T(8,128)S(1)} %bitcast.25), channel_id=1, replica_groups=mesh['gx'=64,'gy'=8] {'gy'}, dimensions={0} | all-to-all | bytes 262144 | tf_op jit(solution)/shard_map/all_to_all | solution.py:447
  17.1 0.8 %fold.1 = f32[64,128]{1,0:T(8,128)} custom-call(f32[256,128]{1,0:T(8,128)S(1)} %bitcast.24, f32[256,128]{1,0:T(8,128)S(1)} %copy-done.4, f32[256,128]{1,0:T(8,128)S(1)} %copy-done.5), custom_call_target="tpu_custom_call" | custom-call | tf_op jit(solution)/shard_map/fold/pallas_call | solution.py:436
  17.9 12.8 %all-to-all-start.1 = ((f32[64,1,128]{2,1,0:T(1,128)}), f32[64,1,128]{2,1,0:T(1,128)S(1)}, u32[]{:S(2)}, u32[]{:S(2)}) async-start(f32[64,1,128]{2,1,0:T(1,128)} %bitcast.4), calls=%async_computation.1 | async-start | bytes 65536 | tf_op jit(solution)/shard_map/all_to_all | solution.py:452
  30.7 2.9 %collective-permute-start = (f32[32,1,32,128]{3,2,1,0:T(8,128)S(1)}, f32[32,1,32,128]{3,2,1,0:T(8,128)S(1)}, u32[]{:S(2)}, u32[]{:S(2)}) collective-permute-start(f32[32,1,32,128]{3,2,1,0:T(8,128)S(1)} %copy-done), channel_id=1, source_target_pairs={{0,8},{8,16},{16,24},{24,32},{32,40},{40,48},{48,56},{56,64},{64,7... | collective-permute-start | bytes 1572872 | tf_op jit(solution)/shard_map/ppermute | solution.py:445
  33.6 1.3 %collective-permute-start.1 = (f32[32,1,32,128]{3,2,1,0:T(8,128)S(1)}, f32[32,1,32,128]{3,2,1,0:T(8,128)S(1)}, u32[]{:S(2)}, u32[]{:S(2)}) collective-permute-start(f32[32,1,32,128]{3,2,1,0:T(8,128)S(1)} %copy-done), channel_id=1, source_target_pairs={{8,0},{16,8},{24,16},{32,24},{40,32},{48,40},{56,48},{64,56},{72,6... | collective-permute-start | bytes 1572872 | tf_op jit(solution)/shard_map/ppermute | solution.py:444
  34.9 6.5 %all-to-all-done.1 = f32[64,1,128]{2,1,0:T(1,128)S(1)} async-done(((f32[64,1,128]{2,1,0:T(1,128)}), f32[64,1,128]{2,1,0:T(1,128)S(1)}, u32[]{:S(2)}, u32[]{:S(2)}) %all-to-all-start.1) | async-done | bytes 32800 | tf_op jit(solution)/shard_map/all_to_all | solution.py:452
  41.5 0.7 middle.1
  42.1 9.4 %all_to_all.45 = f32[8,8,128]{2,1,0:T(8,128)S(1)} all-to-all(f32[8,8,128]{2,1,0:T(8,128)S(1)} %bitcast.29), channel_id=1, replica_groups=mesh['gx'=64,'gy'=8] {'gy'}, dimensions={0} | all-to-all | bytes 65536 | tf_op jit(solution)/shard_map/all_to_all | solution.py:470
  51.6 1.0 %spread.1 = f32[128,128]{1,0:T(8,128)} custom-call(f32[64,128]{1,0:T(8,128)S(1)} %bitcast.27, f32[256,64]{1,0:T(8,128)S(1)} %copy-done.3), custom_call_target="tpu_custom_call" | custom-call | tf_op jit(solution)/shard_map/spread/pallas_call | solution.py:436
  52.5 7.6 %all-to-all-start.3 = ((f32[64,2,128]{2,1,0:T(2,128)}), f32[64,2,128]{2,1,0:T(2,128)S(1)}, u32[]{:S(2)}, u32[]{:S(2)}) async-start(f32[64,2,128]{2,1,0:T(2,128)} %bitcast.8), calls=%async_computation.3 | async-start | bytes 131072 | tf_op jit(solution)/shard_map/all_to_all | solution.py:475
  60.1 0.0 copy-start.10
  60.1 0.1 edges.1
  60.2 3.2 %collective-permute-start.2 = (f32[96,128]{1,0:T(8,128)S(1)}, f32[96,128]{1,0:T(8,128)S(1)}, u32[]{:S(2)}, u32[]{:S(2)}) collective-permute-start(f32[96,128]{1,0:T(8,128)S(1)} %get-tuple-element.7), channel_id=1, source_target_pairs={{0,1},{1,2},{2,3},{3,4},{4,5},{5,6},{6,7},{8,9},{9,10},{10,11},{11... | collective-permute-start | bytes 147464 | tf_op jit(solution)/shard_map/ppermute | solution.py:466
  63.5 1.9 %collective-permute-start.3 = (f32[96,128]{1,0:T(8,128)S(1)}, f32[96,128]{1,0:T(8,128)S(1)}, u32[]{:S(2)}, u32[]{:S(2)}) collective-permute-start(f32[96,128]{1,0:T(8,128)S(1)} %get-tuple-element.8), channel_id=1, source_target_pairs={{1,0},{2,1},{3,2},{4,3},{5,4},{6,5},{7,6},{9,8},{10,9},{11,10},{12... | collective-permute-start | bytes 147464 | tf_op jit(solution)/shard_map/ppermute | solution.py:467
  65.4 0.3 copy.22
  65.6 0.0 copy-start.11
  65.7 0.2 reshape.27.refs_3_.refs_8_
  65.9 0.4 copy-done.11
  66.3 0.1 broadcast_in_dim.2.refs_4_
  66.4 2.3 %conv.1.refs_5_ = f32[1024,128]{1,0:T(8,128)S(1)} custom-call(f32[1024,128]{1,0:T(8,128)S(1)} %bitcast.21, f32[1024,128]{1,0:T(8,128)S(1)} %bitcast.19, f32[1024,128]{1,0:T(8,128)S(1)} %bitcast.23, f32[288,96]{1,0:T(8,128)S(1)} %reshape.27.refs_3_.refs_8_, f32[32,128]{1,0:T(8,128)S(1)} %broadcast_in_dim.2.refs_4_), custom_call_target="tpu_custom_call" | custom-call | tf_op jit(solution)/shard_map/conv/pallas_call | solution.py:424
  68.7 2.5 %all-to-all-done.3 = f32[64,2,128]{2,1,0:T(2,128)S(1)} async-done(((f32[64,2,128]{2,1,0:T(2,128)}), f32[64,2,128]{2,1,0:T(2,128)S(1)}, u32[]{:S(2)}, u32[]{:S(2)}) %all-to-all-start.3) | async-done | bytes 65568 | tf_op jit(solution)/shard_map/all_to_all | solution.py:475
  71.3 2.0 %inverse.1 = f32[1024,128]{1,0:T(8,128)} custom-call(f32[128,128]{1,0:T(8,128)S(1)} %bitcast.26, bf16[256,256]{1,0:T(8,128)(2,1)S(1)} %copy-done.1, bf16[256,256]{1,0:T(8,128)(2,1)S(1)} %copy-done.2, bf16[32,256]{1,0:T(8,128)(2,1)S(1)} %copy-done.6, bf16[32,256]{1,0:T(8,128)(2,1)S(1)} %copy-done.7, f32[1024,128]{1,0:T(8,128)S(1)} %conv.1.refs_5_, ...), custom_call_target="tpu_custom_call" | custom-call | tf_op jit(solution)/shard_map/inverse/pallas_call | solution.py:478
  (24 shorter events, 0.0 us)
Async XLA Ops:
  0.0 17.1 %copy-start.4 = (f32[256,128]{1,0:T(8,128)S(1)}, f32[256,128]{1,0:T(8,128)}, u32[]{:S(2)}) copy-start(f32[256,128]{1,0:T(8,128)} %constant.30.clone.refs_1_) | copy-start | bytes 393220
  0.0 17.1 %copy-start.5 = (f32[256,128]{1,0:T(8,128)S(1)}, f32[256,128]{1,0:T(8,128)}, u32[]{:S(2)}) copy-start(f32[256,128]{1,0:T(8,128)} %constant.31.clone.refs_2_) | copy-start | bytes 393220
  2.4 28.3 %copy-start = (f32[32,1,32,128]{3,2,1,0:T(8,128)S(1)}, f32[32,1,32,128]{3,2,1,0:T(8,128)}, u32[]{:S(2)}) copy-start(f32[32,1,32,128]{3,2,1,0:T(8,128)} %param.16) | copy-start | bytes 1572868
  17.1 24.4 %copy-start.9 = (f32[32,64]{1,0:T(8,128)S(1)}, f32[32,64]{1,0:T(8,128)}, u32[]{:S(2)}) copy-start(f32[32,64]{1,0:T(8,128)} %constant.28.clone.refs_1_) | copy-start | bytes 24580
  17.9 23.6 %copy-start.8 = (f32[8,2048]{1,0:T(8,128)S(1)}, f32[8,2048]{1,0:T(8,128)}, u32[]{:S(2)}) copy-start(f32[8,2048]{1,0:T(8,128)} %refs_2_.3) | copy-start | bytes 196612
  17.9 23.6 %all-to-all-start.1 = ((f32[64,1,128]{2,1,0:T(1,128)}), f32[64,1,128]{2,1,0:T(1,128)S(1)}, u32[]{:S(2)}, u32[]{:S(2)}) async-start(f32[64,1,128]{2,1,0:T(1,128)} %bitcast.4), calls=%async_computation.1 | async-start | bytes 65536 | tf_op jit(solution)/shard_map/all_to_all | solution.py:452
  30.7 29.4 %collective-permute-start = (f32[32,1,32,128]{3,2,1,0:T(8,128)S(1)}, f32[32,1,32,128]{3,2,1,0:T(8,128)S(1)}, u32[]{:S(2)}, u32[]{:S(2)}) collective-permute-start(f32[32,1,32,128]{3,2,1,0:T(8,128)S(1)} %copy-done), channel_id=1, source_target_pairs={{0,8},{8,16},{16,24},{24,32},{32,40},{40,48},{48,56},{56,64},{64,7... | collective-permute-start | bytes 1572872 | tf_op jit(solution)/shard_map/ppermute | solution.py:445
  33.6 26.5 %collective-permute-start.1 = (f32[32,1,32,128]{3,2,1,0:T(8,128)S(1)}, f32[32,1,32,128]{3,2,1,0:T(8,128)S(1)}, u32[]{:S(2)}, u32[]{:S(2)}) collective-permute-start(f32[32,1,32,128]{3,2,1,0:T(8,128)S(1)} %copy-done), channel_id=1, source_target_pairs={{8,0},{16,8},{24,16},{32,24},{40,32},{48,40},{56,48},{64,56},{72,6... | collective-permute-start | bytes 1572872 | tf_op jit(solution)/shard_map/ppermute | solution.py:444
  41.5 10.1 %copy-start.3 = (f32[256,64]{1,0:T(8,128)S(1)}, f32[256,64]{1,0:T(8,128)}, u32[]{:S(2)}) copy-start(f32[256,64]{1,0:T(8,128)} %constant.29.clone.refs_1_) | copy-start | bytes 196612
  52.5 18.7 %all-to-all-start.3 = ((f32[64,2,128]{2,1,0:T(2,128)}), f32[64,2,128]{2,1,0:T(2,128)S(1)}, u32[]{:S(2)}, u32[]{:S(2)}) async-start(f32[64,2,128]{2,1,0:T(2,128)} %bitcast.8), calls=%async_computation.3 | async-start | bytes 131072 | tf_op jit(solution)/shard_map/all_to_all | solution.py:475
  60.1 5.2 %copy-start.10 = (f32[3,3,3,32,32]{4,3,2,1,0:T(8,128)S(1)}, f32[3,3,3,32,32]{4,3,2,1,0:T(8,128)}, u32[]{:S(2)}) copy-start(f32[3,3,3,32,32]{4,3,2,1,0:T(8,128)} %param.17) | copy-start | bytes 331780
  60.2 11.0 %collective-permute-start.2 = (f32[96,128]{1,0:T(8,128)S(1)}, f32[96,128]{1,0:T(8,128)S(1)}, u32[]{:S(2)}, u32[]{:S(2)}) collective-permute-start(f32[96,128]{1,0:T(8,128)S(1)} %get-tuple-element.7), channel_id=1, source_target_pairs={{0,1},{1,2},{2,3},{3,4},{4,5},{5,6},{6,7},{8,9},{9,10},{10,11},{11... | collective-permute-start | bytes 147464 | tf_op jit(solution)/shard_map/ppermute | solution.py:466
  63.5 7.8 %collective-permute-start.3 = (f32[96,128]{1,0:T(8,128)S(1)}, f32[96,128]{1,0:T(8,128)S(1)}, u32[]{:S(2)}, u32[]{:S(2)}) collective-permute-start(f32[96,128]{1,0:T(8,128)S(1)} %get-tuple-element.8), channel_id=1, source_target_pairs={{1,0},{2,1},{3,2},{4,3},{5,4},{6,5},{7,6},{9,8},{10,9},{11,10},{12... | collective-permute-start | bytes 147464 | tf_op jit(solution)/shard_map/ppermute | solution.py:467
  65.6 0.7 copy-start.11
  66.4 4.9 %copy-start.1 = (bf16[256,256]{1,0:T(8,128)(2,1)S(1)}, bf16[256,256]{1,0:T(8,128)(2,1)}, u32[]{:S(2)}) copy-start(bf16[256,256]{1,0:T(8,128)(2,1)} %constant.32.clone.refs_1_) | copy-start | bytes 393220
  66.4 4.9 %copy-start.2 = (bf16[256,256]{1,0:T(8,128)(2,1)S(1)}, bf16[256,256]{1,0:T(8,128)(2,1)}, u32[]{:S(2)}) copy-start(bf16[256,256]{1,0:T(8,128)(2,1)} %constant.33.clone.refs_2_) | copy-start | bytes 393220
  66.4 4.9 %copy-start.6 = (bf16[32,256]{1,0:T(8,128)(2,1)S(1)}, bf16[32,256]{1,0:T(8,128)(2,1)}, u32[]{:S(2)}) copy-start(bf16[32,256]{1,0:T(8,128)(2,1)} %constant.34.clone.refs_3_) | copy-start | bytes 49156
  66.4 4.9 %copy-start.7 = (bf16[32,256]{1,0:T(8,128)(2,1)S(1)}, bf16[32,256]{1,0:T(8,128)(2,1)}, u32[]{:S(2)}) copy-start(bf16[32,256]{1,0:T(8,128)(2,1)} %constant.35.clone.refs_4_) | copy-start | bytes 49156

commit v5 on v4

--- a/solution.py
+++ b/solution.py
@@ -169,11 +169,19 @@
                 pair_ref[row : row + size, lane : lane + channels] = modes[
                     source : source + size, mode * channels : (mode + 1) * channels
                 ]
-    copies_of = out_ref.shape[0] // (CLASSES * rows)
+    copies_of = out_ref.shape[0] // (CLASSES * (rows + channels))
+    place = lax.axis_index("gy")
+    rows_y = cells_ref.shape[0] // channels
+    head = cells_ref[pl.ds(0, channels, stride=rows_y), :]
+    tail = cells_ref[pl.ds(rows_y - 1, channels, stride=rows_y), :]
     for kind in range(CLASSES):
         for each in range(copies_of):
-            start = (kind * copies_of + each) * rows
+            owner = kind * copies_of + each
+            start = owner * (rows + channels)
             out_ref[start : start + rows, :] = pair_ref[kind * rows : (kind + 1) * rows, :]
+            out_ref[start + rows : start + rows + channels, :] = jnp.where(
+                place + 1 == owner, tail, head
+            )
 
 
 def crossed(value, channels, sign):
@@ -189,9 +197,10 @@
 def fold_kernel(rows_ref, cos_ref, sin_ref, out_ref, *, channels):
     rows = out_ref.shape[0] // 2
     total = jnp.zeros((rows, LANES), f32)
-    for start in range(0, rows_ref.shape[0], rows):
+    for start in range(0, cos_ref.shape[0], rows):
         place = slice(start, start + rows)
-        value = rows_ref[place, :]
+        source = start // rows * (rows + channels)
+        value = rows_ref[source : source + rows, :]
         total = total + value * cos_ref[place, :] + crossed(value, channels, 1.0) * sin_ref[place, :]
     other = pltpu.roll(total, LANES // 2, axis=1)
     size = KZ // CLASSES
@@ -263,12 +272,19 @@
         out_ref[start : start + share, :] = mixed
 
 
-def edges_kernel(left_ref, cells_ref, right_ref, tails_ref, heads_ref, *, rows_y, channels):
-    planes = (left_ref, cells_ref, right_ref)
-    for plane in range(3):
-        rows = pl.ds(plane * channels, channels)
-        heads_ref[rows, :] = planes[plane][pl.ds(0, channels, stride=rows_y), :]
-        tails_ref[rows, :] = planes[plane][pl.ds(rows_y - 1, channels, stride=rows_y), :]
+def extend_kernel(cells_ref, rows_ref, out_ref, *, count_y):
+    rows_y = out_ref.shape[0] - 2
+    channels = out_ref.shape[1]
+    place = lax.axis_index("gy")
+    step = rows_ref.shape[0] // count_y
+    below = pl.multiple_of(jnp.maximum(place - 1, 0) * step, 8)
+    above = pl.multiple_of(jnp.minimum(place + 1, count_y - 1) * step, 8)
+    before = rows_ref[pl.ds(below + step - channels, channels), :]
+    after = rows_ref[pl.ds(above + step - channels, channels), :]
+    out_ref[0] = jnp.where(place > 0, before, jnp.zeros_like(before))
+    out_ref[rows_y + 1] = jnp.where(place < count_y - 1, after, jnp.zeros_like(after))
+    for row in range(rows_y):
+        out_ref[row + 1] = cells_ref[pl.ds(row, channels, stride=rows_y), :]
 
 
 def doubled_taps(taps):
@@ -288,21 +304,12 @@
     return parts[1] + below + above
 
 
-def conv_kernel(*refs, planes, rows_y, channels, depth):
-    plane_refs = refs[: len(planes)]
-    taps_ref, base_ref, out_ref, sums_scratch = refs[len(planes) :]
+def conv_kernel(left_ref, cells_ref, right_ref, taps_ref, bias_ref, out_ref, sums_scratch):
+    planes = (left_ref, cells_ref, right_ref)
+    channels, depth = bias_ref.shape
+    rows_y = cells_ref.shape[0] - 2
     width = 3 * channels
-    taps = jnp.concatenate(
-        [taps_ref[:, plane * channels : (plane + 1) * channels] for plane in planes], axis=1
-    )
-    taps = doubled_taps(taps)
-    sums_scratch[0, :width, :] = jnp.zeros((width, depth), f32)
-    sums_scratch[rows_y + 1, 2 * width :, :] = jnp.zeros((width, depth), f32)
-
-    def row_cells(row):
-        return jnp.concatenate(
-            [plane[pl.ds(row, channels, stride=rows_y), :] for plane in plane_refs], axis=0
-        )
+    taps = doubled_taps(taps_ref[...])
 
     def collect(row):
         parts = []
@@ -313,38 +320,30 @@
                 + sums_scratch[row + 1, width + first : width + first + channels, :]
                 + sums_scratch[row + 2, 2 * width + first : 2 * width + first + channels, :]
             )
-        place = pl.ds(row, channels, stride=rows_y)
-        base = base_ref[place, :] if base_ref.shape == out_ref.shape else base_ref[...]
-        out_ref[place, :] = shifted_sum(parts, depth) + base
-
-    for step in range(rows_y // 2):
-        cells = jnp.concatenate([row_cells(2 * step), row_cells(2 * step + 1)], axis=1)
+        out_ref[pl.ds(row, channels, stride=rows_y), :] = shifted_sum(parts, depth) + bias_ref[...]
+
+    for row in range(0, rows_y + 2, 2):
+        cells = jnp.concatenate(
+            [
+                jnp.concatenate([plane[row + side] for plane in planes], axis=0)
+                for side in range(2)
+            ],
+            axis=1,
+        )
         sums = product(taps, doubled_cells(cells), ((1,), (0,)))
-        sums_scratch[2 * step + 1] = sums[:, :depth]
-        sums_scratch[2 * step + 2] = sums[:, depth:]
-        if step:
-            collect(2 * step - 2)
-            collect(2 * step - 1)
-    collect(rows_y - 2)
-    collect(rows_y - 1)
+        sums_scratch[row] = sums[:, :depth]
+        sums_scratch[row + 1] = sums[:, depth:]
+        if row:
+            collect(row - 2)
+            collect(row - 1)
 
 
 def inverse_kernel(
-    rows_ref, wide_high, wide_low, deep_high, deep_low, conv_ref, before_ref, after_ref, taps_ref,
-    out_ref, modes_ref, middle_ref, conv_scratch, *, rows_y
+    rows_ref, wide_high, wide_low, deep_high, deep_low, conv_ref,
+    out_ref, modes_ref, middle_ref
 ):
     channels = modes_ref.shape[1] // KY
     groups = channels // GROUP
-    depth = conv_ref.shape[1]
-    width = 3 * channels
-    conv_scratch[...] = conv_ref[...]
-    taps = jnp.concatenate([taps_ref[:width, :], taps_ref[2 * width :, :]], axis=0)
-    cells = jnp.concatenate([before_ref[...], after_ref[...]], axis=1)
-    sums = product(doubled_taps(taps), doubled_cells(cells), ((1,), (0,)))
-    for row, values in ((0, sums[:width, :depth]), (rows_y - 1, sums[width:, depth:])):
-        place = pl.ds(row, channels, stride=rows_y)
-        parts = [values[r * channels : (r + 1) * channels] for r in range(3)]
-        conv_scratch[place, :] = conv_scratch[place, :] + shifted_sum(parts, depth)
     for mode in range(KY):
         for part in range(2):
             for odd in range(2):
@@ -375,7 +374,7 @@
         for side in range(2):
             start = (first + side) * block
             value = (
-                summed[:, side * LANES : (side + 1) * LANES] + conv_scratch[start : start + block, :]
+                summed[:, side * LANES : (side + 1) * LANES] + conv_ref[start : start + block, :]
             )
             out_ref[start : start + block, :] = (
                 0.5 * value * (1.0 + lax.erf(value * math.sqrt(0.5)))
@@ -399,7 +398,7 @@
     wide, deep = forward_tables(rows_y, length_y, depth)
     outgoing = pl.pallas_call(
         forward_kernel,
-        out_shape=jax.ShapeDtypeStruct((pairs // 2 // CLASSES * count_y, LANES), f32),
+        out_shape=jax.ShapeDtypeStruct(((pairs // 2 // CLASSES + channels) * count_y, LANES), f32),
         in_specs=[pl.BlockSpec(memory_space=pltpu.HBM)] * 5,
         scratch_shapes=[
             pltpu.VMEM(cells.shape, f32),
@@ -420,18 +419,6 @@
     taps = jnp.transpose(conv_weight, (1, 2, 4, 0, 3)).reshape(9 * channels, 3 * channels)
     bias = jnp.broadcast_to(conv_bias[:, None], (channels, depth))
 
-    def conv(name, planes, *operands):
-        return pl.pallas_call(
-            lambda *refs: conv_kernel(
-                *refs, planes=planes, rows_y=rows_y, channels=channels, depth=depth
-            ),
-            out_shape=jax.ShapeDtypeStruct(cells.shape, f32),
-            scratch_shapes=[pltpu.VMEM((rows_y + 2, 9 * channels, depth), f32)],
-            compiler_params=params,
-            cost_estimate=COSTLY.get(name),
-            name=name,
-        )(*operands)
-
     def small(kernel, name, rows, *operands):
         return pl.pallas_call(
             kernel,
@@ -442,9 +429,24 @@
         )(*operands)
 
     right = lax.ppermute(features, "gx", [(i + 1, i) for i in range(count_x - 1)])
-    left = lax.ppermute(features, "gx", [(i, i + 1) for i in range(count_x - 1)])
     half_table, whole_table = long_tables(length_x, count_y, share)
     gathered = lax.all_to_all(outgoing, "gy", 0, 0, tiled=True)
+    plane = jax.ShapeDtypeStruct((rows_y + 2, channels, depth), f32)
+    own = pl.pallas_call(
+        lambda *refs: extend_kernel(*refs, count_y=count_y),
+        out_shape=plane,
+        compiler_params=params,
+        name="extend",
+    )(cells, gathered)
+    left = lax.ppermute(own, "gx", [(i, i + 1) for i in range(count_x - 1)])
+    right = lax.ppermute(own, "gx", [(i + 1, i) for i in range(count_x - 1)])
+    local_term = pl.pallas_call(
+        conv_kernel,
+        out_shape=jax.ShapeDtypeStruct(cells.shape, f32),
+        scratch_shapes=[pltpu.VMEM((rows_y + 2, 9 * channels, depth), f32)],
+        compiler_params=params,
+        name="conv",
+    )(left, own, right, taps, bias)
     folded = small(
         lambda *refs: fold_kernel(*refs, channels=channels),
         "fold", count_x, gathered, *turn_tables(count_y, count_x // 2),
@@ -454,19 +456,6 @@
         lambda *refs: middle_kernel(*refs, channels=channels, norm_factor=norm_factor),
         "middle", count_y * share, arrived, half_table, spectral_weight,
     )
-    left = left.reshape(cells.shape)
-    right = right.reshape(cells.shape)
-    edge = jax.ShapeDtypeStruct((3 * channels, depth), f32)
-    tails, heads = pl.pallas_call(
-        lambda *refs: edges_kernel(*refs, rows_y=rows_y, channels=channels),
-        out_shape=(edge, edge),
-        compiler_params=params,
-        name="edges",
-    )(left, cells, right)
-    before = lax.ppermute(tails, "gy", [(i, i + 1) for i in range(count_y - 1)])
-    after = lax.ppermute(heads, "gy", [(i + 1, i) for i in range(count_y - 1)])
-    local_term = conv("conv", (0, 1, 2), left, cells, right, taps, bias)
-
     shared = lax.all_to_all(mixed, "gy", 0, 0, tiled=True)
     returning = small(
         lambda *refs: spread_kernel(*refs, channels=channels, rows_x=count_x // KY),
@@ -476,16 +465,15 @@
 
     wide, deep = inverse_tables(rows_y, length_y, depth, norm_factor)
     layer_out = pl.pallas_call(
-        lambda *refs: inverse_kernel(*refs, rows_y=rows_y),
+        inverse_kernel,
         out_shape=jax.ShapeDtypeStruct((channels * rows_y, depth), f32),
         scratch_shapes=[
             pltpu.VMEM((2 * KZ, KY * channels), f32),
             pltpu.VMEM((2 * KY * GROUP, channels // GROUP * LANES), f32),
-            pltpu.VMEM((channels * rows_y, depth), f32),
         ],
         compiler_params=params,
         name="inverse",
-    )(whole, *fixed_halves(wide), *fixed_halves(deep), local_term, before, after, taps)
+    )(whole, *fixed_halves(wide), *fixed_halves(deep), local_term)
     return layer_out.reshape(features.shape)
 
 

time: 73.7 us -> 75.3 us (1.022)
  waiting for transfers between devices: 9.05 us -> 14.3 us
  starting transfers between devices: 29.7 us -> 24.8 us
  blocking collectives: 24.1 us -> 25.5 us
    all_to_all x1, waiting for transfers between devices: 2.52 us -> 8.14 us  [local(): whole = lax.all_to_all(returning, 'gx', 0, 0, tiled=True)]
    ppermute x4 -> x2, starting transfers between devices: 9.39 us -> 4.24 us  [the longest x1 2.95 us: local(): left = lax.ppermute(own, 'gx', [(i, i + 1) for i in range(count_x - 1)])]
    all_to_all x1, blocking collectives: 14.7 us -> 15.9 us  [local(): gathered = lax.all_to_all(outgoing, 'gy', 0, 0, tiled=True)]
  transfers between devices with their start and end apart: 6 -> 4, of which waited for: 2 -> 2; matrix products, arithmetic and copies ran while one was open for 1% -> 1% of each run, Pallas kernels for 6% -> 5%
where the time goes in v5:
time: 75.3 us; the launch traced here: 74.9 us
  blocking collectives  25.5 us (34%)
  starting transfers between devices  24.8 us (33%)
  waiting for transfers between devices  14.3 us (19%)
  Pallas kernels  9.15 us (12%)
  local copies, waits for them, and re-layouts  1.01 us (1%)
    all_to_all x1, blocking collectives, local(): gathered = lax.all_to_all(outgoing, 'gy', 0, 0, tiled=True)  15.9 us
    all_to_all x1, starting transfers between devices, local(): arrived = lax.all_to_all(folded, 'gx', 0, 0, tiled=True)  12.6 us
    all_to_all x1, blocking collectives, local(): shared = lax.all_to_all(mixed, 'gy', 0, 0, tiled=True)  9.56 us
    all_to_all x1, waiting for transfers between devices, local(): whole = lax.all_to_all(returning, 'gx', 0, 0, tiled=True)  8.14 us
    all_to_all x1, starting transfers between devices, local(): whole = lax.all_to_all(returning, 'gx', 0, 0, tiled=True)  7.95 us
    all_to_all x1, waiting for transfers between devices, local(): arrived = lax.all_to_all(folded, 'gx', 0, 0, tiled=True)  6.16 us
    ppermute x1, starting transfers between devices, local(): left = lax.ppermute(own, 'gx', [(i, i + 1) for i in range(count_x - 1)])  2.95 us
    pallas_call x3, Pallas kernels, small(): pl.pallas_call(kernel, out_shape=jax.ShapeDtypeStruct((rows, LANES), f32)...  2.47 us
  transfers between devices with their start and end apart: 4, of which 2 were waited for; matrix products, arithmetic and copies ran while one was open for 1% of the time, Pallas kernels for 5%

profile of v5, /device:TPU:1, one launch (start us, length us, event | category | flops | bytes accessed | tf_op | source)
XLA Modules:
  0.0 74.9 jit_solution(144625506318390887)
XLA Ops:
  0.0 2.4 %forward.1 = f32[512,128]{1,0:T(8,128)S(1)} custom-call(f32[1024,128]{1,0:T(8,128)} %bitcast.17, bf16[256,256]{1,0:T(8,128)(2,1)} %constant.24.clone.wide_high_hbm, bf16[256,256]{1,0:T(8,128)(2,1)} %constant.25.clone.wide_low_hbm, bf16[32,256]{1,0:T(8,128)(2,1)} %constant.26.clone.deep_high_hbm, bf16[32,256]{1,0:T(8,128)(2,1)} %constant.27.clone.deep_low_hbm), custom_call_target="tpu_custom_call" | custom-call | tf_op jit(solution)/shard_map/forward/pallas_call | solution.py:399
  2.4 0.0 copy-start
  2.4 15.9 %all_to_all.44 = f32[8,64,128]{2,1,0:T(8,128)S(1)} all-to-all(f32[8,64,128]{2,1,0:T(8,128)S(1)} %bitcast.19), channel_id=1, replica_groups=mesh['gx'=64,'gy'=8] {'gy'}, dimensions={0} | all-to-all | bytes 524288 | tf_op jit(solution)/shard_map/all_to_all | solution.py:433
  18.3 0.8 %fold.1 = f32[64,128]{1,0:T(8,128)} custom-call(f32[512,128]{1,0:T(8,128)S(1)} %bitcast.15, f32[256,128]{1,0:T(8,128)S(1)} %copy-done.1, f32[256,128]{1,0:T(8,128)S(1)} %copy-done.2), custom_call_target="tpu_custom_call" | custom-call | tf_op jit(solution)/shard_map/fold/pallas_call | solution.py:423
  19.1 12.6 %all-to-all-start.1 = ((f32[64,1,128]{2,1,0:T(1,128)}), f32[64,1,128]{2,1,0:T(1,128)S(1)}, u32[]{:S(2)}, u32[]{:S(2)}) async-start(f32[64,1,128]{2,1,0:T(1,128)} %bitcast.4), calls=%async_computation.1 | async-start | bytes 65536 | tf_op jit(solution)/shard_map/all_to_all | solution.py:454
  31.8 0.0 copy-start.8
  31.8 0.0 copy-start.9
  31.8 0.3 extend.1.cells_ref
  32.1 2.9 %collective-permute-start = (f32[34,32,128]{2,1,0:T(8,128)S(1)}, f32[34,32,128]{2,1,0:T(8,128)S(1)}, u32[]{:S(2)}, u32[]{:S(2)}) collective-permute-start(f32[34,32,128]{2,1,0:T(8,128)S(1)} %extend.1.cells_ref), channel_id=1, source_target_pairs={{0,8},{8,16},{16,24},{24,32},{32,40},{40,48},{48,56},{56,64},{64,7... | collective-permute-start | bytes 1671176 | tf_op jit(solution)/shard_map/ppermute | solution.py:441
  35.1 1.3 %collective-permute-start.1 = (f32[34,32,128]{2,1,0:T(8,128)S(1)}, f32[34,32,128]{2,1,0:T(8,128)S(1)}, u32[]{:S(2)}, u32[]{:S(2)}) collective-permute-start(f32[34,32,128]{2,1,0:T(8,128)S(1)} %extend.1.cells_ref), channel_id=1, source_target_pairs={{8,0},{16,8},{24,16},{32,24},{40,32},{48,40},{56,48},{64,56},{72,6... | collective-permute-start | bytes 1671176 | tf_op jit(solution)/shard_map/ppermute | solution.py:442
  36.4 6.2 %all-to-all-done.1 = f32[64,1,128]{2,1,0:T(1,128)S(1)} async-done(((f32[64,1,128]{2,1,0:T(1,128)}), f32[64,1,128]{2,1,0:T(1,128)S(1)}, u32[]{:S(2)}, u32[]{:S(2)}) %all-to-all-start.1) | async-done | bytes 32800 | tf_op jit(solution)/shard_map/all_to_all | solution.py:454
  42.6 0.7 middle.1
  43.2 9.6 %all_to_all.45 = f32[8,8,128]{2,1,0:T(8,128)S(1)} all-to-all(f32[8,8,128]{2,1,0:T(8,128)S(1)} %bitcast.23), channel_id=1, replica_groups=mesh['gx'=64,'gy'=8] {'gy'}, dimensions={0} | all-to-all | bytes 65536 | tf_op jit(solution)/shard_map/all_to_all | solution.py:459
  52.8 1.0 %spread.1 = f32[128,128]{1,0:T(8,128)} custom-call(f32[64,128]{1,0:T(8,128)S(1)} %bitcast.21, f32[256,64]{1,0:T(8,128)S(1)} %copy-done.3), custom_call_target="tpu_custom_call" | custom-call | tf_op jit(solution)/shard_map/spread/pallas_call | solution.py:423
  53.8 8.0 %all-to-all-start.3 = ((f32[64,2,128]{2,1,0:T(2,128)}), f32[64,2,128]{2,1,0:T(2,128)S(1)}, u32[]{:S(2)}, u32[]{:S(2)}) async-start(f32[64,2,128]{2,1,0:T(2,128)} %bitcast.8), calls=%async_computation.3 | async-start | bytes 131072 | tf_op jit(solution)/shard_map/all_to_all | solution.py:464
  61.8 0.3 copy.22
  62.0 0.0 copy-start.11
  62.0 0.2 reshape.19.taps_ref
  62.3 0.0 collective-permute-done.left_ref
  62.3 0.4 copy-done.11
  62.7 0.1 broadcast_in_dim.2.bias_ref
  62.8 2.0 %conv.1.conv_ref = f32[1024,128]{1,0:T(8,128)S(1)} custom-call(f32[34,32,128]{2,1,0:T(8,128)S(1)} %collective-permute-done.left_ref, f32[34,32,128]{2,1,0:T(8,128)S(1)} %extend.1.cells_ref, f32[34,32,128]{2,1,0:T(8,128)S(1)} %collective-permute-done.1.right_ref, f32[288,96]{1,0:T(8,128)S(1)} %reshape.19.taps_ref, f32[32,128]{1,0:T(8,128)S(1)} %broadcast_in_dim.2.bias_ref), custom_call_target="tpu_custom_call" | custom-call | tf_op jit(solution)/shard_map/conv/pallas_call | solution.py:443
  64.7 8.1 %all-to-all-done.3 = f32[64,2,128]{2,1,0:T(2,128)S(1)} async-done(((f32[64,2,128]{2,1,0:T(2,128)}), f32[64,2,128]{2,1,0:T(2,128)S(1)}, u32[]{:S(2)}, u32[]{:S(2)}) %all-to-all-start.3) | async-done | bytes 65568 | tf_op jit(solution)/shard_map/all_to_all | solution.py:464
  72.9 2.0 %inverse.1 = f32[1024,128]{1,0:T(8,128)} custom-call(f32[128,128]{1,0:T(8,128)S(1)} %bitcast.20, bf16[256,256]{1,0:T(8,128)(2,1)S(1)} %copy-done.4, bf16[256,256]{1,0:T(8,128)(2,1)S(1)} %copy-done.5, bf16[32,256]{1,0:T(8,128)(2,1)S(1)} %copy-done.6, bf16[32,256]{1,0:T(8,128)(2,1)S(1)} %copy-done.7, f32[1024,128]{1,0:T(8,128)S(1)} %conv.1.conv_ref), custom_call_target="tpu_custom_call" | custom-call | tf_op jit(solution)/shard_map/inverse/pallas_call | solution.py:467
  (20 shorter events, 0.0 us)
Async XLA Ops:
  0.0 18.3 %copy-start.1 = (f32[256,128]{1,0:T(8,128)S(1)}, f32[256,128]{1,0:T(8,128)}, u32[]{:S(2)}) copy-start(f32[256,128]{1,0:T(8,128)} %constant.30.clone.refs_1_) | copy-start | bytes 393220
  0.0 18.3 %copy-start.2 = (f32[256,128]{1,0:T(8,128)S(1)}, f32[256,128]{1,0:T(8,128)}, u32[]{:S(2)}) copy-start(f32[256,128]{1,0:T(8,128)} %constant.31.clone.refs_2_) | copy-start | bytes 393220
  2.4 29.4 %copy-start = (f32[32,1,32,128]{3,2,1,0:T(8,128)S(1)}, f32[32,1,32,128]{3,2,1,0:T(8,128)}, u32[]{:S(2)}) copy-start(f32[32,1,32,128]{3,2,1,0:T(8,128)} %param.16) | copy-start | bytes 1572868
  19.1 23.4 %all-to-all-start.1 = ((f32[64,1,128]{2,1,0:T(1,128)}), f32[64,1,128]{2,1,0:T(1,128)S(1)}, u32[]{:S(2)}, u32[]{:S(2)}) async-start(f32[64,1,128]{2,1,0:T(1,128)} %bitcast.4), calls=%async_computation.1 | async-start | bytes 65536 | tf_op jit(solution)/shard_map/all_to_all | solution.py:454
  31.8 10.8 %copy-start.8 = (f32[8,2048]{1,0:T(8,128)S(1)}, f32[8,2048]{1,0:T(8,128)}, u32[]{:S(2)}) copy-start(f32[8,2048]{1,0:T(8,128)} %refs_2_.2) | copy-start | bytes 196612
  31.8 10.8 %copy-start.9 = (f32[32,64]{1,0:T(8,128)S(1)}, f32[32,64]{1,0:T(8,128)}, u32[]{:S(2)}) copy-start(f32[32,64]{1,0:T(8,128)} %constant.28.clone.refs_1_) | copy-start | bytes 24580
  32.1 30.1 %collective-permute-start = (f32[34,32,128]{2,1,0:T(8,128)S(1)}, f32[34,32,128]{2,1,0:T(8,128)S(1)}, u32[]{:S(2)}, u32[]{:S(2)}) collective-permute-start(f32[34,32,128]{2,1,0:T(8,128)S(1)} %extend.1.cells_ref), channel_id=1, source_target_pairs={{0,8},{8,16},{16,24},{24,32},{32,40},{40,48},{48,56},{56,64},{64,7... | collective-permute-start | bytes 1671176 | tf_op jit(solution)/shard_map/ppermute | solution.py:441
  35.1 27.2 %collective-permute-start.1 = (f32[34,32,128]{2,1,0:T(8,128)S(1)}, f32[34,32,128]{2,1,0:T(8,128)S(1)}, u32[]{:S(2)}, u32[]{:S(2)}) collective-permute-start(f32[34,32,128]{2,1,0:T(8,128)S(1)} %extend.1.cells_ref), channel_id=1, source_target_pairs={{8,0},{16,8},{24,16},{32,24},{40,32},{48,40},{56,48},{64,56},{72,6... | collective-permute-start | bytes 1671176 | tf_op jit(solution)/shard_map/ppermute | solution.py:442
  42.5 10.3 %copy-start.3 = (f32[256,64]{1,0:T(8,128)S(1)}, f32[256,64]{1,0:T(8,128)}, u32[]{:S(2)}) copy-start(f32[256,64]{1,0:T(8,128)} %constant.29.clone.refs_1_) | copy-start | bytes 196612
  42.6 19.2 %copy-start.10 = (f32[3,3,3,32,32]{4,3,2,1,0:T(8,128)S(1)}, f32[3,3,3,32,32]{4,3,2,1,0:T(8,128)}, u32[]{:S(2)}) copy-start(f32[3,3,3,32,32]{4,3,2,1,0:T(8,128)} %param.17) | copy-start | bytes 331780
  53.8 19.1 %all-to-all-start.3 = ((f32[64,2,128]{2,1,0:T(2,128)}), f32[64,2,128]{2,1,0:T(2,128)S(1)}, u32[]{:S(2)}, u32[]{:S(2)}) async-start(f32[64,2,128]{2,1,0:T(2,128)} %bitcast.8), calls=%async_computation.3 | async-start | bytes 131072 | tf_op jit(solution)/shard_map/all_to_all | solution.py:464
  62.0 0.7 copy-start.11
  62.7 10.1 %copy-start.4 = (bf16[256,256]{1,0:T(8,128)(2,1)S(1)}, bf16[256,256]{1,0:T(8,128)(2,1)}, u32[]{:S(2)}) copy-start(bf16[256,256]{1,0:T(8,128)(2,1)} %constant.32.clone.wide_high) | copy-start | bytes 393220
  62.7 10.1 %copy-start.5 = (bf16[256,256]{1,0:T(8,128)(2,1)S(1)}, bf16[256,256]{1,0:T(8,128)(2,1)}, u32[]{:S(2)}) copy-start(bf16[256,256]{1,0:T(8,128)(2,1)} %constant.33.clone.wide_low) | copy-start | bytes 393220
  62.7 10.1 %copy-start.6 = (bf16[32,256]{1,0:T(8,128)(2,1)S(1)}, bf16[32,256]{1,0:T(8,128)(2,1)}, u32[]{:S(2)}) copy-start(bf16[32,256]{1,0:T(8,128)(2,1)} %constant.34.clone.deep_high) | copy-start | bytes 49156
  62.7 10.1 %copy-start.7 = (bf16[32,256]{1,0:T(8,128)(2,1)S(1)}, bf16[32,256]{1,0:T(8,128)(2,1)}, u32[]{:S(2)}) copy-start(bf16[32,256]{1,0:T(8,128)(2,1)} %constant.35.clone.deep_low) | copy-start | bytes 49156

commit v6 on v4

--- a/solution.py
+++ b/solution.py
@@ -15,7 +15,7 @@
 CLASSES = 4
 LANES = 128
 LONG = pl.CostEstimate(flops=10**10, transcendentals=0, bytes_accessed=1 << 20)
-COSTLY = dict.fromkeys(("middle",), LONG)
+COSTLY = dict.fromkeys((), LONG)
 
 f32 = jnp.float32
 bf16 = jnp.bfloat16
@@ -331,7 +331,7 @@
 
 def inverse_kernel(
     rows_ref, wide_high, wide_low, deep_high, deep_low, conv_ref, before_ref, after_ref, taps_ref,
-    out_ref, modes_ref, middle_ref, conv_scratch, *, rows_y
+    out_hbm, modes_ref, middle_ref, conv_scratch, out_ref, sems, *, rows_y
 ):
     channels = modes_ref.shape[1] // KY
     groups = channels // GROUP
@@ -366,6 +366,7 @@
                 ]
     wide = (wide_high[...], wide_low[...])
     block = wide_high.shape[0]
+    copies = []
     for first in range(0, groups, 2):
         summed = product_of_halves(
             wide,
@@ -380,6 +381,12 @@
             out_ref[start : start + block, :] = (
                 0.5 * value * (1.0 + lax.erf(value * math.sqrt(0.5)))
             )
+        rows = pl.ds(first * block, 2 * block)
+        copy = pltpu.make_async_copy(out_ref.at[rows], out_hbm.at[rows], sems.at[first // 2])
+        copy.start()
+        copies.append(copy)
+    for copy in copies:
+        copy.wait()
 
 
 def local(features, conv_weight, conv_bias, spectral_weight):
@@ -441,7 +448,6 @@
             name=name,
         )(*operands)
 
-    right = lax.ppermute(features, "gx", [(i + 1, i) for i in range(count_x - 1)])
     left = lax.ppermute(features, "gx", [(i, i + 1) for i in range(count_x - 1)])
     half_table, whole_table = long_tables(length_x, count_y, share)
     gathered = lax.all_to_all(outgoing, "gy", 0, 0, tiled=True)
@@ -450,6 +456,8 @@
         "fold", count_x, gathered, *turn_tables(count_y, count_x // 2),
     )
     arrived = lax.all_to_all(folded, "gx", 0, 0, tiled=True)
+    right_cells, arrived = lax.optimization_barrier((features, arrived))
+    right = lax.ppermute(right_cells, "gx", [(i + 1, i) for i in range(count_x - 1)])
     mixed = small(
         lambda *refs: middle_kernel(*refs, channels=channels, norm_factor=norm_factor),
         "middle", count_y * share, arrived, half_table, spectral_weight,
@@ -482,7 +490,10 @@
             pltpu.VMEM((2 * KZ, KY * channels), f32),
             pltpu.VMEM((2 * KY * GROUP, channels // GROUP * LANES), f32),
             pltpu.VMEM((channels * rows_y, depth), f32),
+            pltpu.VMEM((channels * rows_y, depth), f32),
+            pltpu.SemaphoreType.DMA((2,)),
         ],
+        out_specs=pl.BlockSpec(memory_space=pltpu.HBM),
         compiler_params=params,
         name="inverse",
     )(whole, *fixed_halves(wide), *fixed_halves(deep), local_term, before, after, taps)

time: 73.7 us -> 73.6 us (level)
  waiting for transfers between devices: 9.05 us -> 10.4 us
  starting transfers between devices: 29.7 us -> 28.4 us
    all_to_all x1, starting transfers between devices: 7.58 us -> 6.26 us  [local(): whole = lax.all_to_all(returning, 'gx', 0, 0, tiled=True)]
    all_to_all x1, waiting for transfers between devices: 6.52 us -> 7.82 us  [local(): arrived = lax.all_to_all(folded, 'gx', 0, 0, tiled=True)]
where the time goes in v6:
time: 73.6 us; the launch traced here: 73.2 us
  starting transfers between devices  28.4 us (39%)
  blocking collectives  24.1 us (33%)
  waiting for transfers between devices  10.4 us (14%)
  Pallas kernels  9.15 us (12%)
  local copies, waits for them, and re-layouts  1.02 us (1%)
    all_to_all x1, blocking collectives, local(): gathered = lax.all_to_all(outgoing, 'gy', 0, 0, tiled=True)  14.7 us
    all_to_all x1, starting transfers between devices, local(): arrived = lax.all_to_all(folded, 'gx', 0, 0, tiled=True)  12.8 us
    all_to_all x1, blocking collectives, local(): shared = lax.all_to_all(mixed, 'gy', 0, 0, tiled=True)  9.42 us
    all_to_all x1, waiting for transfers between devices, local(): arrived = lax.all_to_all(folded, 'gx', 0, 0, tiled=True)  7.82 us
    all_to_all x1, starting transfers between devices, local(): whole = lax.all_to_all(returning, 'gx', 0, 0, tiled=True)  6.26 us
    ppermute x1, starting transfers between devices, local(): before = lax.ppermute(tails, 'gy', [(i, i + 1) for i in range(count_y - 1)])  3.23 us
    ppermute x1, starting transfers between devices, local(): lax.ppermute(features, 'gx', [(i, i + 1) for i in range(count_x - 1)])  2.95 us
    all_to_all x1, waiting for transfers between devices, local(): whole = lax.all_to_all(returning, 'gx', 0, 0, tiled=True)  2.53 us
  transfers between devices with their start and end apart: 6, of which 2 were waited for; matrix products, arithmetic and copies ran while one was open for 1% of the time, Pallas kernels for 6%

profile of v6, /device:TPU:1, one launch (start us, length us, event | category | flops | bytes accessed | tf_op | source)
XLA Modules:
  0.0 73.2 jit_solution(13305754926808576053)
XLA Ops:
  0.0 2.4 %forward.1 = f32[256,128]{1,0:T(8,128)S(1)} custom-call(f32[1024,128]{1,0:T(8,128)} %bitcast.17, bf16[256,256]{1,0:T(8,128)(2,1)} %constant.24.clone.wide_high_hbm, bf16[256,256]{1,0:T(8,128)(2,1)} %constant.25.clone.wide_low_hbm, bf16[32,256]{1,0:T(8,128)(2,1)} %constant.26.clone.deep_high_hbm, bf16[32,256]{1,0:T(8,128)(2,1)} %constant.27.clone.deep_low_hbm), custom_call_target="tpu_custom_call" | custom-call | tf_op jit(solution)/shard_map/forward/pallas_call | solution.py:407
  2.4 0.0 copy-start
  2.4 14.7 %all_to_all.45 = f32[8,32,128]{2,1,0:T(8,128)S(1)} all-to-all(f32[8,32,128]{2,1,0:T(8,128)S(1)} %bitcast.25), channel_id=1, replica_groups=mesh['gx'=64,'gy'=8] {'gy'}, dimensions={0} | all-to-all | bytes 262144 | tf_op jit(solution)/shard_map/all_to_all | solution.py:453
  17.1 0.8 %fold.1 = f32[64,128]{1,0:T(8,128)} custom-call(f32[256,128]{1,0:T(8,128)S(1)} %bitcast.24, f32[256,128]{1,0:T(8,128)S(1)} %copy-done.4, f32[256,128]{1,0:T(8,128)S(1)} %copy-done.5), custom_call_target="tpu_custom_call" | custom-call | tf_op jit(solution)/shard_map/fold/pallas_call | solution.py:443
  17.9 12.8 %all-to-all-start.1 = ((f32[64,1,128]{2,1,0:T(1,128)}), f32[64,1,128]{2,1,0:T(1,128)S(1)}, u32[]{:S(2)}, u32[]{:S(2)}) async-start(f32[64,1,128]{2,1,0:T(1,128)} %bitcast.4), calls=%async_computation.1 | async-start | bytes 65536 | tf_op jit(solution)/shard_map/all_to_all | solution.py:458
  30.7 2.9 %collective-permute-start = (f32[32,1,32,128]{3,2,1,0:T(8,128)S(1)}, f32[32,1,32,128]{3,2,1,0:T(8,128)S(1)}, u32[]{:S(2)}, u32[]{:S(2)}) collective-permute-start(f32[32,1,32,128]{3,2,1,0:T(8,128)S(1)} %copy-done), channel_id=1, source_target_pairs={{0,8},{8,16},{16,24},{24,32},{32,40},{40,48},{48,56},{56,64},{64,7... | collective-permute-start | bytes 1572872 | tf_op jit(solution)/shard_map/ppermute | solution.py:451
  33.6 7.8 %all-to-all-done.1 = f32[64,1,128]{2,1,0:T(1,128)S(1)} async-done(((f32[64,1,128]{2,1,0:T(1,128)}), f32[64,1,128]{2,1,0:T(1,128)S(1)}, u32[]{:S(2)}, u32[]{:S(2)}) %all-to-all-start.1) | async-done | bytes 32800 | tf_op jit(solution)/shard_map/all_to_all | solution.py:458
  41.5 1.3 %collective-permute-start.1 = (f32[32,1,32,128]{3,2,1,0:T(8,128)S(1)}, f32[32,1,32,128]{3,2,1,0:T(8,128)S(1)}, u32[]{:S(2)}, u32[]{:S(2)}) collective-permute-start(f32[32,1,32,128]{3,2,1,0:T(8,128)S(1)} %copy-done), channel_id=1, source_target_pairs={{8,0},{16,8},{24,16},{32,24},{40,32},{48,40},{56,48},{64,56},{72,6... | collective-permute-start | bytes 1572872 | tf_op jit(solution)/shard_map/ppermute | solution.py:460
  42.8 0.7 middle.1
  43.4 9.4 %all_to_all.46 = f32[8,8,128]{2,1,0:T(8,128)S(1)} all-to-all(f32[8,8,128]{2,1,0:T(8,128)S(1)} %bitcast.29), channel_id=1, replica_groups=mesh['gx'=64,'gy'=8] {'gy'}, dimensions={0} | all-to-all | bytes 65536 | tf_op jit(solution)/shard_map/all_to_all | solution.py:478
  52.9 1.0 %spread.1 = f32[128,128]{1,0:T(8,128)} custom-call(f32[64,128]{1,0:T(8,128)S(1)} %bitcast.27, f32[256,64]{1,0:T(8,128)S(1)} %copy-done.3), custom_call_target="tpu_custom_call" | custom-call | tf_op jit(solution)/shard_map/spread/pallas_call | solution.py:443
  53.8 6.3 %all-to-all-start.3 = ((f32[64,2,128]{2,1,0:T(2,128)}), f32[64,2,128]{2,1,0:T(2,128)S(1)}, u32[]{:S(2)}, u32[]{:S(2)}) async-start(f32[64,2,128]{2,1,0:T(2,128)} %bitcast.8), calls=%async_computation.3 | async-start | bytes 131072 | tf_op jit(solution)/shard_map/all_to_all | solution.py:483
  60.1 0.0 copy-start.10
  60.1 0.1 edges.1
  60.2 3.2 %collective-permute-start.2 = (f32[96,128]{1,0:T(8,128)S(1)}, f32[96,128]{1,0:T(8,128)S(1)}, u32[]{:S(2)}, u32[]{:S(2)}) collective-permute-start(f32[96,128]{1,0:T(8,128)S(1)} %get-tuple-element.11), channel_id=1, source_target_pairs={{0,1},{1,2},{2,3},{3,4},{4,5},{5,6},{6,7},{8,9},{9,10},{10,11},{11... | collective-permute-start | bytes 147464 | tf_op jit(solution)/shard_map/ppermute | solution.py:474
  63.4 1.9 %collective-permute-start.3 = (f32[96,128]{1,0:T(8,128)S(1)}, f32[96,128]{1,0:T(8,128)S(1)}, u32[]{:S(2)}, u32[]{:S(2)}) collective-permute-start(f32[96,128]{1,0:T(8,128)S(1)} %get-tuple-element.12), channel_id=1, source_target_pairs={{1,0},{2,1},{3,2},{4,3},{5,4},{6,5},{7,6},{9,8},{10,9},{11,10},{12... | collective-permute-start | bytes 147464 | tf_op jit(solution)/shard_map/ppermute | solution.py:475
  65.4 0.3 copy.22
  65.6 0.0 copy-start.11
  65.6 0.2 reshape.27.refs_3_.refs_8_
  65.9 0.4 copy-done.11
  66.3 0.1 broadcast_in_dim.2.refs_4_
  66.4 2.3 %conv.1.refs_5_ = f32[1024,128]{1,0:T(8,128)S(1)} custom-call(f32[1024,128]{1,0:T(8,128)S(1)} %bitcast.21, f32[1024,128]{1,0:T(8,128)S(1)} %bitcast.19, f32[1024,128]{1,0:T(8,128)S(1)} %bitcast.23, f32[288,96]{1,0:T(8,128)S(1)} %reshape.27.refs_3_.refs_8_, f32[32,128]{1,0:T(8,128)S(1)} %broadcast_in_dim.2.refs_4_), custom_call_target="tpu_custom_call" | custom-call | tf_op jit(solution)/shard_map/conv/pallas_call | solution.py:431
  68.7 2.5 %all-to-all-done.3 = f32[64,2,128]{2,1,0:T(2,128)S(1)} async-done(((f32[64,2,128]{2,1,0:T(2,128)}), f32[64,2,128]{2,1,0:T(2,128)S(1)}, u32[]{:S(2)}, u32[]{:S(2)}) %all-to-all-start.3) | async-done | bytes 65568 | tf_op jit(solution)/shard_map/all_to_all | solution.py:483
  71.3 1.9 %inverse.1 = f32[1024,128]{1,0:T(8,128)} custom-call(f32[128,128]{1,0:T(8,128)S(1)} %bitcast.26, bf16[256,256]{1,0:T(8,128)(2,1)S(1)} %copy-done.1, bf16[256,256]{1,0:T(8,128)(2,1)S(1)} %copy-done.2, bf16[32,256]{1,0:T(8,128)(2,1)S(1)} %copy-done.7, bf16[32,256]{1,0:T(8,128)(2,1)S(1)} %copy-done.8, f32[1024,128]{1,0:T(8,128)S(1)} %conv.1.refs_5_, ...), custom_call_target="tpu_custom_call" | custom-call | tf_op jit(solution)/shard_map/inverse/pallas_call | solution.py:486
  (24 shorter events, 0.0 us)
Async XLA Ops:
  0.0 17.1 %copy-start.4 = (f32[256,128]{1,0:T(8,128)S(1)}, f32[256,128]{1,0:T(8,128)}, u32[]{:S(2)}) copy-start(f32[256,128]{1,0:T(8,128)} %constant.30.clone.refs_1_) | copy-start | bytes 393220
  0.0 17.1 %copy-start.5 = (f32[256,128]{1,0:T(8,128)S(1)}, f32[256,128]{1,0:T(8,128)}, u32[]{:S(2)}) copy-start(f32[256,128]{1,0:T(8,128)} %constant.31.clone.refs_2_) | copy-start | bytes 393220
  2.4 28.3 %copy-start = (f32[32,1,32,128]{3,2,1,0:T(8,128)S(1)}, f32[32,1,32,128]{3,2,1,0:T(8,128)}, u32[]{:S(2)}) copy-start(f32[32,1,32,128]{3,2,1,0:T(8,128)} %param.16) | copy-start | bytes 1572868
  17.1 25.7 %copy-start.9 = (f32[32,64]{1,0:T(8,128)S(1)}, f32[32,64]{1,0:T(8,128)}, u32[]{:S(2)}) copy-start(f32[32,64]{1,0:T(8,128)} %constant.28.clone.refs_1_) | copy-start | bytes 24580
  17.9 24.9 %copy-start.6 = (f32[8,2048]{1,0:T(8,128)S(1)}, f32[8,2048]{1,0:T(8,128)}, u32[]{:S(2)}) copy-start(f32[8,2048]{1,0:T(8,128)} %refs_2_.3) | copy-start | bytes 196612
  17.9 35.0 %copy-start.3 = (f32[256,64]{1,0:T(8,128)S(1)}, f32[256,64]{1,0:T(8,128)}, u32[]{:S(2)}) copy-start(f32[256,64]{1,0:T(8,128)} %constant.29.clone.refs_1_) | copy-start | bytes 196612
  17.9 23.6 %all-to-all-start.1 = ((f32[64,1,128]{2,1,0:T(1,128)}), f32[64,1,128]{2,1,0:T(1,128)S(1)}, u32[]{:S(2)}, u32[]{:S(2)}) async-start(f32[64,1,128]{2,1,0:T(1,128)} %bitcast.4), calls=%async_computation.1 | async-start | bytes 65536 | tf_op jit(solution)/shard_map/all_to_all | solution.py:458
  30.7 29.4 %collective-permute-start = (f32[32,1,32,128]{3,2,1,0:T(8,128)S(1)}, f32[32,1,32,128]{3,2,1,0:T(8,128)S(1)}, u32[]{:S(2)}, u32[]{:S(2)}) collective-permute-start(f32[32,1,32,128]{3,2,1,0:T(8,128)S(1)} %copy-done), channel_id=1, source_target_pairs={{0,8},{8,16},{16,24},{24,32},{32,40},{40,48},{48,56},{56,64},{64,7... | collective-permute-start | bytes 1572872 | tf_op jit(solution)/shard_map/ppermute | solution.py:451
  41.5 18.7 %collective-permute-start.1 = (f32[32,1,32,128]{3,2,1,0:T(8,128)S(1)}, f32[32,1,32,128]{3,2,1,0:T(8,128)S(1)}, u32[]{:S(2)}, u32[]{:S(2)}) collective-permute-start(f32[32,1,32,128]{3,2,1,0:T(8,128)S(1)} %copy-done), channel_id=1, source_target_pairs={{8,0},{16,8},{24,16},{32,24},{40,32},{48,40},{56,48},{64,56},{72,6... | collective-permute-start | bytes 1572872 | tf_op jit(solution)/shard_map/ppermute | solution.py:460
  53.8 17.4 %all-to-all-start.3 = ((f32[64,2,128]{2,1,0:T(2,128)}), f32[64,2,128]{2,1,0:T(2,128)S(1)}, u32[]{:S(2)}, u32[]{:S(2)}) async-start(f32[64,2,128]{2,1,0:T(2,128)} %bitcast.8), calls=%async_computation.3 | async-start | bytes 131072 | tf_op jit(solution)/shard_map/all_to_all | solution.py:483
  60.1 5.2 %copy-start.10 = (f32[3,3,3,32,32]{4,3,2,1,0:T(8,128)S(1)}, f32[3,3,3,32,32]{4,3,2,1,0:T(8,128)}, u32[]{:S(2)}) copy-start(f32[3,3,3,32,32]{4,3,2,1,0:T(8,128)} %param.17) | copy-start | bytes 331780
  60.2 11.0 %collective-permute-start.2 = (f32[96,128]{1,0:T(8,128)S(1)}, f32[96,128]{1,0:T(8,128)S(1)}, u32[]{:S(2)}, u32[]{:S(2)}) collective-permute-start(f32[96,128]{1,0:T(8,128)S(1)} %get-tuple-element.11), channel_id=1, source_target_pairs={{0,1},{1,2},{2,3},{3,4},{4,5},{5,6},{6,7},{8,9},{9,10},{10,11},{11... | collective-permute-start | bytes 147464 | tf_op jit(solution)/shard_map/ppermute | solution.py:474
  63.4 7.8 %collective-permute-start.3 = (f32[96,128]{1,0:T(8,128)S(1)}, f32[96,128]{1,0:T(8,128)S(1)}, u32[]{:S(2)}, u32[]{:S(2)}) collective-permute-start(f32[96,128]{1,0:T(8,128)S(1)} %get-tuple-element.12), channel_id=1, source_target_pairs={{1,0},{2,1},{3,2},{4,3},{5,4},{6,5},{7,6},{9,8},{10,9},{11,10},{12... | collective-permute-start | bytes 147464 | tf_op jit(solution)/shard_map/ppermute | solution.py:475
  65.6 0.7 copy-start.11
  66.4 4.9 %copy-start.1 = (bf16[256,256]{1,0:T(8,128)(2,1)S(1)}, bf16[256,256]{1,0:T(8,128)(2,1)}, u32[]{:S(2)}) copy-start(bf16[256,256]{1,0:T(8,128)(2,1)} %constant.32.clone.refs_1_) | copy-start | bytes 393220
  66.4 4.9 %copy-start.2 = (bf16[256,256]{1,0:T(8,128)(2,1)S(1)}, bf16[256,256]{1,0:T(8,128)(2,1)}, u32[]{:S(2)}) copy-start(bf16[256,256]{1,0:T(8,128)(2,1)} %constant.33.clone.refs_2_) | copy-start | bytes 393220
  66.4 4.9 %copy-start.7 = (bf16[32,256]{1,0:T(8,128)(2,1)S(1)}, bf16[32,256]{1,0:T(8,128)(2,1)}, u32[]{:S(2)}) copy-start(bf16[32,256]{1,0:T(8,128)(2,1)} %constant.34.clone.refs_3_) | copy-start | bytes 49156
  66.4 4.9 %copy-start.8 = (bf16[32,256]{1,0:T(8,128)(2,1)S(1)}, bf16[32,256]{1,0:T(8,128)(2,1)}, u32[]{:S(2)}) copy-start(bf16[32,256]{1,0:T(8,128)(2,1)} %constant.35.clone.refs_4_) | copy-start | bytes 49156

commit v7 on v6

--- a/solution.py
+++ b/solution.py
@@ -214,12 +214,8 @@
         lane = lax.broadcasted_iota(jnp.int32, even.shape, 1)
         modes = jnp.where(lane < LANES // 2, even, odd)
         both = jnp.concatenate([modes, crossed(modes, channels, -1.0)], axis=0)
-        out_ref[pl.ds(tile, length, stride=2), :] = lax.dot_general(
-            basis,
-            both,
-            (((0,), (0,)), ((), ())),
-            precision=highest,
-            preferred_element_type=f32,
+        out_ref[pl.ds(tile, length, stride=2), :] = product_of_halves(
+            halves_of(basis), halves_of(both), ((0,), (0,))
         )
 
 
@@ -227,7 +223,7 @@
     share = weight_ref.shape[0]
     half = lax.rem(lax.axis_index("gy"), KX // share)
     basis = table_ref[pl.ds(pl.multiple_of(half * 2 * share, 2 * share), 2 * share), :]
-    sums = jnp.dot(basis, rows_ref[...], precision=highest, preferred_element_type=f32)
+    sums = product_of_halves(halves_of(basis), halves_of(rows_ref[...]), ((1,), (0,)))
     sums = norm_factor * (sums[:share] + crossed(sums[share:], channels, 1.0))
     hat_real = sums[:, :channels]
     hat_imag = sums[:, channels : 2 * channels]

time: 73.6 us -> 73.5 us (level)
  transfers between devices with their start and end apart: 6 -> 6, of which waited for: 2 -> 2; matrix products, arithmetic and copies ran while one was open for 1% -> 1% of each run, Pallas kernels for 6% -> 5%
where the time goes in v7:
time: 73.5 us; the launch traced here: 73.1 us
  starting transfers between devices  28.4 us (39%)
  blocking collectives  24.1 us (33%)
  waiting for transfers between devices  10.3 us (14%)
  Pallas kernels  9.06 us (12%)
  local copies, waits for them, and re-layouts  1.02 us (1%)
    all_to_all x1, blocking collectives, local(): gathered = lax.all_to_all(outgoing, 'gy', 0, 0, tiled=True)  14.7 us
    all_to_all x1, starting transfers between devices, local(): arrived = lax.all_to_all(folded, 'gx', 0, 0, tiled=True)  12.8 us
    all_to_all x1, blocking collectives, local(): shared = lax.all_to_all(mixed, 'gy', 0, 0, tiled=True)  9.4 us
    all_to_all x1, waiting for transfers between devices, local(): arrived = lax.all_to_all(folded, 'gx', 0, 0, tiled=True)  7.82 us
    all_to_all x1, starting transfers between devices, local(): whole = lax.all_to_all(returning, 'gx', 0, 0, tiled=True)  6.26 us
    ppermute x1, starting transfers between devices, local(): before = lax.ppermute(tails, 'gy', [(i, i + 1) for i in range(count_y - 1)])  3.23 us
    ppermute x1, starting transfers between devices, local(): lax.ppermute(features, 'gx', [(i, i + 1) for i in range(count_x - 1)])  2.95 us
    all_to_all x1, waiting for transfers between devices, local(): whole = lax.all_to_all(returning, 'gx', 0, 0, tiled=True)  2.52 us
  transfers between devices with their start and end apart: 6, of which 2 were waited for; matrix products, arithmetic and copies ran while one was open for 1% of the time, Pallas kernels for 5%

profile of v7, /device:TPU:1, one launch (start us, length us, event | category | flops | bytes accessed | tf_op | source)
XLA Modules:
  0.0 73.1 jit_solution(1857711474843514597)
XLA Ops:
  0.0 2.4 %forward.1 = f32[256,128]{1,0:T(8,128)S(1)} custom-call(f32[1024,128]{1,0:T(8,128)} %bitcast.17, bf16[256,256]{1,0:T(8,128)(2,1)} %constant.24.clone.wide_high_hbm, bf16[256,256]{1,0:T(8,128)(2,1)} %constant.25.clone.wide_low_hbm, bf16[32,256]{1,0:T(8,128)(2,1)} %constant.26.clone.deep_high_hbm, bf16[32,256]{1,0:T(8,128)(2,1)} %constant.27.clone.deep_low_hbm), custom_call_target="tpu_custom_call" | custom-call | tf_op jit(solution)/shard_map/forward/pallas_call | solution.py:403
  2.4 0.0 copy-start
  2.4 14.7 %all_to_all.45 = f32[8,32,128]{2,1,0:T(8,128)S(1)} all-to-all(f32[8,32,128]{2,1,0:T(8,128)S(1)} %bitcast.25), channel_id=1, replica_groups=mesh['gx'=64,'gy'=8] {'gy'}, dimensions={0} | all-to-all | bytes 262144 | tf_op jit(solution)/shard_map/all_to_all | solution.py:449
  17.1 0.8 %fold.1 = f32[64,128]{1,0:T(8,128)} custom-call(f32[256,128]{1,0:T(8,128)S(1)} %bitcast.24, f32[256,128]{1,0:T(8,128)S(1)} %copy-done.4, f32[256,128]{1,0:T(8,128)S(1)} %copy-done.5), custom_call_target="tpu_custom_call" | custom-call | tf_op jit(solution)/shard_map/fold/pallas_call | solution.py:439
  17.9 12.8 %all-to-all-start.1 = ((f32[64,1,128]{2,1,0:T(1,128)}), f32[64,1,128]{2,1,0:T(1,128)S(1)}, u32[]{:S(2)}, u32[]{:S(2)}) async-start(f32[64,1,128]{2,1,0:T(1,128)} %bitcast.4), calls=%async_computation.1 | async-start | bytes 65536 | tf_op jit(solution)/shard_map/all_to_all | solution.py:454
  30.7 2.9 %collective-permute-start = (f32[32,1,32,128]{3,2,1,0:T(8,128)S(1)}, f32[32,1,32,128]{3,2,1,0:T(8,128)S(1)}, u32[]{:S(2)}, u32[]{:S(2)}) collective-permute-start(f32[32,1,32,128]{3,2,1,0:T(8,128)S(1)} %copy-done), channel_id=1, source_target_pairs={{0,8},{8,16},{16,24},{24,32},{32,40},{40,48},{48,56},{56,64},{64,7... | collective-permute-start | bytes 1572872 | tf_op jit(solution)/shard_map/ppermute | solution.py:447
  33.6 7.8 %all-to-all-done.1 = f32[64,1,128]{2,1,0:T(1,128)S(1)} async-done(((f32[64,1,128]{2,1,0:T(1,128)}), f32[64,1,128]{2,1,0:T(1,128)S(1)}, u32[]{:S(2)}, u32[]{:S(2)}) %all-to-all-start.1) | async-done | bytes 32800 | tf_op jit(solution)/shard_map/all_to_all | solution.py:454
  41.5 1.3 %collective-permute-start.1 = (f32[32,1,32,128]{3,2,1,0:T(8,128)S(1)}, f32[32,1,32,128]{3,2,1,0:T(8,128)S(1)}, u32[]{:S(2)}, u32[]{:S(2)}) collective-permute-start(f32[32,1,32,128]{3,2,1,0:T(8,128)S(1)} %copy-done), channel_id=1, source_target_pairs={{8,0},{16,8},{24,16},{32,24},{40,32},{48,40},{56,48},{64,56},{72,6... | collective-permute-start | bytes 1572872 | tf_op jit(solution)/shard_map/ppermute | solution.py:456
  42.8 0.6 middle.1
  43.4 9.4 %all_to_all.46 = f32[8,8,128]{2,1,0:T(8,128)S(1)} all-to-all(f32[8,8,128]{2,1,0:T(8,128)S(1)} %bitcast.29), channel_id=1, replica_groups=mesh['gx'=64,'gy'=8] {'gy'}, dimensions={0} | all-to-all | bytes 65536 | tf_op jit(solution)/shard_map/all_to_all | solution.py:474
  52.8 0.9 %spread.1 = f32[128,128]{1,0:T(8,128)} custom-call(f32[64,128]{1,0:T(8,128)S(1)} %bitcast.27, f32[256,64]{1,0:T(8,128)S(1)} %copy-done.3), custom_call_target="tpu_custom_call" | custom-call | tf_op jit(solution)/shard_map/spread/pallas_call | solution.py:439
  53.7 6.3 %all-to-all-start.3 = ((f32[64,2,128]{2,1,0:T(2,128)}), f32[64,2,128]{2,1,0:T(2,128)S(1)}, u32[]{:S(2)}, u32[]{:S(2)}) async-start(f32[64,2,128]{2,1,0:T(2,128)} %bitcast.8), calls=%async_computation.3 | async-start | bytes 131072 | tf_op jit(solution)/shard_map/all_to_all | solution.py:479
  60.0 0.0 copy-start.10
  60.0 0.1 edges.1
  60.1 3.2 %collective-permute-start.2 = (f32[96,128]{1,0:T(8,128)S(1)}, f32[96,128]{1,0:T(8,128)S(1)}, u32[]{:S(2)}, u32[]{:S(2)}) collective-permute-start(f32[96,128]{1,0:T(8,128)S(1)} %get-tuple-element.11), channel_id=1, source_target_pairs={{0,1},{1,2},{2,3},{3,4},{4,5},{5,6},{6,7},{8,9},{9,10},{10,11},{11... | collective-permute-start | bytes 147464 | tf_op jit(solution)/shard_map/ppermute | solution.py:470
  63.3 1.9 %collective-permute-start.3 = (f32[96,128]{1,0:T(8,128)S(1)}, f32[96,128]{1,0:T(8,128)S(1)}, u32[]{:S(2)}, u32[]{:S(2)}) collective-permute-start(f32[96,128]{1,0:T(8,128)S(1)} %get-tuple-element.12), channel_id=1, source_target_pairs={{1,0},{2,1},{3,2},{4,3},{5,4},{6,5},{7,6},{9,8},{10,9},{11,10},{12... | collective-permute-start | bytes 147464 | tf_op jit(solution)/shard_map/ppermute | solution.py:471
  65.3 0.3 copy.22
  65.5 0.0 copy-start.11
  65.5 0.2 reshape.27.refs_3_.refs_8_
  65.8 0.4 copy-done.11
  66.2 0.1 broadcast_in_dim.2.refs_4_
  66.3 2.3 %conv.1.refs_5_ = f32[1024,128]{1,0:T(8,128)S(1)} custom-call(f32[1024,128]{1,0:T(8,128)S(1)} %bitcast.21, f32[1024,128]{1,0:T(8,128)S(1)} %bitcast.19, f32[1024,128]{1,0:T(8,128)S(1)} %bitcast.23, f32[288,96]{1,0:T(8,128)S(1)} %reshape.27.refs_3_.refs_8_, f32[32,128]{1,0:T(8,128)S(1)} %broadcast_in_dim.2.refs_4_), custom_call_target="tpu_custom_call" | custom-call | tf_op jit(solution)/shard_map/conv/pallas_call | solution.py:427
  68.6 2.5 %all-to-all-done.3 = f32[64,2,128]{2,1,0:T(2,128)S(1)} async-done(((f32[64,2,128]{2,1,0:T(2,128)}), f32[64,2,128]{2,1,0:T(2,128)S(1)}, u32[]{:S(2)}, u32[]{:S(2)}) %all-to-all-start.3) | async-done | bytes 65568 | tf_op jit(solution)/shard_map/all_to_all | solution.py:479
  71.1 1.9 %inverse.1 = f32[1024,128]{1,0:T(8,128)} custom-call(f32[128,128]{1,0:T(8,128)S(1)} %bitcast.26, bf16[256,256]{1,0:T(8,128)(2,1)S(1)} %copy-done.1, bf16[256,256]{1,0:T(8,128)(2,1)S(1)} %copy-done.2, bf16[32,256]{1,0:T(8,128)(2,1)S(1)} %copy-done.7, bf16[32,256]{1,0:T(8,128)(2,1)S(1)} %copy-done.8, f32[1024,128]{1,0:T(8,128)S(1)} %conv.1.refs_5_, ...), custom_call_target="tpu_custom_call" | custom-call | tf_op jit(solution)/shard_map/inverse/pallas_call | solution.py:482
  (24 shorter events, 0.0 us)
Async XLA Ops:
  0.0 17.1 %copy-start.4 = (f32[256,128]{1,0:T(8,128)S(1)}, f32[256,128]{1,0:T(8,128)}, u32[]{:S(2)}) copy-start(f32[256,128]{1,0:T(8,128)} %constant.30.clone.refs_1_) | copy-start | bytes 393220
  0.0 17.1 %copy-start.5 = (f32[256,128]{1,0:T(8,128)S(1)}, f32[256,128]{1,0:T(8,128)}, u32[]{:S(2)}) copy-start(f32[256,128]{1,0:T(8,128)} %constant.31.clone.refs_2_) | copy-start | bytes 393220
  2.4 28.3 %copy-start = (f32[32,1,32,128]{3,2,1,0:T(8,128)S(1)}, f32[32,1,32,128]{3,2,1,0:T(8,128)}, u32[]{:S(2)}) copy-start(f32[32,1,32,128]{3,2,1,0:T(8,128)} %param.16) | copy-start | bytes 1572868
  17.1 25.7 %copy-start.9 = (f32[32,64]{1,0:T(8,128)S(1)}, f32[32,64]{1,0:T(8,128)}, u32[]{:S(2)}) copy-start(f32[32,64]{1,0:T(8,128)} %constant.28.clone.refs_1_) | copy-start | bytes 24580
  17.9 24.9 %copy-start.6 = (f32[8,2048]{1,0:T(8,128)S(1)}, f32[8,2048]{1,0:T(8,128)}, u32[]{:S(2)}) copy-start(f32[8,2048]{1,0:T(8,128)} %refs_2_.3) | copy-start | bytes 196612
  17.9 34.9 %copy-start.3 = (f32[256,64]{1,0:T(8,128)S(1)}, f32[256,64]{1,0:T(8,128)}, u32[]{:S(2)}) copy-start(f32[256,64]{1,0:T(8,128)} %constant.29.clone.refs_1_) | copy-start | bytes 196612
  17.9 23.6 %all-to-all-start.1 = ((f32[64,1,128]{2,1,0:T(1,128)}), f32[64,1,128]{2,1,0:T(1,128)S(1)}, u32[]{:S(2)}, u32[]{:S(2)}) async-start(f32[64,1,128]{2,1,0:T(1,128)} %bitcast.4), calls=%async_computation.1 | async-start | bytes 65536 | tf_op jit(solution)/shard_map/all_to_all | solution.py:454
  30.7 29.3 %collective-permute-start = (f32[32,1,32,128]{3,2,1,0:T(8,128)S(1)}, f32[32,1,32,128]{3,2,1,0:T(8,128)S(1)}, u32[]{:S(2)}, u32[]{:S(2)}) collective-permute-start(f32[32,1,32,128]{3,2,1,0:T(8,128)S(1)} %copy-done), channel_id=1, source_target_pairs={{0,8},{8,16},{16,24},{24,32},{32,40},{40,48},{48,56},{56,64},{64,7... | collective-permute-start | bytes 1572872 | tf_op jit(solution)/shard_map/ppermute | solution.py:447
  41.5 18.5 %collective-permute-start.1 = (f32[32,1,32,128]{3,2,1,0:T(8,128)S(1)}, f32[32,1,32,128]{3,2,1,0:T(8,128)S(1)}, u32[]{:S(2)}, u32[]{:S(2)}) collective-permute-start(f32[32,1,32,128]{3,2,1,0:T(8,128)S(1)} %copy-done), channel_id=1, source_target_pairs={{8,0},{16,8},{24,16},{32,24},{40,32},{48,40},{56,48},{64,56},{72,6... | collective-permute-start | bytes 1572872 | tf_op jit(solution)/shard_map/ppermute | solution.py:456
  53.7 17.4 %all-to-all-start.3 = ((f32[64,2,128]{2,1,0:T(2,128)}), f32[64,2,128]{2,1,0:T(2,128)S(1)}, u32[]{:S(2)}, u32[]{:S(2)}) async-start(f32[64,2,128]{2,1,0:T(2,128)} %bitcast.8), calls=%async_computation.3 | async-start | bytes 131072 | tf_op jit(solution)/shard_map/all_to_all | solution.py:479
  60.0 5.3 %copy-start.10 = (f32[3,3,3,32,32]{4,3,2,1,0:T(8,128)S(1)}, f32[3,3,3,32,32]{4,3,2,1,0:T(8,128)}, u32[]{:S(2)}) copy-start(f32[3,3,3,32,32]{4,3,2,1,0:T(8,128)} %param.17) | copy-start | bytes 331780
  60.1 11.0 %collective-permute-start.2 = (f32[96,128]{1,0:T(8,128)S(1)}, f32[96,128]{1,0:T(8,128)S(1)}, u32[]{:S(2)}, u32[]{:S(2)}) collective-permute-start(f32[96,128]{1,0:T(8,128)S(1)} %get-tuple-element.11), channel_id=1, source_target_pairs={{0,1},{1,2},{2,3},{3,4},{4,5},{5,6},{6,7},{8,9},{9,10},{10,11},{11... | collective-permute-start | bytes 147464 | tf_op jit(solution)/shard_map/ppermute | solution.py:470
  63.3 7.8 %collective-permute-start.3 = (f32[96,128]{1,0:T(8,128)S(1)}, f32[96,128]{1,0:T(8,128)S(1)}, u32[]{:S(2)}, u32[]{:S(2)}) collective-permute-start(f32[96,128]{1,0:T(8,128)S(1)} %get-tuple-element.12), channel_id=1, source_target_pairs={{1,0},{2,1},{3,2},{4,3},{5,4},{6,5},{7,6},{9,8},{10,9},{11,10},{12... | collective-permute-start | bytes 147464 | tf_op jit(solution)/shard_map/ppermute | solution.py:471
  65.5 0.7 copy-start.11
  66.2 4.9 %copy-start.1 = (bf16[256,256]{1,0:T(8,128)(2,1)S(1)}, bf16[256,256]{1,0:T(8,128)(2,1)}, u32[]{:S(2)}) copy-start(bf16[256,256]{1,0:T(8,128)(2,1)} %constant.32.clone.refs_1_) | copy-start | bytes 393220
  66.3 4.9 %copy-start.2 = (bf16[256,256]{1,0:T(8,128)(2,1)S(1)}, bf16[256,256]{1,0:T(8,128)(2,1)}, u32[]{:S(2)}) copy-start(bf16[256,256]{1,0:T(8,128)(2,1)} %constant.33.clone.refs_2_) | copy-start | bytes 393220
  66.3 4.9 %copy-start.7 = (bf16[32,256]{1,0:T(8,128)(2,1)S(1)}, bf16[32,256]{1,0:T(8,128)(2,1)}, u32[]{:S(2)}) copy-start(bf16[32,256]{1,0:T(8,128)(2,1)} %constant.34.clone.refs_3_) | copy-start | bytes 49156
  66.3 4.9 %copy-start.8 = (bf16[32,256]{1,0:T(8,128)(2,1)S(1)}, bf16[32,256]{1,0:T(8,128)(2,1)}, u32[]{:S(2)}) copy-start(bf16[32,256]{1,0:T(8,128)(2,1)} %constant.35.clone.refs_4_) | copy-start | bytes 49156
